TPU v7x, 128 devices: a whole 4x4x4 slice. The times are simulated.
128 devices in a mesh: gx: 16 (over y, z), gy: 8 (over x, core).
Axes of the slice: x: 4, y: 4, z: 4, core: 2. Of those that a mesh axis runs over, the one named last changes fastest.
Arguments:
- u_now: float32 [3, 256, 256, 128], P(None, 'gx', 'gy'), may hold values from -3 to 3
- u_prev: float32 [3, 256, 256, 128], P(None, 'gx', 'gy'), may hold values from -3 to 3
- density: float32 [256, 256, 128], P('gx', 'gy'), may hold values from 1 to 2
- shear_mod: float32 [256, 256, 128], P('gx', 'gy'), may hold values from 0.4 to 1
- lame_first: float32 [256, 256, 128], P('gx', 'gy'), may hold values from 0.4 to 1
- storey_disp: float32 [3, 64, 131072], P(None, None, ('gx', 'gy')), may hold values from -2 to 2
- storey_vel: float32 [3, 64, 131072], P(None, None, ('gx', 'gy')), may hold values from -2 to 2
- hyst_fraction: float32 [3, 64, 131072], P(None, None, ('gx', 'gy')), may hold values from -1 to 1
- branch_flags: int32 [3, 64, 131072], P(None, None, ('gx', 'gy')), may hold values from 0 to 2
- stiffness: float32 [64, 131072], P(None, ('gx', 'gy')), may hold values from 0.5 to 2
- storey_mass: float32 [64, 131072], P(None, ('gx', 'gy')), may hold values from 0.7 to 1.4
- yield_drift: float32 [64, 131072], P(None, ('gx', 'gy')), may hold values from 0.1 to 1
- storey_count: int32 [131072], P(('gx', 'gy')), may hold values from 8 to 64
- footprint_tile: int32 [131072, 1], P(('gx', 'gy')), may hold values from 0 to 127; in each aligned block of 1024 rows (0 to 1023, 1024 to 2047, ...) at most 16 rows name the same one
- footprint_cell: int32 [131072], P(('gx', 'gy')), may hold values from 0 to 511
Outputs:
- field_now: float32 [3, 256, 256, 128], P(None, 'gx', 'gy')
- field_before: float32 [3, 256, 256, 128], P(None, 'gx', 'gy')
- final_disp: float32 [3, 64, 131072], P(None, None, ('gx', 'gy'))
- final_vel: float32 [3, 64, 131072], P(None, None, ('gx', 'gy'))
- final_hyst: float32 [3, 64, 131072], P(None, None, ('gx', 'gy'))
Inputs may be any that keep to these rules, and one draw needn't show every extreme that they name: `footprint_tile`: among the buildings of one device at most 16 name the same tile, a bound that some block reaches.
All inputs are finite; a program needn't handle non-finite values.
Results may differ from a plain program's by a relative error of at most 0.000061.
Values sent between devices are 32-bit elements; how exact they have to be, the bound alone decides.
No kernel may reach another device: no remote copies, remote signals or barrier semaphores. Data moves between devices by JAX's collectives and lax.ppermute only.
A program may use at most 128 MiB of HBM per device.

v0:
```python
import jax
import jax.numpy as jnp
from jax import lax
from jax.sharding import PartitionSpec as P

STEPS = 8


time_step = 0.35
post_share = 0.1
damping_rate = 0.05


def with_halo(array, sides, width):
    for axis, dim in sides:
        size, length = (lax.axis_size(axis), array.shape[dim])
        up = [(i, (i + 1) % size) for i in range(size - 1)]
        down = [(j, i) for i, j in up]
        last = lax.slice_in_dim(array, length - width, length, axis=dim)
        first = lax.slice_in_dim(array, 0, width, axis=dim)
        before = lax.ppermute(last, axis, up)
        after = lax.ppermute(first, axis, down)
        array = jnp.concatenate([before, array, after], axis=dim)
    return array


def shifted(padded, direction, offset):
    starts = [2, 2, 2]
    starts[direction] = starts[direction] + offset
    size_x = padded.shape[-3] - 4
    size_y = padded.shape[-2] - 4
    size_z = padded.shape[-1] - 4
    return padded[
        ...,
        starts[0] : starts[0] + size_x,
        starts[1] : starts[1] + size_y,
        starts[2] : starts[2] + size_z,
    ]


def central(padded, direction):
    near = shifted(padded, direction, 1) - shifted(padded, direction, -1)
    far_part = shifted(padded, direction, 2) - shifted(padded, direction, -2)
    return (8.0 * near - far_part) / 12.0


def stresses(padded, lame, shear_value):
    gradients = [
        [central(padded[component], direction) for direction in range(3)] for component in range(3)
    ]
    trace_sum = gradients[0][0] + gradients[1][1] + gradients[2][2]
    normal_x = lame * trace_sum + 2.0 * shear_value * gradients[0][0]
    normal_y = lame * trace_sum + 2.0 * shear_value * gradients[1][1]
    normal_z = lame * trace_sum + 2.0 * shear_value * gradients[2][2]
    shear_xy = shear_value * (gradients[0][1] + gradients[1][0])
    shear_xz = shear_value * (gradients[0][2] + gradients[2][0])
    shear_yz = shear_value * (gradients[1][2] + gradients[2][1])
    return jnp.stack([normal_x, normal_y, normal_z, shear_xy, shear_xz, shear_yz])


def divergence(padded):
    force_x = central(padded[0], 0) + central(padded[3], 1) + central(padded[4], 2)
    force_y = central(padded[3], 0) + central(padded[1], 1) + central(padded[5], 2)
    force_z = central(padded[4], 0) + central(padded[5], 1) + central(padded[2], 2)
    return jnp.stack([force_x, force_y, force_z])


def pad_depth(field):
    return jnp.pad(field, ((0, 0), (0, 0), (0, 0), (2, 2)))


def drifts(disp):
    lower = jnp.concatenate([jnp.zeros_like(disp[:, :1]), disp[:, :-1]], axis=1)
    return disp - lower


def building_start(storey_disp, storey_vel, hyst_fraction, branch_flags, yield_drift, storey_count):
    levels = storey_disp.shape[1]
    storey_mask = (jnp.arange(levels, dtype=jnp.int32)[:, None] < storey_count[None, :]).astype(
        jnp.float32
    )
    disp = storey_disp * storey_mask
    vel = storey_vel * storey_mask
    elastic = hyst_fraction * yield_drift
    hyst = (
        jnp.where(
            branch_flags == 1, yield_drift, jnp.where(branch_flags == 2, -yield_drift, elastic)
        )
        * storey_mask
    )
    return (storey_mask, disp, vel, hyst, drifts(disp))


def building_step(disp, vel, hyst, drift, ground, stiffness, storey_mass, yield_drift, storey_mask):
    spring = stiffness * (post_share * drift + (1.0 - post_share) * hyst) * storey_mask
    above = jnp.concatenate([spring[:, 1:], jnp.zeros_like(spring[:, :1])], axis=1)
    accel = (above - spring) / storey_mass - damping_rate * vel - ground[:, None, :]
    vel = (vel + time_step * accel) * storey_mask
    disp = (disp + time_step * vel) * storey_mask
    new_drift = drifts(disp)
    hyst = jnp.clip(hyst + new_drift - drift, -yield_drift, yield_drift) * storey_mask
    return (disp, vel, hyst, new_drift)


def local(
    u_now,
    u_prev,
    density,
    shear_mod,
    lame_first,
    storey_disp,
    storey_vel,
    hyst_fraction,
    branch_flags,
    stiffness,
    storey_mass,
    yield_drift,
    storey_count,
    footprint_tile,
    footprint_cell,
):
    cells_x = density.shape[0]
    cells_y = density.shape[1]
    current = u_now
    previous = u_prev
    surfaces = []
    for timestep in range(STEPS):
        widened = with_halo(current, (("gx", 1), ("gy", 2)), 2)
        local_stress = stresses(pad_depth(widened), lame_first, shear_mod)
        stress = pad_depth(with_halo(local_stress, (("gx", 1), ("gy", 2)), 2))
        accel = divergence(stress) / density
        surfaces.append(accel[:, :, :, 0])
        current, previous = (2.0 * current - previous + time_step * time_step * accel, current)
    devices = lax.axis_size("gx") * lax.axis_size("gy")
    building_count = footprint_cell.shape[0]
    capacity = 2 * building_count // devices
    owner_tile = footprint_tile[:, 0]
    onehot = (owner_tile[:, None] == jnp.arange(devices, dtype=jnp.int32)[None, :]).astype(
        jnp.int32
    )
    slot_rank = jnp.sum(jnp.cumsum(onehot, axis=0) * onehot, axis=1) - 1
    position = owner_tile * capacity + slot_rank
    requests = jnp.zeros((devices * capacity,), jnp.int32).at[position].set(footprint_cell)
    incoming = lax.all_to_all(requests, ("gx", "gy"), split_axis=0, concat_axis=0, tiled=True)
    history = jnp.stack(surfaces).reshape(STEPS * 3, cells_x * cells_y)
    answers = jnp.take(history, incoming, axis=1)
    returned = lax.all_to_all(answers, ("gx", "gy"), split_axis=1, concat_axis=1, tiled=True)
    ground = jnp.take(returned, position, axis=1).reshape(STEPS, 3, building_count)
    storey_mask, disp, vel, hyst, drift = building_start(
        storey_disp, storey_vel, hyst_fraction, branch_flags, yield_drift, storey_count
    )
    for timestep in range(STEPS):
        disp, vel, hyst, drift = building_step(
            disp,
            vel,
            hyst,
            drift,
            ground[timestep],
            stiffness,
            storey_mass,
            yield_drift,
            storey_mask,
        )
    return (current, previous, disp, vel, hyst)


def solution(mesh):
    placed = (
        P(None, "gx", "gy", None),
        P(None, "gx", "gy", None),
        P("gx", "gy", None),
        P("gx", "gy", None),
        P("gx", "gy", None),
        P(None, None, ("gx", "gy")),
        P(None, None, ("gx", "gy")),
        P(None, None, ("gx", "gy")),
        P(None, None, ("gx", "gy")),
        P(None, ("gx", "gy")),
        P(None, ("gx", "gy")),
        P(None, ("gx", "gy")),
        P(("gx", "gy")),
        P(("gx", "gy"), None),
        P(("gx", "gy")),
    )
    return jax.shard_map(
        local,
        mesh=mesh,
        in_specs=placed,
        out_specs=(
            P(None, "gx", "gy", None),
            P(None, "gx", "gy", None),
            P(None, None, ("gx", "gy")),
            P(None, None, ("gx", "gy")),
            P(None, None, ("gx", "gy")),
        ),
        check_vma=False,
    )
```

profile of v0, /device:TPU:1, one launch (start us, length us, event | category | flops | bytes accessed | tf_op | source)
XLA Modules:
  0.0 512.1 jit_solution(793128600443438768)
XLA Ops:
  1.6 4.4 collective-permute-start
  11.6 4.9 collective-permute-start.2
  33.1 4.1 collective-permute-done.5
  37.3 4.6 collective-permute-start.6
  43.9 4.3 collective-permute-done.7
  60.9 4.3 collective-permute-done.9
  84.3 4.1 collective-permute-done.13
  89.2 4.3 collective-permute-start.14
  95.7 4.4 collective-permute-done.15
  113.2 4.0 collective-permute-done.17
  136.0 4.1 collective-permute-done.21
  145.7 4.2 collective-permute-done.23
  157.3 4.6 collective-permute-start.24
  163.2 4.5 scatter_custom_fusion
  168.4 9.5 %all-to-all-start = ((s32[128,16,1]{1,2,0:T(1,128)}), s32[128,16,1]{1,2,0:T(1,128)S(1)}, u32[]{:S(2)}, u32[]{:S(2)}) async-start(s32[128,16,1]{1,2,0:T(1,128)} %bitcast.151), calls=%async_computation | async-start | bytes 131072 | tf_op jit(solution)/shard_map/all_to_all | solution.py:144
  198.1 4.1 collective-permute-done.29
  203.0 4.6 collective-permute-start.30
  214.1 4.3 select_maximum_fusion.16
  230.8 4.9 collective-permute-start.34
  246.0 4.2 collective-permute-start.36
  253.0 4.1 collective-permute-done.37
  257.2 4.9 collective-permute-start.38
  264.4 4.0 collective-permute-done.39
  296.8 4.0 collective-permute-start.44
  303.7 4.1 collective-permute-done.45
  352.8 4.1 collective-permute-done.53
  362.6 4.0 collective-permute-done.55
  401.5 4.1 collective-permute-done.61
  410.5 4.2 collective-permute-done.63
  422.6 7.6 %gather_fusion = f32[2048,24]{1,0:T(8,128)} fusion(f32[24,512]{0,1:T(8,128)S(1)} %copy.471, s32[2048]{0:T(1024)S(1)} %broadcast_clamp_fusion), kind=kCustom, calls=%fused_computation | custom fusion | bytes 401408 | tf_op jit(solution)/shard_map/jit(_take)/gather | solution.py:146
  433.3 8.0 %all-to-all-start.1 = ((f32[128,1,384]{2,1,0:T(1,128)}), f32[128,1,384]{2,1,0:T(1,128)S(1)}, u32[]{:S(2)}, u32[]{:S(2)}) async-start(f32[128,1,384]{2,1,0:T(1,128)} %reshape.185), calls=%async_computation.1 | async-start | bytes 393216 | tf_op jit(solution)/shard_map/all_to_all | solution.py:147
  441.3 10.4 %all-to-all-done.1 = f32[128,1,384]{2,1,0:T(1,128)S(1)} async-done(((f32[128,1,384]{2,1,0:T(1,128)}), f32[128,1,384]{2,1,0:T(1,128)S(1)}, u32[]{:S(2)}, u32[]{:S(2)}) %all-to-all-start.1) | async-done | bytes 196640 | tf_op jit(solution)/shard_map/all_to_all | solution.py:147
  (442 shorter events, 352.5 us)
Async XLA Ops:
  11.6 6.9 %collective-permute-start.2 = (f32[3,20,2,128]{3,2,1,0:T(2,128)S(1)}, f32[3,20,2,128]{3,2,1,0:T(2,128)S(1)}, u32[]{:S(2)}, u32[]{:S(2)}) collective-permute-start(f32[3,20,2,128]{3,2,1,0:T(2,128)S(1)} %get-tuple-element.207), channel_id=1, source_target_pairs={{0,1},{1,2},{2,3},{3,4},{4,5},{5,6},{6,7},{8,9},{9,10},{10,11},{11... | collective-permute-start | bytes 184328 | tf_op jit(solution)/shard_map/ppermute | solution.py:21
  26.8 6.3 %collective-permute-start.4 = (f32[6,2,32,128]{3,2,1,0:T(8,128)S(1)}, f32[6,2,32,128]{3,2,1,0:T(8,128)S(1)}, u32[]{:S(2)}, u32[]{:S(2)}) collective-permute-start(f32[6,2,32,128]{3,2,1,0:T(8,128)S(1)} %get-tuple-element.191), channel_id=1, source_target_pairs={{0,8},{8,16},{16,24},{24,32},{32,40},{40,48},{48,56},{56,64},{64,7... | collective-permute-start | bytes 589832 | tf_op jit(solution)/shard_map/ppermute | solution.py:21
  30.3 6.9 %collective-permute-start.5 = (f32[6,2,32,128]{3,2,1,0:T(8,128)S(1)}, f32[6,2,32,128]{3,2,1,0:T(8,128)S(1)}, u32[]{:S(2)}, u32[]{:S(2)}) collective-permute-start(f32[6,2,32,128]{3,2,1,0:T(8,128)S(1)} %get-tuple-element.192), channel_id=1, source_target_pairs={{8,0},{16,8},{24,16},{32,24},{40,32},{48,40},{56,48},{64,56},{72,6... | collective-permute-start | bytes 589832 | tf_op jit(solution)/shard_map/ppermute | solution.py:22
  37.3 6.6 %collective-permute-start.6 = (f32[6,20,2,128]{3,2,1,0:T(2,128)S(1)}, f32[6,20,2,128]{3,2,1,0:T(2,128)S(1)}, u32[]{:S(2)}, u32[]{:S(2)}) collective-permute-start(f32[6,20,2,128]{3,2,1,0:T(2,128)S(1)} %get-tuple-element.175), channel_id=1, source_target_pairs={{0,1},{1,2},{2,3},{3,4},{4,5},{5,6},{6,7},{8,9},{9,10},{10,11},{11... | collective-permute-start | bytes 368648 | tf_op jit(solution)/shard_map/ppermute | solution.py:21
  41.9 6.2 %collective-permute-start.7 = (f32[6,20,2,128]{3,2,1,0:T(2,128)S(1)}, f32[6,20,2,128]{3,2,1,0:T(2,128)S(1)}, u32[]{:S(2)}, u32[]{:S(2)}) collective-permute-start(f32[6,20,2,128]{3,2,1,0:T(2,128)S(1)} %get-tuple-element.176), channel_id=1, source_target_pairs={{1,0},{2,1},{3,2},{4,3},{5,4},{6,5},{7,6},{9,8},{10,9},{11,10},{12... | collective-permute-start | bytes 368648 | tf_op jit(solution)/shard_map/ppermute | solution.py:22
  77.8 6.5 %collective-permute-start.12 = (f32[6,2,32,128]{3,2,1,0:T(8,128)S(1)}, f32[6,2,32,128]{3,2,1,0:T(8,128)S(1)}, u32[]{:S(2)}, u32[]{:S(2)}) collective-permute-start(f32[6,2,32,128]{3,2,1,0:T(8,128)S(1)} %get-tuple-element.189), channel_id=1, source_target_pairs={{0,8},{8,16},{16,24},{24,32},{32,40},{40,48},{48,56},{56,64},{64,7... | collective-permute-start | bytes 589832 | tf_op jit(solution)/shard_map/ppermute | solution.py:21
  81.6 6.9 %collective-permute-start.13 = (f32[6,2,32,128]{3,2,1,0:T(8,128)S(1)}, f32[6,2,32,128]{3,2,1,0:T(8,128)S(1)}, u32[]{:S(2)}, u32[]{:S(2)}) collective-permute-start(f32[6,2,32,128]{3,2,1,0:T(8,128)S(1)} %get-tuple-element.190), channel_id=1, source_target_pairs={{8,0},{16,8},{24,16},{32,24},{40,32},{48,40},{56,48},{64,56},{72,6... | collective-permute-start | bytes 589832 | tf_op jit(solution)/shard_map/ppermute | solution.py:22
  89.2 6.5 %collective-permute-start.14 = (f32[6,20,2,128]{3,2,1,0:T(2,128)}, f32[6,20,2,128]{3,2,1,0:T(2,128)S(1)}, u32[]{:S(2)}, u32[]{:S(2)}) collective-permute-start(f32[6,20,2,128]{3,2,1,0:T(2,128)} %get-tuple-element.173), channel_id=1, source_target_pairs={{0,1},{1,2},{2,3},{3,4},{4,5},{5,6},{6,7},{8,9},{9,10},{10,11},{11... | collective-permute-start | bytes 368648 | tf_op jit(solution)/shard_map/ppermute | solution.py:21
  93.6 6.5 %collective-permute-start.15 = (f32[6,20,2,128]{3,2,1,0:T(2,128)}, f32[6,20,2,128]{3,2,1,0:T(2,128)}, u32[]{:S(2)}, u32[]{:S(2)}) collective-permute-start(f32[6,20,2,128]{3,2,1,0:T(2,128)} %get-tuple-element.174), channel_id=1, source_target_pairs={{1,0},{2,1},{3,2},{4,3},{5,4},{6,5},{7,6},{9,8},{10,9},{11,10},{12... | collective-permute-start | bytes 368648 | tf_op jit(solution)/shard_map/ppermute | solution.py:22
  129.7 6.4 %collective-permute-start.20 = (f32[6,2,32,128]{3,2,1,0:T(8,128)S(1)}, f32[6,2,32,128]{3,2,1,0:T(8,128)S(1)}, u32[]{:S(2)}, u32[]{:S(2)}) collective-permute-start(f32[6,2,32,128]{3,2,1,0:T(8,128)S(1)} %get-tuple-element.187), channel_id=1, source_target_pairs={{0,8},{8,16},{16,24},{24,32},{32,40},{40,48},{48,56},{56,64},{64,7... | collective-permute-start | bytes 589832 | tf_op jit(solution)/shard_map/ppermute | solution.py:21
  133.3 6.9 %collective-permute-start.21 = (f32[6,2,32,128]{3,2,1,0:T(8,128)S(1)}, f32[6,2,32,128]{3,2,1,0:T(8,128)S(1)}, u32[]{:S(2)}, u32[]{:S(2)}) collective-permute-start(f32[6,2,32,128]{3,2,1,0:T(8,128)S(1)} %get-tuple-element.188), channel_id=1, source_target_pairs={{8,0},{16,8},{24,16},{32,24},{40,32},{48,40},{56,48},{64,56},{72,6... | collective-permute-start | bytes 589832 | tf_op jit(solution)/shard_map/ppermute | solution.py:22
  143.8 6.2 %collective-permute-start.23 = (f32[6,20,2,128]{3,2,1,0:T(2,128)S(1)}, f32[6,20,2,128]{3,2,1,0:T(2,128)S(1)}, u32[]{:S(2)}, u32[]{:S(2)}) collective-permute-start(f32[6,20,2,128]{3,2,1,0:T(2,128)S(1)} %get-tuple-element.172), channel_id=1, source_target_pairs={{1,0},{2,1},{3,2},{4,3},{5,4},{6,5},{7,6},{9,8},{10,9},{11,10},{12... | collective-permute-start | bytes 368648 | tf_op jit(solution)/shard_map/ppermute | solution.py:22
  157.3 20.6 %collective-permute-start.24 = (f32[3,2,32,128]{3,2,1,0:T(8,128)S(1)}, f32[3,2,32,128]{3,2,1,0:T(8,128)S(1)}, u32[]{:S(2)}, u32[]{:S(2)}) collective-permute-start(f32[3,2,32,128]{3,2,1,0:T(8,128)S(1)} %get-tuple-element.217), channel_id=1, source_target_pairs={{0,8},{8,16},{16,24},{24,32},{32,40},{40,48},{48,56},{56,64},{64,7... | collective-permute-start | bytes 294920 | tf_op jit(solution)/shard_map/ppermute | solution.py:21
  161.9 16.1 %collective-permute-start.25 = (f32[3,2,32,128]{3,2,1,0:T(8,128)S(1)}, f32[3,2,32,128]{3,2,1,0:T(8,128)S(1)}, u32[]{:S(2)}, u32[]{:S(2)}) collective-permute-start(f32[3,2,32,128]{3,2,1,0:T(8,128)S(1)} %get-tuple-element.218), channel_id=1, source_target_pairs={{8,0},{16,8},{24,16},{32,24},{40,32},{48,40},{56,48},{64,56},{72,6... | collective-permute-start | bytes 294920 | tf_op jit(solution)/shard_map/ppermute | solution.py:22
  168.4 43.6 %all-to-all-start = ((s32[128,16,1]{1,2,0:T(1,128)}), s32[128,16,1]{1,2,0:T(1,128)S(1)}, u32[]{:S(2)}, u32[]{:S(2)}) async-start(s32[128,16,1]{1,2,0:T(1,128)} %bitcast.151), calls=%async_computation | async-start | bytes 131072 | tf_op jit(solution)/shard_map/all_to_all | solution.py:144
  195.3 6.9 %collective-permute-start.29 = (f32[6,2,32,128]{3,2,1,0:T(8,128)S(1)}, f32[6,2,32,128]{3,2,1,0:T(8,128)S(1)}, u32[]{:S(2)}, u32[]{:S(2)}) collective-permute-start(f32[6,2,32,128]{3,2,1,0:T(8,128)S(1)} %get-tuple-element.186), channel_id=1, source_target_pairs={{8,0},{16,8},{24,16},{32,24},{40,32},{48,40},{56,48},{64,56},{72,6... | collective-permute-start | bytes 589832 | tf_op jit(solution)/shard_map/ppermute | solution.py:22
  203.0 10.5 %collective-permute-start.30 = (f32[6,20,2,128]{3,2,1,0:T(2,128)}, f32[6,20,2,128]{3,2,1,0:T(2,128)}, u32[]{:S(2)}, u32[]{:S(2)}) collective-permute-start(f32[6,20,2,128]{3,2,1,0:T(2,128)} %get-tuple-element.169), channel_id=1, source_target_pairs={{0,1},{1,2},{2,3},{3,4},{4,5},{5,6},{6,7},{8,9},{9,10},{10,11},{11... | collective-permute-start | bytes 368648 | tf_op jit(solution)/shard_map/ppermute | solution.py:21
  207.6 6.5 %collective-permute-start.31 = (f32[6,20,2,128]{3,2,1,0:T(2,128)}, f32[6,20,2,128]{3,2,1,0:T(2,128)}, u32[]{:S(2)}, u32[]{:S(2)}) collective-permute-start(f32[6,20,2,128]{3,2,1,0:T(2,128)} %get-tuple-element.170), channel_id=1, source_target_pairs={{1,0},{2,1},{3,2},{4,3},{5,4},{6,5},{7,6},{9,8},{10,9},{11,10},{12... | collective-permute-start | bytes 368648 | tf_op jit(solution)/shard_map/ppermute | solution.py:22
  230.8 7.1 %collective-permute-start.34 = (f32[3,20,2,128]{3,2,1,0:T(2,128)S(1)}, f32[3,20,2,128]{3,2,1,0:T(2,128)S(1)}, u32[]{:S(2)}, u32[]{:S(2)}) collective-permute-start(f32[3,20,2,128]{3,2,1,0:T(2,128)S(1)} %get-tuple-element.199), channel_id=1, source_target_pairs={{0,1},{1,2},{2,3},{3,4},{4,5},{5,6},{6,7},{8,9},{9,10},{10,11},{11... | collective-permute-start | bytes 184328 | tf_op jit(solution)/shard_map/ppermute | solution.py:21
  246.0 7.0 %collective-permute-start.36 = (f32[6,2,32,128]{3,2,1,0:T(8,128)S(1)}, f32[6,2,32,128]{3,2,1,0:T(8,128)S(1)}, u32[]{:S(2)}, u32[]{:S(2)}) collective-permute-start(f32[6,2,32,128]{3,2,1,0:T(8,128)S(1)} %get-tuple-element.183), channel_id=1, source_target_pairs={{0,8},{8,16},{16,24},{24,32},{32,40},{40,48},{48,56},{56,64},{64,7... | collective-permute-start | bytes 589832 | tf_op jit(solution)/shard_map/ppermute | solution.py:21
  250.2 6.9 %collective-permute-start.37 = (f32[6,2,32,128]{3,2,1,0:T(8,128)S(1)}, f32[6,2,32,128]{3,2,1,0:T(8,128)S(1)}, u32[]{:S(2)}, u32[]{:S(2)}) collective-permute-start(f32[6,2,32,128]{3,2,1,0:T(8,128)S(1)} %get-tuple-element.184), channel_id=1, source_target_pairs={{8,0},{16,8},{24,16},{32,24},{40,32},{48,40},{56,48},{64,56},{72,6... | collective-permute-start | bytes 589832 | tf_op jit(solution)/shard_map/ppermute | solution.py:22
  257.2 7.1 %collective-permute-start.38 = (f32[6,20,2,128]{3,2,1,0:T(2,128)S(1)}, f32[6,20,2,128]{3,2,1,0:T(2,128)S(1)}, u32[]{:S(2)}, u32[]{:S(2)}) collective-permute-start(f32[6,20,2,128]{3,2,1,0:T(2,128)S(1)} %get-tuple-element.167), channel_id=1, source_target_pairs={{0,1},{1,2},{2,3},{3,4},{4,5},{5,6},{6,7},{8,9},{9,10},{10,11},{11... | collective-permute-start | bytes 368648 | tf_op jit(solution)/shard_map/ppermute | solution.py:21
  262.1 6.2 %collective-permute-start.39 = (f32[6,20,2,128]{3,2,1,0:T(2,128)S(1)}, f32[6,20,2,128]{3,2,1,0:T(2,128)S(1)}, u32[]{:S(2)}, u32[]{:S(2)}) collective-permute-start(f32[6,20,2,128]{3,2,1,0:T(2,128)S(1)} %get-tuple-element.168), channel_id=1, source_target_pairs={{1,0},{2,1},{3,2},{4,3},{5,4},{6,5},{7,6},{9,8},{10,9},{11,10},{12... | collective-permute-start | bytes 368648 | tf_op jit(solution)/shard_map/ppermute | solution.py:22
  296.8 6.8 %collective-permute-start.44 = (f32[6,2,32,128]{3,2,1,0:T(8,128)S(1)}, f32[6,2,32,128]{3,2,1,0:T(8,128)S(1)}, u32[]{:S(2)}, u32[]{:S(2)}) collective-permute-start(f32[6,2,32,128]{3,2,1,0:T(8,128)S(1)} %get-tuple-element.181), channel_id=1, source_target_pairs={{0,8},{8,16},{16,24},{24,32},{32,40},{40,48},{48,56},{56,64},{64,7... | collective-permute-start | bytes 589832 | tf_op jit(solution)/shard_map/ppermute | solution.py:21
  300.9 6.9 %collective-permute-start.45 = (f32[6,2,32,128]{3,2,1,0:T(8,128)S(1)}, f32[6,2,32,128]{3,2,1,0:T(8,128)S(1)}, u32[]{:S(2)}, u32[]{:S(2)}) collective-permute-start(f32[6,2,32,128]{3,2,1,0:T(8,128)S(1)} %get-tuple-element.182), channel_id=1, source_target_pairs={{8,0},{16,8},{24,16},{32,24},{40,32},{48,40},{56,48},{64,56},{72,6... | collective-permute-start | bytes 589832 | tf_op jit(solution)/shard_map/ppermute | solution.py:22
  311.7 6.2 %collective-permute-start.47 = (f32[6,20,2,128]{3,2,1,0:T(2,128)S(1)}, f32[6,20,2,128]{3,2,1,0:T(2,128)S(1)}, u32[]{:S(2)}, u32[]{:S(2)}) collective-permute-start(f32[6,20,2,128]{3,2,1,0:T(2,128)S(1)} %get-tuple-element.166), channel_id=1, source_target_pairs={{1,0},{2,1},{3,2},{4,3},{5,4},{6,5},{7,6},{9,8},{10,9},{11,10},{12... | collective-permute-start | bytes 368648 | tf_op jit(solution)/shard_map/ppermute | solution.py:22
  346.3 6.5 %collective-permute-start.52 = (f32[6,2,32,128]{3,2,1,0:T(8,128)S(1)}, f32[6,2,32,128]{3,2,1,0:T(8,128)S(1)}, u32[]{:S(2)}, u32[]{:S(2)}) collective-permute-start(f32[6,2,32,128]{3,2,1,0:T(8,128)S(1)} %get-tuple-element.179), channel_id=1, source_target_pairs={{0,8},{8,16},{16,24},{24,32},{32,40},{40,48},{48,56},{56,64},{64,7... | collective-permute-start | bytes 589832 | tf_op jit(solution)/shard_map/ppermute | solution.py:21
  350.0 6.9 %collective-permute-start.53 = (f32[6,2,32,128]{3,2,1,0:T(8,128)S(1)}, f32[6,2,32,128]{3,2,1,0:T(8,128)S(1)}, u32[]{:S(2)}, u32[]{:S(2)}) collective-permute-start(f32[6,2,32,128]{3,2,1,0:T(8,128)S(1)} %get-tuple-element.180), channel_id=1, source_target_pairs={{8,0},{16,8},{24,16},{32,24},{40,32},{48,40},{56,48},{64,56},{72,6... | collective-permute-start | bytes 589832 | tf_op jit(solution)/shard_map/ppermute | solution.py:22
  360.4 6.2 %collective-permute-start.55 = (f32[6,20,2,128]{3,2,1,0:T(2,128)S(1)}, f32[6,20,2,128]{3,2,1,0:T(2,128)S(1)}, u32[]{:S(2)}, u32[]{:S(2)}) collective-permute-start(f32[6,20,2,128]{3,2,1,0:T(2,128)S(1)} %get-tuple-element.164), channel_id=1, source_target_pairs={{1,0},{2,1},{3,2},{4,3},{5,4},{6,5},{7,6},{9,8},{10,9},{11,10},{12... | collective-permute-start | bytes 368648 | tf_op jit(solution)/shard_map/ppermute | solution.py:22
  395.0 6.5 %collective-permute-start.60 = (f32[6,2,32,128]{3,2,1,0:T(8,128)S(1)}, f32[6,2,32,128]{3,2,1,0:T(8,128)S(1)}, u32[]{:S(2)}, u32[]{:S(2)}) collective-permute-start(f32[6,2,32,128]{3,2,1,0:T(8,128)S(1)} %get-tuple-element.177), channel_id=1, source_target_pairs={{0,8},{8,16},{16,24},{24,32},{32,40},{40,48},{48,56},{56,64},{64,7... | collective-permute-start | bytes 589832 | tf_op jit(solution)/shard_map/ppermute | solution.py:21
  398.7 6.9 %collective-permute-start.61 = (f32[6,2,32,128]{3,2,1,0:T(8,128)S(1)}, f32[6,2,32,128]{3,2,1,0:T(8,128)S(1)}, u32[]{:S(2)}, u32[]{:S(2)}) collective-permute-start(f32[6,2,32,128]{3,2,1,0:T(8,128)S(1)} %get-tuple-element.178), channel_id=1, source_target_pairs={{8,0},{16,8},{24,16},{32,24},{40,32},{48,40},{56,48},{64,56},{72,6... | collective-permute-start | bytes 589832 | tf_op jit(solution)/shard_map/ppermute | solution.py:22
  433.3 18.4 %all-to-all-start.1 = ((f32[128,1,384]{2,1,0:T(1,128)}), f32[128,1,384]{2,1,0:T(1,128)S(1)}, u32[]{:S(2)}, u32[]{:S(2)}) async-start(f32[128,1,384]{2,1,0:T(1,128)} %reshape.185), calls=%async_computation.1 | async-start | bytes 393216 | tf_op jit(solution)/shard_map/all_to_all | solution.py:147
  (91 other events, 563.9 us)
where the time goes:
time: 522 us; the launch traced here: 512 us
  starting transfers between devices  191 us (37%)
  waiting for transfers between devices  138 us (26%)
  other arithmetic  122 us (23%)
  local copies, waits for them, and re-layouts  56.6 us (11%)
    ppermute x32, starting transfers between devices, with_halo(): before = lax.ppermute(last, axis, up)  121 us
    ppermute x32, waiting for transfers between devices, with_halo(): after = lax.ppermute(first, axis, down)  115 us
    ppermute x32, starting transfers between devices, with_halo(): after = lax.ppermute(first, axis, down)  53.2 us
    concatenate x16, other arithmetic, with_halo(): array = jnp.concatenate([before, array, after], axis=dim)  34.5 us
    mul x8, other arithmetic, building_step(): disp = (disp + time_step * vel) * storey_mask  23.4 us
    another operation x24, other arithmetic, divergence(): return jnp.stack([force_x, force_y, force_z])  19.6 us
    unnamed x41, other arithmetic  18.5 us
    ppermute x32, waiting for transfers between devices, with_halo(): before = lax.ppermute(last, axis, up)  12.9 us
  transfers between devices with their start and end apart: 66, of which 48 were waited for; matrix products, arithmetic and copies ran while one was open for 3% of the time, Pallas kernels for 0%

commit v1 on v0

v1 whole, which is shorter than its diff:
```python
import jax
import jax.numpy as jnp
from jax import lax
from jax.experimental import pallas as pl
from jax.experimental.pallas import tpu as pltpu
from jax.sharding import PartitionSpec as P

STEPS = 8
DT = 0.35
POST = 0.1
DAMP = 0.05
F32 = jnp.float32
BF16 = jnp.bfloat16
VM = pl.BlockSpec(memory_space=pltpu.VMEM)
SM = pl.BlockSpec(memory_space=pltpu.SMEM)
HB = pl.BlockSpec(memory_space=pl.ANY)
CP = pltpu.CompilerParams(vmem_limit_bytes=56 << 20)
YR = 56

XPARTS = ((0, 3, 8), (1, 3, 4), (2, 1, 6), (3, 1, 6), (4, 1, 4))
XPLANES = sum(c * w for _, c, w in XPARTS)
YBLOCKS = sum(c * (16 + 2 * w) for _, c, w in XPARTS)


def sds(*shape):
    return jax.ShapeDtypeStruct(shape, F32)


def ring(x, axis, step):
    n = lax.axis_size(axis)
    return lax.ppermute(x, axis, [(i, (i + step) % n) for i in range(n)])


def split3(x):
    hi = x.astype(BF16)
    rest = x - hi.astype(F32)
    mid = rest.astype(BF16)
    low = (rest - mid.astype(F32)).astype(BF16)
    return hi, mid, low


def at_comp(ref, comps, c, rows, cols):
    return ref.at[c, rows, cols] if comps == 3 else ref.at[rows, cols]


def pack_x_kernel(u, p, la, mu, de, up, down, sem):
    args = (u, p, la, mu, de)
    copies = []
    off = 0
    for a, comps, w in XPARTS:
        for c in range(comps):
            full = pl.ds(0, 32)
            src_up = at_comp(args[a], comps, c, pl.ds(16 - w, w), full)
            src_dn = at_comp(args[a], comps, c, pl.ds(0, w), full)
            n = len(copies)
            copies.append(pltpu.make_async_copy(src_up, up.at[pl.ds(off, w)], sem.at[n]))
            copies.append(pltpu.make_async_copy(src_dn, down.at[pl.ds(off, w)], sem.at[n + 1]))
            off += w
    for cp in copies:
        cp.start()
    for cp in copies:
        cp.wait()


def pack_y_kernel(u, p, la, mu, de, north, south, up, down, sem):
    args = (u, p, la, mu, de)
    copies = []
    off = 0
    src = 0
    for a, comps, w in XPARTS:
        for c in range(comps):
            for dst, col in ((up, 24), (down, 0)):
                n = len(copies)
                s = at_comp(args[a], comps, c, pl.ds(0, 16), pl.ds(col, 8))
                cp = pltpu.make_async_copy(s, dst.at[pl.ds(off + w, 16)], sem.at[n])
                cp.start()
                copies.append(cp)
                dst[off : off + w] = north[src : src + w, col : col + 8]
                dst[off + w + 16 : off + 2 * w + 16] = south[src : src + w, col : col + 8]
            off += 16 + 2 * w
            src += w
    for cp in copies:
        cp.wait()


def pack_round_kernel(top, bot, north, south, up, down):
    for dst, col in ((up, 24), (down, 0)):
        dst[:, 0:8] = north[:, :, col : col + 8]
        dst[:, 8:16] = top[:, :, col : col + 8]
        dst[:, 16:24] = bot[:, :, col : col + 8]
        dst[:, 24:32] = south[:, :, col : col + 8]


def lane_coefs():
    z = lax.broadcasted_iota(jnp.int32, (8, 128), 1)
    one = jnp.full((8, 128), 1.0, F32)
    zero = jnp.zeros((8, 128), F32)
    return (
        jnp.where(z < 127, 8.0 * one, zero),
        jnp.where(z >= 1, 8.0 * one, zero),
        jnp.where(z < 126, one, zero),
        jnp.where(z >= 2, one, zero),
    )


def dz(f, coefs):
    cp1, cm1, cp2, cm2 = coefs
    near = cp1 * pltpu.roll(f, 127, 1) - cm1 * pltpu.roll(f, 1, 1)
    far = cp2 * pltpu.roll(f, 126, 1) - cm2 * pltpu.roll(f, 2, 1)
    return near - far


def dx(ref, c, x, y):
    ys = pl.ds(y, 8)
    near = ref[c, x + 1, ys] - ref[c, x - 1, ys]
    far = ref[c, x + 2, ys] - ref[c, x - 2, ys]
    return 8.0 * near - far


def dy(ref, c, x, y):
    near = ref[c, x, pl.ds(y + 1, 8)] - ref[c, x, pl.ds(y - 1, 8)]
    far = ref[c, x, pl.ds(y + 2, 8)] - ref[c, x, pl.ds(y - 2, 8)]
    return 8.0 * near - far


def stress_pass(u, ux, s, lam, mu, x0, nx, y0, blocks):
    def body(i, carry):
        coefs = lane_coefs()
        gx = i + x0
        x = gx - ux
        for b in range(blocks):
            y = y0 + 8 * b
            ys = pl.ds(y, 8)
            m = mu[gx - 2, ys]
            la = lam[gx - 2, ys]
            g00 = dx(u, 0, x, y)
            g11 = dy(u, 1, x, y)
            g22 = dz(u[2, x, ys], coefs)
            lt = la * (g00 + g11 + g22)
            m2 = m + m
            s[0, gx, ys] = lt + m2 * g00
            s[1, gx, ys] = lt + m2 * g11
            s[2, gx, ys] = lt + m2 * g22
            s[3, gx, ys] = m * (dy(u, 0, x, y) + dx(u, 1, x, y))
            s[4, gx, ys] = m * (dz(u[0, x, ys], coefs) + dx(u, 2, x, y))
            s[5, gx, ys] = m * (dz(u[1, x, ys], coefs) + dy(u, 2, x, y))
        return carry

    lax.fori_loop(0, nx, body, 0)


def force(s, q, x, y, coefs):
    ys = pl.ds(y, 8)
    f0 = dx(s, 0, x, y) + dy(s, 3, x, y) + dz(s[4, x, ys], coefs)
    f1 = dx(s, 3, x, y) + dy(s, 1, x, y) + dz(s[5, x, ys], coefs)
    f2 = dx(s, 4, x, y) + dy(s, 5, x, y) + dz(s[2, x, ys], coefs)
    return q * f0, q * f1, q * f2


def surface(fs, slot, old):
    lane = lax.broadcasted_iota(jnp.int32, (8, 128), 1)
    for c, f in enumerate(fs):
        v = pltpu.roll(f, slot + c, 1) if slot + c else f
        old = jnp.where(lane == slot + c, v, old)
    return old


def wave_two_steps(ue, prev, lam, mu, q, s, hs, u1, hist, store):
    stress_pass(ue, 0, s, lam, mu, 2, 28, 2, 6)

    def first(i, carry):
        coefs = lane_coefs()
        for b in range(5):
            y = 4 + 8 * b
            ys = pl.ds(y, 8)
            fs = force(s, q[i, ys], i + 4, y, coefs)
            hs[i, 8 * b : 8 * b + 8] = surface(fs, 0, jnp.zeros((8, 128), F32))
            for c in range(3):
                now = ue[c, i + 4, ys]
                u1[c, i, ys] = (now - prev[c, i, ys]) + (now + fs[c])
        return carry

    lax.fori_loop(0, 24, first, 0)
    stress_pass(u1, 4, s, lam, mu, 6, 20, 6, 5)

    def second(part):
        def body(j, carry):
            i = j + 8 * part
            coefs = lane_coefs()
            for b in range(4):
                y = 8 + 8 * b
                ys = pl.ds(y, 8)
                fs = force(s, q[i + 4, ys], i + 8, y, coefs)
                r = pl.multiple_of(i * 32 + 8 * b, 8)
                hist[pl.ds(r, 8)] = surface(fs, 3, hs[i + 4, 8 * b + 4 : 8 * b + 12])
                for c in range(3):
                    now = u1[c, i + 4, ys]
                    store(part, c, j, 8 * b, (now - ue[c, i + 8, ys]) + (now + fs[c]))
            return carry

        lax.fori_loop(0, 8, body, 0)

    second(0)
    second(1)


def fill(ext, c, w, lead, parts, flags):
    center, north, south, west, east = parts
    fn, fs, fw, fe = flags
    ref = ext if lead is None else ext.at[lead]

    def row(i, f):
        ref[i, 0:8] = west(i) * (f * fw)
        ref[i, 40:48] = east(i) * (f * fe)

    for i in range(w):
        row(i, fn)
        ref[i, 8:40] = north(i) * fn
        row(16 + w + i, fs)
        ref[16 + w + i, 8:40] = south(i) * fs

    def mid(i, carry):
        row(w + i, 1.0)
        ref[w + i, 8:40] = center(i)
        return carry

    lax.fori_loop(0, 16, mid, 0)


def first_round_kernel(flags, u, p, la, mu, de, north, south, west, east, top, bot, u1, lam, muo, q, hist, ue, pe, s, hs):
    fl = [flags[0, k] for k in range(4)]
    args = (u, p, la, mu, de)
    exts = (ue, pe, lam, muo, q)
    src = 0
    off = 0
    for a, comps, w in XPARTS:
        for c in range(comps):
            arg = args[a]
            parts = (
                (lambda i, arg=arg, c=c: arg[c, i]) if comps == 3 else (lambda i, arg=arg: arg[i]),
                lambda i, src=src: north[src + i],
                lambda i, src=src: south[src + i],
                lambda i, off=off: west[off + i],
                lambda i, off=off: east[off + i],
            )
            fill(exts[a], c, w, c if comps == 3 else None, parts, fl)
            src += w
            off += 16 + 2 * w

    def scale(i, carry):
        lam[i] = lam[i] * (1.0 / 12.0)
        muo[i] = muo[i] * (1.0 / 12.0)
        return carry

    lax.fori_loop(0, 28, scale, 0)

    def invert(i, carry):
        d = q[i]
        q[i] = jnp.where(d > 0.0, (DT * DT / 12.0) / jnp.where(d > 0.0, d, 1.0), 0.0)
        return carry

    lax.fori_loop(0, 24, invert, 0)
    finish_rows(ue, pe, lam, muo, q, s, hs, u1, hist, top, bot)


def finish_rows(ue, pe, lam, mu, q, s, hs, u1, hist, top, bot):
    def store(part, c, j, y, v):
        (top, bot)[part][c, j, pl.ds(y, 8)] = v

    wave_two_steps(ue, pe, lam, mu, q, s, hs, u1, hist, store)


def fill_round(flags, top, bot, north, south, west, east, ue):
    fn, fs, fw, fe = [flags[0, k] for k in range(4)]
    for c in range(3):

        def rows(i, carry, c=c):
            ue[c, i, 0:8] = west[c, i] * (fn * fw)
            ue[c, i, 8:40] = north[c, i] * fn
            ue[c, i, 40:48] = east[c, i] * (fn * fe)
            ue[c, 8 + i, 0:8] = west[c, 8 + i] * fw
            ue[c, 8 + i, 8:40] = top[c, i]
            ue[c, 8 + i, 40:48] = east[c, 8 + i] * fe
            ue[c, 16 + i, 0:8] = west[c, 16 + i] * fw
            ue[c, 16 + i, 8:40] = bot[c, i]
            ue[c, 16 + i, 40:48] = east[c, 16 + i] * fe
            ue[c, 24 + i, 0:8] = west[c, 24 + i] * (fs * fw)
            ue[c, 24 + i, 8:40] = south[c, i] * fs
            ue[c, 24 + i, 40:48] = east[c, 24 + i] * (fs * fe)
            return carry

        lax.fori_loop(0, 8, rows, 0)


def round_kernel(flags, top, bot, north, south, west, east, prev, lam, mu, q, top2, bot2, u1, hist, ue, s, hs):
    fill_round(flags, top, bot, north, south, west, east, ue)
    finish_rows(ue, prev, lam, mu, q, s, hs, u1, hist, top2, bot2)


def last_kernel(flags, top, bot, north, south, west, east, prev, lam, mu, q, now, before, hist, ue, s, hs, u1):
    fill_round(flags, top, bot, north, south, west, east, ue)

    def store(part, c, j, y, v):
        i = j + 8 * part
        now[c, i, pl.ds(y, 8)] = v
        before[c, i, pl.ds(y, 8)] = u1[c, i + 4, pl.ds(y + 8, 8)]

    wave_two_steps(ue, prev, lam, mu, q, s, hs, u1, hist, store)


def request_kernel(tile, cell, req, key, kmod, a_ref, bhi, blo):
    ones = jnp.ones((128, 128), F32)
    sub = lax.broadcasted_iota(jnp.int32, (128, 128), 0)
    lan = lax.broadcasted_iota(jnp.int32, (128, 128), 1)
    cols = [(ones * tile[i : i + 1, :]).T for i in range(8)]
    row512 = lax.broadcasted_iota(jnp.int32, (512, 128), 0).astype(F32)
    subf = sub.astype(F32)
    for j in range(8):
        mine = tile[j : j + 1, :]
        acc = jnp.where((cols[j] == mine) & (sub < lan), 1.0, 0.0)
        for i in range(j):
            acc = acc + jnp.where(cols[i] == mine, 1.0, 0.0)
        rank = jnp.sum(acc, axis=0, keepdims=True)
        quarter = jnp.floor(rank * 0.25)
        kj = mine * 4.0 + quarter
        mj = rank - 4.0 * quarter
        key[j : j + 1, :] = kj
        kmod[j : j + 1, :] = mj
        lanes = pl.ds(128 * j, 128)
        a_ref[:, lanes] = jnp.where(row512 == kj, 1.0, 0.0).astype(BF16)
        cj = cell[j : j + 1, :]
        hi = jnp.floor(cj * (1.0 / 32.0))
        hit = subf == mj
        bhi[:, lanes] = jnp.where(hit, hi, 0.0).astype(BF16)
        blo[:, lanes] = jnp.where(hit, cj - 32.0 * hi, 0.0).astype(BF16)
    dims = (((1,), (1,)), ((), ()))
    top = lax.dot_general(a_ref[...], bhi[...], dims, preferred_element_type=F32)
    low = lax.dot_general(a_ref[...], blo[...], dims, preferred_element_type=F32)
    req[...] = (32.0 * top + low).reshape(128, 4, 128)


def answer_kernel(inc, h0, h1, h2, h3, out, hs):
    h = h0[...] + pltpu.roll(h1[...], 6, 1) + pltpu.roll(h2[...], 12, 1) + pltpu.roll(h3[...], 18, 1)
    cells = inc[...].reshape(512, 128)
    lane = lax.broadcasted_iota(jnp.int32, (512, 512), 1).astype(F32)
    acc = jnp.zeros((512, 128), F32)
    for k in range(4):
        hot = jnp.where(lane == cells[:, k : k + 1], 1.0, 0.0).astype(BF16)
        for piece in split3(pltpu.roll(h, 32 * k, 1) if k else h):
            acc = acc + jnp.dot(hot, piece, preferred_element_type=F32)
    out[...] = acc.reshape(128, 4, 128)


def building_kernel(ret, key, kmod, d_in, v_in, hf, br, st, ms, yd, cnt, d_out, v_out, h_out, pieces):
    @pl.when(pl.program_id(0) == 0)
    def _():
        full = ret[...].reshape(512, 128).T
        for n, piece in enumerate(split3(full)):
            pieces[n] = piece

    row512 = lax.broadcasted_iota(jnp.int32, (512, 128), 0).astype(F32)
    hot = jnp.where(row512 == key[0], 1.0, 0.0).astype(BF16)
    g = jnp.dot(pieces[0], hot, preferred_element_type=F32)
    g = g + jnp.dot(pieces[1], hot, preferred_element_type=F32)
    g = g + jnp.dot(pieces[2], hot, preferred_element_type=F32)
    km = kmod[0]
    ground = jnp.zeros((32, 128), F32)
    for k in range(4):
        ground = ground + jnp.where(km == k, g[32 * k : 32 * k + 32], 0.0)
    ground = ground * (1.0 / DT)
    level = lax.broadcasted_iota(jnp.int32, (64, 128), 0)
    mask = jnp.where(level < cnt[0], 1.0, 0.0)
    stiff = st[...] * mask
    yld = yd[...] * mask
    gain = DT / ms[...]
    first_row = level == 0
    last_row = level == 63

    def drift_of(x):
        return x - jnp.where(first_row, 0.0, pltpu.roll(x, 1, 0))

    for c in range(3):
        disp = d_in[c] * mask
        vel = v_in[c] * mask
        flag = br[c]
        hyst = jnp.where(flag == 1, yld, jnp.where(flag == 2, -yld, hf[c] * yld))
        drift = drift_of(disp)
        for t in range(STEPS):
            spring = stiff * (POST * drift + (1.0 - POST) * hyst)
            above = jnp.where(last_row, 0.0, pltpu.roll(spring, 63, 0))
            row = ground[3 * t + c : 3 * t + c + 1]
            vel = vel * (1.0 - DT * DAMP) + (gain * (above - spring) - mask * row)
            disp = disp + DT * vel
            new = drift_of(disp)
            hyst = jnp.minimum(jnp.maximum(hyst + new - drift, -yld), yld)
            drift = new
        d_out[c] = disp
        v_out[c] = vel
        h_out[c] = hyst


def local(u, p, de, mu, la, sd, sv, hf, br, st, ms, yd, cnt, tile, cell):
    ix = lax.axis_index("gx")
    iy = lax.axis_index("gy")
    nx = lax.axis_size("gx")
    ny = lax.axis_size("gy")
    edge = jnp.stack([ix > 0, ix < nx - 1, iy > 0, iy < ny - 1]).astype(F32).reshape(1, 4)

    up, down = pl.pallas_call(
        pack_x_kernel,
        out_shape=[sds(XPLANES, 32, 128)] * 2,
        in_specs=[HB] * 5,
        out_specs=[VM] * 2,
        scratch_shapes=[pltpu.SemaphoreType.DMA((18,))],
        compiler_params=CP,
        name="pack_x",
    )(u, p, la, mu, de)
    north = ring(up, "gx", 1)
    south = ring(down, "gx", -1)

    req, key, kmod = pl.pallas_call(
        request_kernel,
        out_shape=[sds(128, 4, 128), sds(8, 128), sds(8, 128)],
        in_specs=[VM] * 2,
        out_specs=[VM] * 3,
        scratch_shapes=[pltpu.VMEM((512, 1024), BF16), pltpu.VMEM((128, 1024), BF16), pltpu.VMEM((128, 1024), BF16)],
        compiler_params=CP,
        name="requests",
    )(tile.reshape(8, 128).astype(F32), cell.reshape(8, 128).astype(F32))
    incoming = lax.all_to_all(req, ("gx", "gy"), 0, 0, tiled=True)

    up, down = pl.pallas_call(
        pack_y_kernel,
        out_shape=[sds(YBLOCKS, 8, 128)] * 2,
        in_specs=[HB] * 5 + [VM] * 2,
        out_specs=[VM] * 2,
        scratch_shapes=[pltpu.SemaphoreType.DMA((18,))],
        compiler_params=CP,
        name="pack_y",
    )(u, p, la, mu, de, north, south)
    west = ring(up, "gy", 1)
    east = ring(down, "gy", -1)

    half = sds(3, 8, 32, 128)
    ue = pltpu.VMEM((3, 32, YR, 128), F32)
    ss = pltpu.VMEM((6, 32, YR, 128), F32)
    hh = pltpu.VMEM((24, 48, 128), F32)
    u1s = sds(3, 24, YR, 128)
    top, bot, prev, lam, mu2, q, hist = pl.pallas_call(
        first_round_kernel,
        out_shape=[half, half, u1s, sds(28, YR, 128), sds(28, YR, 128), sds(24, YR, 128), sds(512, 128)],
        in_specs=[SM] + [VM] * 9,
        out_specs=[VM] * 7,
        scratch_shapes=[ue, pltpu.VMEM((3, 24, YR, 128), F32), ss, hh],
        compiler_params=CP,
        name="wave_first",
    )(edge, u, p, la, mu, de, north, south, west, east)
    hists = [hist]
    for r in range(1, 4):
        north = ring(bot, "gx", 1)
        south = ring(top, "gx", -1)
        up, down = pl.pallas_call(
            pack_round_kernel,
            out_shape=[sds(3, 32, 8, 128)] * 2,
            in_specs=[VM] * 4,
            out_specs=[VM] * 2,
            compiler_params=CP,
            name="pack_round",
        )(top, bot, north, south)
        west = ring(up, "gy", 1)
        east = ring(down, "gy", -1)
        ins = (edge, top, bot, north, south, west, east, prev, lam, mu2, q)
        if r < 3:
            top, bot, prev, hist = pl.pallas_call(
                round_kernel,
                out_shape=[half, half, u1s, sds(512, 128)],
                in_specs=[SM] + [VM] * 10,
                out_specs=[VM] * 4,
                scratch_shapes=[ue, ss, hh],
                compiler_params=CP,
                name="wave_round",
            )(*ins)
        else:
            now, before, hist = pl.pallas_call(
                last_kernel,
                out_shape=[sds(3, 16, 32, 128)] * 2 + [sds(512, 128)],
                in_specs=[SM] + [VM] * 10,
                out_specs=[VM] * 3,
                scratch_shapes=[ue, ss, hh, pltpu.VMEM((3, 24, YR, 128), F32)],
                compiler_params=CP,
                name="wave_last",
            )(*ins)
        hists.append(hist)

    answers = pl.pallas_call(
        answer_kernel,
        out_shape=sds(128, 4, 128),
        in_specs=[VM] * 5,
        out_specs=VM,
        scratch_shapes=[pltpu.VMEM((8, 128), F32)],
        compiler_params=CP,
        name="answers",
    )(incoming, *hists)
    returned = lax.all_to_all(answers, ("gx", "gy"), 0, 0, tiled=True)

    lanes3 = pl.BlockSpec((3, 64, 128), lambda i: (0, 0, i))
    lanes2 = pl.BlockSpec((64, 128), lambda i: (0, i))
    rows = pl.BlockSpec((1, 1, 128), lambda i: (i, 0, 0))
    disp, vel, hyst = pl.pallas_call(
        building_kernel,
        out_shape=[sds(3, 64, 1024)] * 3,
        grid=(8,),
        in_specs=[pl.BlockSpec((128, 4, 128), lambda i: (0, 0, 0)), rows, rows]
        + [lanes3] * 4
        + [lanes2] * 3
        + [rows],
        out_specs=[lanes3] * 3,
        scratch_shapes=[pltpu.VMEM((3, 128, 512), BF16)],
        compiler_params=CP,
        name="buildings",
    )(
        returned,
        key.reshape(8, 1, 128),
        kmod.reshape(8, 1, 128),
        sd,
        sv,
        hf,
        br,
        st,
        ms,
        yd,
        cnt.reshape(8, 1, 128),
    )
    return now, before, disp, vel, hyst


def solution(mesh):
    grid = P(None, "gx", "gy", None)
    cells = P("gx", "gy", None)
    both = ("gx", "gy")
    b3 = P(None, None, both)
    b2 = P(None, both)
    b1 = P(both)
    return jax.shard_map(
        local,
        mesh=mesh,
        in_specs=(grid, grid, cells, cells, cells, b3, b3, b3, b3, b2, b2, b2, b1, P(both, None), b1),
        out_specs=(grid, grid, b3, b3, b3),
        check_vma=False,
    )
```

time: 522 us -> 254 us (0.49); the launches traced: 512 us -> 253 us
  starting transfers between devices: 191 us -> 38.1 us
  other arithmetic: 122 us -> 1.85 us
  Pallas kernels: 0 us -> 108 us
  waiting for transfers between devices: 138 us -> 73 us
  local copies, waits for them, and re-layouts: 56.6 us -> 10.4 us
  blocking collectives: 0 us -> 20.8 us
    ppermute x64 -> x16, starting transfers between devices: 174 us -> 30 us  [ring(): return lax.ppermute(x, axis, [(i, (i + step) % n) for i in range(n)])]
    pallas_call x0 -> x12, Pallas kernels: none -> 108 us  [the longest x2 37.8 us: local(): pl.pallas_call(round_kernel, out_shape=[half, half, u1s, sds(512, 128)],...]
    ppermute x64 -> x16, waiting for transfers between devices: 128 us -> 73 us  [ring(): return lax.ppermute(x, axis, [(i, (i + step) % n) for i in range(n)])]
    concatenate x16 -> x0, other arithmetic: 34.5 us -> none  [with_halo(): array = jnp.concatenate([before, array, after], axis=dim)]
    mul x18 -> x0, other arithmetic: 33.8 us -> none  [the longest x8 23.4 us: building_step(): disp = (disp + time_step * vel) * storey_mask]
    another operation x35 -> x0, other arithmetic: 24.3 us -> none  [the longest x24 19.6 us: divergence(): return jnp.stack([force_x, force_y, force_z])]
    slice x42 -> x0, local copies, waits for them, and re-layouts: 21.8 us -> none  [the longest x9 10.5 us: local(): ground[timestep]]
    all_to_all x0 -> x1, blocking collectives: none -> 20.8 us  [local(): returned = lax.all_to_all(answers, ('gx', 'gy'), 0, 0, tiled=True)]
  transfers between devices with their start and end apart: 66 -> 17, of which waited for: 48 -> 10; matrix products, arithmetic and copies ran while one was open for 3% -> 1% of each run, Pallas kernels for 0% -> 8%
where the time goes in v1:
time: 254 us; the launch traced here: 253 us
  Pallas kernels  108 us (43%)
  waiting for transfers between devices  73 us (29%)
  starting transfers between devices  38.1 us (15%)
  blocking collectives  20.8 us (8%)
  local copies, waits for them, and re-layouts  10.4 us (4%)
    ppermute x16, waiting for transfers between devices, ring(): return lax.ppermute(x, axis, [(i, (i + step) % n) for i in range(n)])  73 us
    pallas_call x2, Pallas kernels, local(): pl.pallas_call(round_kernel, out_shape=[half, half, u1s, sds(512, 128)],...  37.8 us
    ppermute x16, starting transfers between devices, ring(): return lax.ppermute(x, axis, [(i, (i + step) % n) for i in range(n)])  30 us
    pallas_call x1, Pallas kernels, local(): pl.pallas_call(first_round_kernel, out_shape=[half, half, u1s, sds(28, YR...  21 us
    all_to_all x1, blocking collectives, local(): returned = lax.all_to_all(answers, ('gx', 'gy'), 0, 0, tiled=True)  20.8 us
    pallas_call x1, Pallas kernels, local(): pl.pallas_call(last_kernel, out_shape=[sds(3, 16, 32, 128)] * 2 + [sds(51...  18.6 us
    unnamed x38, local copies, waits for them, and re-layouts  10.4 us
    pallas_call x1, Pallas kernels, local(): pl.pallas_call(building_kernel, out_shape=[sds(3, 64, 1024)] * 3, grid=(8...  10.2 us
  transfers between devices with their start and end apart: 17, of which 10 were waited for; matrix products, arithmetic and copies ran while one was open for 1% of the time, Pallas kernels for 8%

profile of v1, /device:TPU:1, one launch (start us, length us, event | category | flops | bytes accessed | tf_op | source)
XLA Modules:
  0.0 253.3 jit_solution(13127793405415301973)
XLA Ops:
  0.6 2.8 %pack_x.1 = (f32[52,32,128]{2,1,0:T(8,128)}, f32[52,32,128]{2,1,0:T(8,128)}) custom-call(f32[3,16,32,128]{3,2,1,0:T(8,128)} %u.5, f32[3,16,32,128]{3,2,1,0:T(8,128)} %p.5, f32[16,32,128]{2,1,0:T(8,128)} %la.5, f32[16,32,128]{2,1,0:T(8,128)} %mu.5, f32[16,32,128]{2,1,0:T(8,128)} %de.5), custom_call_target="tpu_custom_call" | custom-call | tf_op jit(solution)/shard_map/pack_x/pallas_call | solution.py:409
  3.4 2.5 %collective-permute-start = (f32[52,32,128]{2,1,0:T(8,128)}, f32[52,32,128]{2,1,0:T(8,128)S(1)}, u32[]{:S(2)}, u32[]{:S(2)}) collective-permute-start(f32[52,32,128]{2,1,0:T(8,128)} %get-tuple-element.39), channel_id=1, source_target_pairs={{0,8},{8,16},{16,24},{24,32},{32,40},{40,48},{48,56},{56,64},{64,7... | collective-permute-start | bytes 2555912 | tf_op jit(solution)/shard_map/ppermute | solution.py:31
  6.0 4.7 %collective-permute-start.1 = (f32[52,32,128]{2,1,0:T(8,128)}, f32[52,32,128]{2,1,0:T(8,128)S(1)}, u32[]{:S(2)}, u32[]{:S(2)}) collective-permute-start(f32[52,32,128]{2,1,0:T(8,128)} %get-tuple-element.40), channel_id=1, source_target_pairs={{0,120},{8,0},{16,8},{24,16},{32,24},{40,32},{48,40},{56,48},{64,5... | collective-permute-start | bytes 2555912 | tf_op jit(solution)/shard_map/ppermute | solution.py:31
  10.6 18.8 %collective-permute-done.north = f32[52,32,128]{2,1,0:T(8,128)S(1)} collective-permute-done((f32[52,32,128]{2,1,0:T(8,128)}, f32[52,32,128]{2,1,0:T(8,128)S(1)}, u32[]{:S(2)}, u32[]{:S(2)}) %collective-permute-start) | collective-permute-done | bytes 852000 | tf_op jit(solution)/shard_map/ppermute | solution.py:31
  31.3 4.2 %pack_y.1 = (f32[248,8,128]{2,1,0:T(8,128)}, f32[248,8,128]{2,1,0:T(8,128)}) custom-call(f32[3,16,32,128]{3,2,1,0:T(8,128)} %u.5, f32[3,16,32,128]{3,2,1,0:T(8,128)} %p.5, f32[16,32,128]{2,1,0:T(8,128)} %la.5, f32[16,32,128]{2,1,0:T(8,128)} %mu.5, f32[16,32,128]{2,1,0:T(8,128)} %de.5, f32[52,32,128]{2,1,0:T(8,128)} %copy-done, f32[52,32,128]{2,1,0:T(8,128)} %copy-done.1), custom_call_target="tpu_custom_call" | custom-call | tf_op jit(solution)/shard_map/pack_y/pallas_call | solution.py:432
  35.5 2.3 collective-permute-start.2
  38.5 11.0 %collective-permute-done.2.west = f32[248,8,128]{2,1,0:T(8,128)S(1)} collective-permute-done((f32[248,8,128]{2,1,0:T(8,128)}, f32[248,8,128]{2,1,0:T(8,128)S(1)}, u32[]{:S(2)}, u32[]{:S(2)}) %collective-permute-start.2) | collective-permute-done | bytes 1015840 | tf_op jit(solution)/shard_map/ppermute | solution.py:31
  49.5 2.4 collective-permute-done.3.east
  52.9 21.0 %wave_first.1 = (f32[3,8,32,128]{3,2,1,0:T(8,128)}, f32[3,8,32,128]{3,2,1,0:T(8,128)}, f32[3,24,56,128]{3,2,1,0:T(8,128)}, f32[28,56,128]{2,1,0:T(8,128)}, f32[2...) custom-call(f32[1,4]{1,0:T(1,128)} %add_convert_fusion.flags, f32[3,16,32,128]{3,2,1,0:T(8,128)} %u.5, ...), custom_call_target="tpu_custom_call" | custom-call | tf_op jit(solution)/shard_map/wave_first/pallas_call | solution.py:449
  74.0 4.8 %collective-permute-start.5 = (f32[3,8,32,128]{3,2,1,0:T(8,128)}, f32[3,8,32,128]{3,2,1,0:T(8,128)S(1)}, u32[]{:S(2)}, u32[]{:S(2)}) collective-permute-start(f32[3,8,32,128]{3,2,1,0:T(8,128)} %get-tuple-element.43.top), channel_id=1, source_target_pairs={{0,120},{8,0},{16,8},{24,16},{32,24},{40,32},{48,40},{56,48},{64,5... | collective-permute-start | bytes 1179656 | tf_op jit(solution)/shard_map/ppermute | solution.py:31
  78.8 8.3 %collective-permute-done.4.north = f32[3,8,32,128]{3,2,1,0:T(8,128)S(1)} collective-permute-done((f32[3,8,32,128]{3,2,1,0:T(8,128)}, f32[3,8,32,128]{3,2,1,0:T(8,128)S(1)}, u32[]{:S(2)}, u32[]{:S(2)}) %collective-permute-start.4) | collective-permute-done | bytes 393248 | tf_op jit(solution)/shard_map/ppermute | solution.py:31
  88.5 2.3 pack_round.3
  90.8 3.1 %collective-permute-start.6 = (f32[3,32,8,128]{3,2,1,0:T(8,128)}, f32[3,32,8,128]{3,2,1,0:T(8,128)S(1)}, u32[]{:S(2)}, u32[]{:S(2)}) collective-permute-start(f32[3,32,8,128]{3,2,1,0:T(8,128)} %get-tuple-element.45), channel_id=1, source_target_pairs={{0,1},{1,2},{2,3},{3,4},{4,5},{5,6},{6,7},{7,0},{8,9},{9,10},{10,1... | collective-permute-start | bytes 1179656 | tf_op jit(solution)/shard_map/ppermute | solution.py:31
  93.9 5.0 %collective-permute-done.6.west = f32[3,32,8,128]{3,2,1,0:T(8,128)S(1)} collective-permute-done((f32[3,32,8,128]{3,2,1,0:T(8,128)}, f32[3,32,8,128]{3,2,1,0:T(8,128)S(1)}, u32[]{:S(2)}, u32[]{:S(2)}) %collective-permute-start.6) | collective-permute-done | bytes 393248 | tf_op jit(solution)/shard_map/ppermute | solution.py:31
  99.0 2.4 collective-permute-done.7.east
  102.1 18.9 %wave_round.2 = (f32[3,8,32,128]{3,2,1,0:T(8,128)}, f32[3,8,32,128]{3,2,1,0:T(8,128)}, f32[3,24,56,128]{3,2,1,0:T(8,128)}, f32[512,128]{1,0:T(8,128)}) custom-call(f32[1,4]{1,0:T(1,128)} %add_convert_fusion.flags, f32[3,8,32,128]{3,2,1,0:T(8,128)} %get-tuple-element.43.top, f32[3,8,32,128]{3,2,1,0:T(8,128)} %get-tuple-element.44.bot, ...), custom_call_target="tpu_custom_call" | custom-call | tf_op jit(solution)/shard_map/wave_round/pallas_call | solution.py:474
  121.0 4.8 %collective-permute-start.9 = (f32[3,8,32,128]{3,2,1,0:T(8,128)}, f32[3,8,32,128]{3,2,1,0:T(8,128)S(1)}, u32[]{:S(2)}, u32[]{:S(2)}) collective-permute-start(f32[3,8,32,128]{3,2,1,0:T(8,128)} %get-tuple-element.51.top), channel_id=1, source_target_pairs={{0,120},{8,0},{16,8},{24,16},{32,24},{40,32},{48,40},{56,48},{64,5... | collective-permute-start | bytes 1179656 | tf_op jit(solution)/shard_map/ppermute | solution.py:31
  125.8 9.2 %collective-permute-done.8.north = f32[3,8,32,128]{3,2,1,0:T(8,128)S(1)} collective-permute-done((f32[3,8,32,128]{3,2,1,0:T(8,128)}, f32[3,8,32,128]{3,2,1,0:T(8,128)S(1)}, u32[]{:S(2)}, u32[]{:S(2)}) %collective-permute-start.8) | collective-permute-done | bytes 393248 | tf_op jit(solution)/shard_map/ppermute | solution.py:31
  136.5 2.3 pack_round.4
  140.2 5.0 %collective-permute-done.10.west = f32[3,32,8,128]{3,2,1,0:T(8,128)S(1)} collective-permute-done((f32[3,32,8,128]{3,2,1,0:T(8,128)}, f32[3,32,8,128]{3,2,1,0:T(8,128)S(1)}, u32[]{:S(2)}, u32[]{:S(2)}) %collective-permute-start.10) | collective-permute-done | bytes 393248 | tf_op jit(solution)/shard_map/ppermute | solution.py:31
  145.2 2.7 %collective-permute-done.11.east = f32[3,32,8,128]{3,2,1,0:T(8,128)S(1)} collective-permute-done((f32[3,32,8,128]{3,2,1,0:T(8,128)}, f32[3,32,8,128]{3,2,1,0:T(8,128)S(1)}, u32[]{:S(2)}, u32[]{:S(2)}) %collective-permute-start.11) | collective-permute-done | bytes 393248 | tf_op jit(solution)/shard_map/ppermute | solution.py:31
  148.7 19.0 %wave_round.3 = (f32[3,8,32,128]{3,2,1,0:T(8,128)}, f32[3,8,32,128]{3,2,1,0:T(8,128)}, f32[3,24,56,128]{3,2,1,0:T(8,128)}, f32[512,128]{1,0:T(8,128)}) custom-call(f32[1,4]{1,0:T(1,128)} %add_convert_fusion.flags, f32[3,8,32,128]{3,2,1,0:T(8,128)} %get-tuple-element.51.top, f32[3,8,32,128]{3,2,1,0:T(8,128)} %get-tuple-element.52.bot, ...), custom_call_target="tpu_custom_call" | custom-call | tf_op jit(solution)/shard_map/wave_round/pallas_call | solution.py:474
  167.6 4.8 %collective-permute-start.13 = (f32[3,8,32,128]{3,2,1,0:T(8,128)}, f32[3,8,32,128]{3,2,1,0:T(8,128)S(1)}, u32[]{:S(2)}, u32[]{:S(2)}) collective-permute-start(f32[3,8,32,128]{3,2,1,0:T(8,128)} %get-tuple-element.56.top), channel_id=1, source_target_pairs={{0,120},{8,0},{16,8},{24,16},{32,24},{40,32},{48,40},{56,48},{64,5... | collective-permute-start | bytes 1179656 | tf_op jit(solution)/shard_map/ppermute | solution.py:31
  173.0 8.2 %collective-permute-done.12.north = f32[3,8,32,128]{3,2,1,0:T(8,128)S(1)} collective-permute-done((f32[3,8,32,128]{3,2,1,0:T(8,128)}, f32[3,8,32,128]{3,2,1,0:T(8,128)S(1)}, u32[]{:S(2)}, u32[]{:S(2)}) %collective-permute-start.12) | collective-permute-done | bytes 393248 | tf_op jit(solution)/shard_map/ppermute | solution.py:31
  182.7 2.3 pack_round.5
  184.9 1.6 collective-permute-start.14
  187.1 2.5 requests.1
  189.6 8.1 %all-to-all-start = ((f32[128,4,128]{2,1,0:T(4,128)}), f32[128,4,128]{2,1,0:T(4,128)S(1)}, u32[]{:S(2)}, u32[]{:S(2)}) async-start(f32[128,4,128]{2,1,0:T(4,128)} %get-tuple-element.63), calls=%async_computation | async-start | bytes 524288 | tf_op jit(solution)/shard_map/all_to_all | solution.py:430
  198.6 18.6 %wave_last.1 = (f32[3,16,32,128]{3,2,1,0:T(8,128)}, f32[3,16,32,128]{3,2,1,0:T(8,128)}, f32[512,128]{1,0:T(8,128)}) custom-call(f32[1,4]{1,0:T(1,128)} %add_convert_fusion.flags, f32[3,8,32,128]{3,2,1,0:T(8,128)} %get-tuple-element.56.top, f32[3,8,32,128]{3,2,1,0:T(8,128)} %get-tuple-element.57.bot, f32[3,8,32,128]{3,2,1,0:T(8,128)} %copy-done.2, ...), custom_call_target="tpu_custom_call" | custom-call | tf_op jit(solution)/shard_map/wave_last/pallas_call | solution.py:484
  217.9 4.4 %answers.1 = f32[128,4,128]{2,1,0:T(4,128)} custom-call(f32[128,4,128]{2,1,0:T(4,128)} %copy-done.8, f32[512,128]{1,0:T(8,128)} %get-tuple-element.64.h0, f32[512,128]{1,0:T(8,128)} %get-tuple-element.65.h1, f32[512,128]{1,0:T(8,128)} %get-tuple-element.66.h2, f32[512,128]{1,0:T(8,128)} %get-tuple-element.67.h3), custom_call_target="tpu_custom_call" | custom-call | tf_op jit(solution)/shard_map/answers/pallas_call | solution.py:495
  222.3 20.8 %all_to_all.10.ret = f32[128,4,128]{2,1,0:T(4,128)} all-to-all(f32[128,4,128]{2,1,0:T(4,128)} %answers.1), channel_id=1, replica_groups=mesh['gx'=16,'gy'=8] {'gx','gy'}, dimensions={0} | all-to-all | bytes 524288 | tf_op jit(solution)/shard_map/all_to_all | solution.py:504
  243.1 10.2 %buildings.1 = (f32[3,64,1024]{2,1,0:T(8,128)}, f32[3,64,1024]{2,1,0:T(8,128)}, f32[3,64,1024]{2,1,0:T(8,128)}) custom-call(f32[128,4,128]{2,1,0:T(4,128)} %all_to_all.10.ret, f32[8,1,128]{2,1,0:T(1,128)} %bitcast.12, f32[8,1,128]{2,1,0:T(1,128)} %bitcast.13, f32[3,64,1024]{2,1,0:T(8,128)} %d_in.1, f32[3,64,1024]{2,1,0:T(8,128)} %v_in.1, f32[3,64,1024]{2,1,0:T(8,128)} %hf.1, ...), custom_call_target="tpu_custom_call" | custom-call | tf_op jit(solution)/shard_map/buildings/pallas_call | solution.py:509
  (56 shorter events, 13.8 us)
Async XLA Ops:
  3.4 26.0 %collective-permute-start = (f32[52,32,128]{2,1,0:T(8,128)}, f32[52,32,128]{2,1,0:T(8,128)S(1)}, u32[]{:S(2)}, u32[]{:S(2)}) collective-permute-start(f32[52,32,128]{2,1,0:T(8,128)} %get-tuple-element.39), channel_id=1, source_target_pairs={{0,8},{8,16},{16,24},{24,32},{32,40},{40,48},{48,56},{56,64},{64,7... | collective-permute-start | bytes 2555912 | tf_op jit(solution)/shard_map/ppermute | solution.py:31
  6.0 23.5 %collective-permute-start.1 = (f32[52,32,128]{2,1,0:T(8,128)}, f32[52,32,128]{2,1,0:T(8,128)S(1)}, u32[]{:S(2)}, u32[]{:S(2)}) collective-permute-start(f32[52,32,128]{2,1,0:T(8,128)} %get-tuple-element.40), channel_id=1, source_target_pairs={{0,120},{8,0},{16,8},{24,16},{32,24},{40,32},{48,40},{56,48},{64,5... | collective-permute-start | bytes 2555912 | tf_op jit(solution)/shard_map/ppermute | solution.py:31
  29.4 0.9 copy-start
  30.4 0.9 copy-start.1
  35.5 14.0 %collective-permute-start.2 = (f32[248,8,128]{2,1,0:T(8,128)}, f32[248,8,128]{2,1,0:T(8,128)S(1)}, u32[]{:S(2)}, u32[]{:S(2)}) collective-permute-start(f32[248,8,128]{2,1,0:T(8,128)} %get-tuple-element.41), channel_id=1, source_target_pairs={{0,1},{1,2},{2,3},{3,4},{4,5},{5,6},{6,7},{7,0},{8,9},{9,10},{10,1... | collective-permute-start | bytes 3047432 | tf_op jit(solution)/shard_map/ppermute | solution.py:31
  37.8 14.1 %collective-permute-start.3 = (f32[248,8,128]{2,1,0:T(8,128)}, f32[248,8,128]{2,1,0:T(8,128)S(1)}, u32[]{:S(2)}, u32[]{:S(2)}) collective-permute-start(f32[248,8,128]{2,1,0:T(8,128)} %get-tuple-element.42), channel_id=1, source_target_pairs={{0,7},{1,0},{2,1},{3,2},{4,3},{5,4},{6,5},{7,6},{8,15},{9,8},{10,9... | collective-permute-start | bytes 3047432 | tf_op jit(solution)/shard_map/ppermute | solution.py:31
  49.5 2.4 copy-start.9
  51.9 1.0 copy-start.10
  74.0 13.1 %collective-permute-start.4 = (f32[3,8,32,128]{3,2,1,0:T(8,128)}, f32[3,8,32,128]{3,2,1,0:T(8,128)S(1)}, u32[]{:S(2)}, u32[]{:S(2)}) collective-permute-start(f32[3,8,32,128]{3,2,1,0:T(8,128)} %get-tuple-element.44.bot), channel_id=1, source_target_pairs={{0,8},{8,16},{16,24},{24,32},{32,40},{40,48},{48,56},{56,64},{64,7... | collective-permute-start | bytes 1179656 | tf_op jit(solution)/shard_map/ppermute | solution.py:31
  74.0 13.1 %collective-permute-start.5 = (f32[3,8,32,128]{3,2,1,0:T(8,128)}, f32[3,8,32,128]{3,2,1,0:T(8,128)S(1)}, u32[]{:S(2)}, u32[]{:S(2)}) collective-permute-start(f32[3,8,32,128]{3,2,1,0:T(8,128)} %get-tuple-element.43.top), channel_id=1, source_target_pairs={{0,120},{8,0},{16,8},{24,16},{32,24},{40,32},{48,40},{56,48},{64,5... | collective-permute-start | bytes 1179656 | tf_op jit(solution)/shard_map/ppermute | solution.py:31
  87.0 0.7 copy-start.4
  90.8 8.1 %collective-permute-start.6 = (f32[3,32,8,128]{3,2,1,0:T(8,128)}, f32[3,32,8,128]{3,2,1,0:T(8,128)S(1)}, u32[]{:S(2)}, u32[]{:S(2)}) collective-permute-start(f32[3,32,8,128]{3,2,1,0:T(8,128)} %get-tuple-element.45), channel_id=1, source_target_pairs={{0,1},{1,2},{2,3},{3,4},{4,5},{5,6},{6,7},{7,0},{8,9},{9,10},{10,1... | collective-permute-start | bytes 1179656 | tf_op jit(solution)/shard_map/ppermute | solution.py:31
  93.9 7.4 %collective-permute-start.7 = (f32[3,32,8,128]{3,2,1,0:T(8,128)}, f32[3,32,8,128]{3,2,1,0:T(8,128)S(1)}, u32[]{:S(2)}, u32[]{:S(2)}) collective-permute-start(f32[3,32,8,128]{3,2,1,0:T(8,128)} %get-tuple-element.46), channel_id=1, source_target_pairs={{0,7},{1,0},{2,1},{3,2},{4,3},{5,4},{6,5},{7,6},{8,15},{9,8},{10,9... | collective-permute-start | bytes 1179656 | tf_op jit(solution)/shard_map/ppermute | solution.py:31
  99.0 2.4 copy-start.13
  101.3 0.8 copy-start.15
  121.0 14.0 %collective-permute-start.8 = (f32[3,8,32,128]{3,2,1,0:T(8,128)}, f32[3,8,32,128]{3,2,1,0:T(8,128)S(1)}, u32[]{:S(2)}, u32[]{:S(2)}) collective-permute-start(f32[3,8,32,128]{3,2,1,0:T(8,128)} %get-tuple-element.52.bot), channel_id=1, source_target_pairs={{0,8},{8,16},{16,24},{24,32},{32,40},{40,48},{48,56},{56,64},{64,7... | collective-permute-start | bytes 1179656 | tf_op jit(solution)/shard_map/ppermute | solution.py:31
  121.0 14.0 %collective-permute-start.9 = (f32[3,8,32,128]{3,2,1,0:T(8,128)}, f32[3,8,32,128]{3,2,1,0:T(8,128)S(1)}, u32[]{:S(2)}, u32[]{:S(2)}) collective-permute-start(f32[3,8,32,128]{3,2,1,0:T(8,128)} %get-tuple-element.51.top), channel_id=1, source_target_pairs={{0,120},{8,0},{16,8},{24,16},{32,24},{40,32},{48,40},{56,48},{64,5... | collective-permute-start | bytes 1179656 | tf_op jit(solution)/shard_map/ppermute | solution.py:31
  135.0 0.7 copy-start.5
  138.7 6.5 %collective-permute-start.10 = (f32[3,32,8,128]{3,2,1,0:T(8,128)}, f32[3,32,8,128]{3,2,1,0:T(8,128)S(1)}, u32[]{:S(2)}, u32[]{:S(2)}) collective-permute-start(f32[3,32,8,128]{3,2,1,0:T(8,128)} %get-tuple-element.53), channel_id=1, source_target_pairs={{0,1},{1,2},{2,3},{3,4},{4,5},{5,6},{6,7},{7,0},{8,9},{9,10},{10,1... | collective-permute-start | bytes 1179656 | tf_op jit(solution)/shard_map/ppermute | solution.py:31
  140.2 7.7 %collective-permute-start.11 = (f32[3,32,8,128]{3,2,1,0:T(8,128)}, f32[3,32,8,128]{3,2,1,0:T(8,128)S(1)}, u32[]{:S(2)}, u32[]{:S(2)}) collective-permute-start(f32[3,32,8,128]{3,2,1,0:T(8,128)} %get-tuple-element.54), channel_id=1, source_target_pairs={{0,7},{1,0},{2,1},{3,2},{4,3},{5,4},{6,5},{7,6},{8,15},{9,8},{10,9... | collective-permute-start | bytes 1179656 | tf_op jit(solution)/shard_map/ppermute | solution.py:31
  145.2 2.7 %copy-start.14 = (f32[3,32,8,128]{3,2,1,0:T(8,128)}, f32[3,32,8,128]{3,2,1,0:T(8,128)S(1)}, u32[]{:S(2)}) copy-start(f32[3,32,8,128]{3,2,1,0:T(8,128)S(1)} %collective-permute-done.10.west) | copy-start | bytes 1179652
  147.9 0.7 copy-start.16
  148.7 23.8 %copy-start.17 = (s32[1024,1]{0,1:T(1,128)S(1)}, s32[1024,1]{0,1:T(1,128)}, u32[]{:S(2)}) copy-start(s32[1024,1]{0,1:T(1,128)} %param.28) | copy-start | bytes 12292
  148.7 37.9 %copy-start.18 = (s32[1024]{0:T(1024)S(1)}, s32[1024]{0:T(1024)}, u32[]{:S(2)}) copy-start(s32[1024]{0:T(1024)} %param.29) | copy-start | bytes 12292
  167.6 13.5 %collective-permute-start.12 = (f32[3,8,32,128]{3,2,1,0:T(8,128)}, f32[3,8,32,128]{3,2,1,0:T(8,128)S(1)}, u32[]{:S(2)}, u32[]{:S(2)}) collective-permute-start(f32[3,8,32,128]{3,2,1,0:T(8,128)} %get-tuple-element.57.bot), channel_id=1, source_target_pairs={{0,8},{8,16},{16,24},{24,32},{32,40},{40,48},{48,56},{56,64},{64,7... | collective-permute-start | bytes 1179656 | tf_op jit(solution)/shard_map/ppermute | solution.py:31
  167.6 13.5 %collective-permute-start.13 = (f32[3,8,32,128]{3,2,1,0:T(8,128)}, f32[3,8,32,128]{3,2,1,0:T(8,128)S(1)}, u32[]{:S(2)}, u32[]{:S(2)}) collective-permute-start(f32[3,8,32,128]{3,2,1,0:T(8,128)} %get-tuple-element.56.top), channel_id=1, source_target_pairs={{0,120},{8,0},{16,8},{24,16},{32,24},{40,32},{48,40},{56,48},{64,5... | collective-permute-start | bytes 1179656 | tf_op jit(solution)/shard_map/ppermute | solution.py:31
  181.2 0.7 copy-start.2
  184.9 12.8 %collective-permute-start.14 = (f32[3,32,8,128]{3,2,1,0:T(8,128)}, f32[3,32,8,128]{3,2,1,0:T(8,128)S(1)}, u32[]{:S(2)}, u32[]{:S(2)}) collective-permute-start(f32[3,32,8,128]{3,2,1,0:T(8,128)} %get-tuple-element.58), channel_id=1, source_target_pairs={{0,1},{1,2},{2,3},{3,4},{4,5},{5,6},{6,7},{7,0},{8,9},{9,10},{10,1... | collective-permute-start | bytes 1179656 | tf_op jit(solution)/shard_map/ppermute | solution.py:31
  186.5 11.2 %collective-permute-start.15 = (f32[3,32,8,128]{3,2,1,0:T(8,128)}, f32[3,32,8,128]{3,2,1,0:T(8,128)S(1)}, u32[]{:S(2)}, u32[]{:S(2)}) collective-permute-start(f32[3,32,8,128]{3,2,1,0:T(8,128)} %get-tuple-element.59), channel_id=1, source_target_pairs={{0,7},{1,0},{2,1},{3,2},{4,3},{5,4},{6,5},{7,6},{8,15},{9,8},{10,9... | collective-permute-start | bytes 1179656 | tf_op jit(solution)/shard_map/ppermute | solution.py:31
  189.6 27.6 %all-to-all-start = ((f32[128,4,128]{2,1,0:T(4,128)}), f32[128,4,128]{2,1,0:T(4,128)S(1)}, u32[]{:S(2)}, u32[]{:S(2)}) async-start(f32[128,4,128]{2,1,0:T(4,128)} %get-tuple-element.63), calls=%async_computation | async-start | bytes 524288 | tf_op jit(solution)/shard_map/all_to_all | solution.py:430
  197.7 0.8 copy-start.11
  197.7 0.9 copy-start.12
  (4 other events, 2.9 us)

commit v2 on v1

v2 whole, which is shorter than its diff:
```python
import jax
import jax.numpy as jnp
from jax import lax
from jax.experimental import pallas as pl
from jax.experimental.pallas import tpu as pltpu
from jax.sharding import PartitionSpec as P

STEPS = 8
DT = 0.35
POST = 0.1
DAMP = 0.05
F32 = jnp.float32
BF16 = jnp.bfloat16
VM = pl.BlockSpec(memory_space=pltpu.VMEM)
SM = pl.BlockSpec(memory_space=pltpu.SMEM)
HB = pl.BlockSpec(memory_space=pl.ANY)
CP = pltpu.CompilerParams(vmem_limit_bytes=24 << 20)
UNROLL = 4
YR = 56

XPARTS = ((0, 3, 8), (1, 3, 4), (2, 1, 6), (3, 1, 6), (4, 1, 4))
XPLANES = sum(c * w for _, c, w in XPARTS)
YBLOCKS = sum(c * (16 + 2 * w) for _, c, w in XPARTS)


def sds(*shape):
    return jax.ShapeDtypeStruct(shape, F32)


def ring(x, axis, step):
    n = lax.axis_size(axis)
    return lax.ppermute(x, axis, [(i, (i + step) % n) for i in range(n)])


def split3(x):
    hi = x.astype(BF16)
    rest = x - hi.astype(F32)
    mid = rest.astype(BF16)
    low = (rest - mid.astype(F32)).astype(BF16)
    return hi, mid, low


def at_comp(ref, comps, c, rows, cols):
    return ref.at[c, rows, cols] if comps == 3 else ref.at[rows, cols]


def pack_x_kernel(u, p, la, mu, de, up, down, sem):
    args = (u, p, la, mu, de)
    copies = []
    off = 0
    for a, comps, w in XPARTS:
        for c in range(comps):
            full = pl.ds(0, 32)
            src_up = at_comp(args[a], comps, c, pl.ds(16 - w, w), full)
            src_dn = at_comp(args[a], comps, c, pl.ds(0, w), full)
            n = len(copies)
            copies.append(pltpu.make_async_copy(src_up, up.at[pl.ds(off, w)], sem.at[n]))
            copies.append(pltpu.make_async_copy(src_dn, down.at[pl.ds(off, w)], sem.at[n + 1]))
            off += w
    for cp in copies:
        cp.start()
    for cp in copies:
        cp.wait()


def pack_y_kernel(u, p, la, mu, de, north, south, up, down, sem):
    args = (u, p, la, mu, de)
    copies = []
    off = 0
    src = 0
    for a, comps, w in XPARTS:
        for c in range(comps):
            for dst, col in ((up, 24), (down, 0)):
                n = len(copies)
                s = at_comp(args[a], comps, c, pl.ds(0, 16), pl.ds(col, 8))
                cp = pltpu.make_async_copy(s, dst.at[pl.ds(off + w, 16)], sem.at[n])
                cp.start()
                copies.append(cp)
                dst[off : off + w] = north[src : src + w, col : col + 8]
                dst[off + w + 16 : off + 2 * w + 16] = south[src : src + w, col : col + 8]
            off += 16 + 2 * w
            src += w
    for cp in copies:
        cp.wait()


def pack_round_kernel(top, bot, north, south, up, down):
    for dst, col in ((up, 24), (down, 0)):
        dst[:, 0:8] = north[:, :, col : col + 8]
        dst[:, 8:16] = top[:, :, col : col + 8]
        dst[:, 16:24] = bot[:, :, col : col + 8]
        dst[:, 24:32] = south[:, :, col : col + 8]


def z_matrix():
    i = lax.broadcasted_iota(jnp.int32, (256, 128), 0)
    j = lax.broadcasted_iota(jnp.int32, (256, 128), 1)
    d = jnp.where(i < 128, i, i - 128) - j
    one = jnp.ones((256, 128), F32)
    near = jnp.where(d == 1, 8.0 * one, 0.0) - jnp.where(d == -1, 8.0 * one, 0.0)
    far = jnp.where(d == 2, one, 0.0) - jnp.where(d == -2, one, 0.0)
    return (near - far).astype(BF16)


def pieces2(f):
    hi = f.astype(BF16)
    lo = (f - hi.astype(F32)).astype(BF16)
    return jnp.concatenate([hi, lo], axis=1)


def dz_all(fields, mz):
    n = fields[0].shape[0]
    lhs = jnp.concatenate([pieces2(f) for f in fields], axis=0)
    out = jnp.dot(lhs, mz, preferred_element_type=F32)
    return [out[n * k : n * k + n] for k in range(len(fields))]


def dx(rows, k):
    return 8.0 * (rows[k + 3] - rows[k + 1]) - (rows[k + 4] - rows[k])


def dy(ref, c, x, y, n):
    near = ref[c, x, pl.ds(y + 1, n)] - ref[c, x, pl.ds(y - 1, n)]
    far = ref[c, x, pl.ds(y + 2, n)] - ref[c, x, pl.ds(y - 2, n)]
    return 8.0 * near - far


def stress_pass(u, ux, s, lam, mu, mz, x0, nx, y, n):
    ys = pl.ds(y, n)

    def body(i, carry):
        g0 = i * UNROLL + x0
        rows = [[u[c, g0 - ux - 2 + j, ys] for j in range(UNROLL + 4)] for c in range(3)]
        zs = dz_all([rows[c][k + 2] for k in range(UNROLL) for c in range(3)], mz[...])
        for k in range(UNROLL):
            gx = g0 + k
            x = gx - ux
            z0, z1, z2 = zs[3 * k : 3 * k + 3]
            m = mu[gx - 2, ys]
            g00 = dx(rows[0], k)
            g11 = dy(u, 1, x, y, n)
            lt = lam[gx - 2, ys] * (g00 + g11 + z2)
            m2 = m + m
            s[0, gx, ys] = lt + m2 * g00
            s[1, gx, ys] = lt + m2 * g11
            s[2, gx, ys] = lt + m2 * z2
            s[3, gx, ys] = m * (dy(u, 0, x, y, n) + dx(rows[1], k))
            s[4, gx, ys] = m * (z0 + dx(rows[2], k))
            s[5, gx, ys] = m * (z1 + dy(u, 2, x, y, n))
        return carry

    lax.fori_loop(0, nx // UNROLL, body, 0)


def forces(s, q, mz, g0, y, n):
    ys = pl.ds(y, n)
    rows = [[s[c, g0 - 2 + j, ys] for j in range(UNROLL + 4)] for c in (0, 3, 4)]
    fields = []
    for k in range(UNROLL):
        fields += [rows[2][k + 2], s[5, g0 + k, ys], s[2, g0 + k, ys]]
    zs = dz_all(fields, mz[...])
    out = []
    for k in range(UNROLL):
        x = g0 + k
        z0, z1, z2 = zs[3 * k : 3 * k + 3]
        qk = q[x - 4, ys]
        out.append(
            (
                qk * (dx(rows[0], k) + dy(s, 3, x, y, n) + z0),
                qk * (dx(rows[1], k) + dy(s, 1, x, y, n) + z1),
                qk * (dx(rows[2], k) + dy(s, 5, x, y, n) + z2),
            )
        )
    return out


def surface(fs, slot, old):
    lane = lax.broadcasted_iota(jnp.int32, fs[0].shape, 1)
    for c, f in enumerate(fs):
        v = pltpu.roll(f, slot + c, 1) if slot + c else f
        old = jnp.where(lane == slot + c, v, old)
    return old


def wave_two_steps(ue, prev, lam, mu, q, s, hs, mz, u1, hist, store):
    mz[...] = z_matrix()
    stress_pass(ue, 0, s, lam, mu, mz, 2, 28, 2, 48)

    def first(start, count, stride, seen):
        def body(j, carry):
            i0 = start + j * stride
            for k, fs in enumerate(forces(s, q, mz, i0 + 4, 4, 48)):
                i = i0 + k
                if seen:
                    hs[i - 4] = surface(fs, 0, jnp.zeros((48, 128), F32))
                for c in range(3):
                    now = ue[c, i + 4, 4:52]
                    u1[c, i, 4:52] = (now - prev[c, i, 4:52]) + (now + fs[c])
            return carry

        lax.fori_loop(0, count, body, 0)

    first(0, 2, 20, False)
    first(4, 16 // UNROLL, UNROLL, True)
    if UNROLL == 2:
        first(2, 2, 20, False)
    stress_pass(u1, 4, s, lam, mu, mz, 6, 20, 6, 48)

    def second(part):
        def body(j0, carry):
            i0 = j0 * UNROLL + 8 * part
            for k, fs in enumerate(forces(s, q, mz, i0 + 8, 8, 32)):
                i = i0 + k
                r = pl.multiple_of(i * 32, 32)
                hist[pl.ds(r, 32)] = surface(fs, 3, hs[i, 4:36])
                for c in range(3):
                    now = u1[c, i + 4, 8:40]
                    store(part, c, j0 * UNROLL + k, (now - ue[c, i + 8, 8:40]) + (now + fs[c]))
            return carry

        lax.fori_loop(0, 8 // UNROLL, body, 0)

    second(0)
    second(1)


def fill(ext, c, w, lead, parts, flags):
    center, north, south, west, east = parts
    fn, fs, fw, fe = flags
    ref = ext if lead is None else ext.at[lead]

    def row(i, f):
        ref[i, 0:8] = west(i) * (f * fw)
        ref[i, 40:48] = east(i) * (f * fe)

    for i in range(w):
        row(i, fn)
        ref[i, 8:40] = north(i) * fn
        row(16 + w + i, fs)
        ref[16 + w + i, 8:40] = south(i) * fs

    def mid(i, carry):
        row(w + i, 1.0)
        ref[w + i, 8:40] = center(i)
        return carry

    lax.fori_loop(0, 16, mid, 0)


def first_round_kernel(flags, u, p, la, mu, de, north, south, west, east, top, bot, u1, lam, muo, q, hist, ue, pe, s, hs, mz):
    fl = [flags[0, k] for k in range(4)]
    args = (u, p, la, mu, de)
    exts = (ue, pe, lam, muo, q)
    src = 0
    off = 0
    for a, comps, w in XPARTS:
        for c in range(comps):
            arg = args[a]
            parts = (
                (lambda i, arg=arg, c=c: arg[c, i]) if comps == 3 else (lambda i, arg=arg: arg[i]),
                lambda i, src=src: north[src + i],
                lambda i, src=src: south[src + i],
                lambda i, off=off: west[off + i],
                lambda i, off=off: east[off + i],
            )
            fill(exts[a], c, w, c if comps == 3 else None, parts, fl)
            src += w
            off += 16 + 2 * w

    def scale(i, carry):
        lam[i] = lam[i] * (1.0 / 12.0)
        muo[i] = muo[i] * (1.0 / 12.0)
        return carry

    lax.fori_loop(0, 28, scale, 0)

    def invert(i, carry):
        d = q[i]
        q[i] = jnp.where(d > 0.0, (DT * DT / 12.0) / jnp.where(d > 0.0, d, 1.0), 0.0)
        return carry

    lax.fori_loop(0, 24, invert, 0)
    finish_rows(ue, pe, lam, muo, q, s, hs, mz, u1, hist, top, bot)


def finish_rows(ue, pe, lam, mu, q, s, hs, mz, u1, hist, top, bot):
    def store(part, c, j, v):
        (top, bot)[part][c, j] = v

    wave_two_steps(ue, pe, lam, mu, q, s, hs, mz, u1, hist, store)


def fill_round(flags, top, bot, north, south, west, east, ue):
    fn, fs, fw, fe = [flags[0, k] for k in range(4)]
    for c in range(3):

        def rows(i, carry, c=c):
            ue[c, i, 0:8] = west[c, i] * (fn * fw)
            ue[c, i, 8:40] = north[c, i] * fn
            ue[c, i, 40:48] = east[c, i] * (fn * fe)
            ue[c, 8 + i, 0:8] = west[c, 8 + i] * fw
            ue[c, 8 + i, 8:40] = top[c, i]
            ue[c, 8 + i, 40:48] = east[c, 8 + i] * fe
            ue[c, 16 + i, 0:8] = west[c, 16 + i] * fw
            ue[c, 16 + i, 8:40] = bot[c, i]
            ue[c, 16 + i, 40:48] = east[c, 16 + i] * fe
            ue[c, 24 + i, 0:8] = west[c, 24 + i] * (fs * fw)
            ue[c, 24 + i, 8:40] = south[c, i] * fs
            ue[c, 24 + i, 40:48] = east[c, 24 + i] * (fs * fe)
            return carry

        lax.fori_loop(0, 8, rows, 0)


def round_kernel(flags, top, bot, north, south, west, east, prev, lam, mu, q, top2, bot2, u1, hist, ue, s, hs, mz):
    fill_round(flags, top, bot, north, south, west, east, ue)
    finish_rows(ue, prev, lam, mu, q, s, hs, mz, u1, hist, top2, bot2)


def last_kernel(flags, top, bot, north, south, west, east, prev, lam, mu, q, now, before, hist, ue, s, hs, mz, u1):
    fill_round(flags, top, bot, north, south, west, east, ue)

    def store(part, c, j, v):
        i = j + 8 * part
        now[c, i] = v
        before[c, i] = u1[c, i + 4, 8:40]

    wave_two_steps(ue, prev, lam, mu, q, s, hs, mz, u1, hist, store)


def request_kernel(tile, cell, req, key, kmod, a_ref, bhi, blo):
    ones = jnp.ones((128, 128), F32)
    sub = lax.broadcasted_iota(jnp.int32, (128, 128), 0)
    lan = lax.broadcasted_iota(jnp.int32, (128, 128), 1)
    cols = [(ones * tile[i : i + 1, :]).T for i in range(8)]
    row512 = lax.broadcasted_iota(jnp.int32, (512, 128), 0).astype(F32)
    subf = sub.astype(F32)
    for j in range(8):
        mine = tile[j : j + 1, :]
        acc = jnp.where((cols[j] == mine) & (sub < lan), 1.0, 0.0)
        for i in range(j):
            acc = acc + jnp.where(cols[i] == mine, 1.0, 0.0)
        rank = jnp.sum(acc, axis=0, keepdims=True)
        quarter = jnp.floor(rank * 0.25)
        kj = mine * 4.0 + quarter
        mj = rank - 4.0 * quarter
        key[j : j + 1, :] = kj
        kmod[j : j + 1, :] = mj
        lanes = pl.ds(128 * j, 128)
        a_ref[:, lanes] = jnp.where(row512 == kj, 1.0, 0.0).astype(BF16)
        cj = cell[j : j + 1, :]
        hi = jnp.floor(cj * (1.0 / 32.0))
        hit = subf == mj
        bhi[:, lanes] = jnp.where(hit, hi, 0.0).astype(BF16)
        blo[:, lanes] = jnp.where(hit, cj - 32.0 * hi, 0.0).astype(BF16)
    dims = (((1,), (1,)), ((), ()))
    top = lax.dot_general(a_ref[...], bhi[...], dims, preferred_element_type=F32)
    low = lax.dot_general(a_ref[...], blo[...], dims, preferred_element_type=F32)
    req[...] = (32.0 * top + low).reshape(128, 4, 128)


def hot_kernel(inc, hot):
    cells = inc[...].reshape(512, 128)
    lane = lax.broadcasted_iota(jnp.int32, (512, 512), 1).astype(F32)
    for k in range(4):
        hot[k] = jnp.where(lane == cells[:, k : k + 1], 1.0, 0.0).astype(BF16)


def pick(h, hot):
    acc = jnp.zeros((512, 128), F32)
    for k in range(4):
        hk = pltpu.roll(h, 32 * k, 1) if k else h
        hi = hk.astype(BF16)
        mid = (hk - hi.astype(F32)).astype(BF16)
        both = jnp.dot(hot[k], jnp.concatenate([hi, mid], axis=1), preferred_element_type=F32)
        acc = acc + (both[:, :128] + both[:, 128:])
    return acc


def early_answer_kernel(hot, h0, h1, h2, out):
    h = h0[...] + pltpu.roll(h1[...], 6, 1) + pltpu.roll(h2[...], 12, 1)
    out[...] = pick(h, hot)


def answer_kernel(hot, early, h3, out):
    out[...] = (early[...] + pick(pltpu.roll(h3[...], 18, 1), hot)).reshape(128, 4, 128)


def building_start_kernel(d_in, v_in, hf, br, st, ms, yd, cnt, disp, vel, hyst, stiff, yld, gain):
    level = lax.broadcasted_iota(jnp.int32, (64, 128), 0)
    mask = jnp.where(level < cnt[0], 1.0, 0.0)
    y = yd[...] * mask
    stiff[...] = st[...] * mask
    yld[...] = y
    gain[...] = DT / ms[...]
    for c in range(3):
        disp[c] = d_in[c] * mask
        vel[c] = v_in[c] * mask
        flag = br[c]
        hyst[c] = jnp.where(flag == 1, y, jnp.where(flag == 2, -y, hf[c] * y))


def building_kernel(ret, key, kmod, cnt, d_in, v_in, h_in, st, yd, gn, d_out, v_out, h_out, ground, bufs, sem):
    pieces = split3(ret[...].reshape(512, 128).T)[:2]
    row512 = lax.broadcasted_iota(jnp.int32, (512, 128), 0).astype(F32)
    for j in range(8):
        lanes = pl.ds(128 * j, 128)
        hot = jnp.where(row512 == key[j : j + 1, :], 1.0, 0.0).astype(BF16)
        g = jnp.dot(pieces[0], hot, preferred_element_type=F32)
        g = g + jnp.dot(pieces[1], hot, preferred_element_type=F32)
        km = kmod[j : j + 1, :]
        acc = jnp.zeros((32, 128), F32)
        for k in range(4):
            acc = acc + jnp.where(km == k, g[32 * k : 32 * k + 32], 0.0)
        ground[:, lanes] = acc * (1.0 / DT)
    outs = (d_out, v_out, h_out)
    copies = []
    for c in range(3):

        def chunk(j, carry, c=c):
            lanes = pl.ds(pl.multiple_of(j * 128, 128), 128)
            level = lax.broadcasted_iota(jnp.int32, (64, 128), 0)
            first_row = level == 0
            last_row = level == 63
            mask = jnp.where(level < cnt[0:1, lanes], 1.0, 0.0)

            def drift_of(x):
                return x - jnp.where(first_row, 0.0, pltpu.roll(x, 1, 0))

            stiff = st[:, lanes]
            yld = yd[:, lanes]
            gain = gn[:, lanes]
            disp = d_in[c, :, lanes]
            vel = v_in[c, :, lanes]
            hyst = h_in[c, :, lanes]
            drift = drift_of(disp)
            for t in range(STEPS):
                spring = stiff * (POST * drift + (1.0 - POST) * hyst)
                above = jnp.where(last_row, 0.0, pltpu.roll(spring, 63, 0))
                row = ground[3 * t + c : 3 * t + c + 1, lanes]
                vel = vel * (1.0 - DT * DAMP) + (gain * (above - spring) - mask * row)
                disp = disp + DT * vel
                new = drift_of(disp)
                hyst = jnp.minimum(jnp.maximum(hyst + new - drift, -yld), yld)
                drift = new
            bufs[0, c, :, lanes] = disp
            bufs[1, c, :, lanes] = vel
            bufs[2, c, :, lanes] = hyst
            return carry

        lax.fori_loop(0, 8, chunk, 0)
        for n in range(3):
            cp = pltpu.make_async_copy(bufs.at[n, c], outs[n].at[c], sem.at[3 * c + n])
            cp.start()
            copies.append(cp)
    for cp in copies:
        cp.wait()


def building_start(sd, sv, hf, br, st, ms, yd, cnt):
    lanes3 = pl.BlockSpec((3, 64, 128), lambda i: (0, 0, i))
    lanes2 = pl.BlockSpec((64, 128), lambda i: (0, i))
    rows = pl.BlockSpec((1, 1, 128), lambda i: (i, 0, 0))
    return pl.pallas_call(
        building_start_kernel,
        out_shape=[sds(3, 64, 1024)] * 3 + [sds(64, 1024)] * 3,
        grid=(8,),
        in_specs=[lanes3] * 4 + [lanes2] * 3 + [rows],
        out_specs=[lanes3] * 3 + [lanes2] * 3,
        compiler_params=CP,
        name="building_start",
    )(sd, sv, hf, br, st, ms, yd, cnt.reshape(8, 1, 128))


def local(u, p, de, mu, la, sd, sv, hf, br, st, ms, yd, cnt, tile, cell):
    ix = lax.axis_index("gx")
    iy = lax.axis_index("gy")
    nx = lax.axis_size("gx")
    ny = lax.axis_size("gy")
    edge = jnp.stack([ix > 0, ix < nx - 1, iy > 0, iy < ny - 1]).astype(F32).reshape(1, 4)

    up, down = pl.pallas_call(
        pack_x_kernel,
        out_shape=[sds(XPLANES, 32, 128)] * 2,
        in_specs=[HB] * 5,
        out_specs=[VM] * 2,
        scratch_shapes=[pltpu.SemaphoreType.DMA((18,))],
        compiler_params=CP,
        name="pack_x",
    )(u, p, la, mu, de)
    north = ring(up, "gx", 1)
    south = ring(down, "gx", -1)

    req, key, kmod = pl.pallas_call(
        request_kernel,
        out_shape=[sds(128, 4, 128), sds(8, 128), sds(8, 128)],
        in_specs=[VM] * 2,
        out_specs=[VM] * 3,
        scratch_shapes=[pltpu.VMEM((512, 1024), BF16), pltpu.VMEM((128, 1024), BF16), pltpu.VMEM((128, 1024), BF16)],
        compiler_params=CP,
        name="requests",
    )(tile.reshape(8, 128).astype(F32), cell.reshape(8, 128).astype(F32))
    incoming = lax.all_to_all(req, ("gx", "gy"), 0, 0, tiled=True)
    north, south, incoming = lax.optimization_barrier((north, south, incoming))

    up, down = pl.pallas_call(
        pack_y_kernel,
        out_shape=[sds(YBLOCKS, 8, 128)] * 2,
        in_specs=[HB] * 5 + [VM] * 2,
        out_specs=[VM] * 2,
        scratch_shapes=[pltpu.SemaphoreType.DMA((18,))],
        compiler_params=CP,
        name="pack_y",
    )(u, p, la, mu, de, north, south)
    west = ring(up, "gy", 1)
    east = ring(down, "gy", -1)

    half = sds(3, 8, 32, 128)
    ue = pltpu.VMEM((3, 32, YR, 128), F32)
    ss = pltpu.VMEM((6, 32, YR, 128), F32)
    hh = pltpu.VMEM((16, 48, 128), F32)
    mz = pltpu.VMEM((256, 128), BF16)
    u1s = sds(3, 24, YR, 128)
    top, bot, prev, lam, mu2, q, hist = pl.pallas_call(
        first_round_kernel,
        out_shape=[half, half, u1s, sds(28, YR, 128), sds(28, YR, 128), sds(24, YR, 128), sds(512, 128)],
        in_specs=[SM] + [VM] * 9,
        out_specs=[VM] * 7,
        scratch_shapes=[ue, pltpu.VMEM((3, 24, YR, 128), F32), ss, hh, mz],
        compiler_params=CP,
        name="wave_first",
    )(edge, u, p, la, mu, de, north, south, west, east)
    hists = [hist]
    for r in range(1, 4):
        north = ring(bot, "gx", 1)
        south = ring(top, "gx", -1)
        if r == 1:
            starts = building_start(sd, sv, hf, br, st, ms, yd, cnt)
            hot = pl.pallas_call(
                hot_kernel,
                out_shape=jax.ShapeDtypeStruct((4, 512, 512), BF16),
                in_specs=[VM],
                out_specs=VM,
                compiler_params=CP,
                name="hot",
            )(incoming)
            north, south, hot, starts = lax.optimization_barrier((north, south, hot, starts))
        up, down = pl.pallas_call(
            pack_round_kernel,
            out_shape=[sds(3, 32, 8, 128)] * 2,
            in_specs=[VM] * 4,
            out_specs=[VM] * 2,
            compiler_params=CP,
            name="pack_round",
        )(top, bot, north, south)
        west = ring(up, "gy", 1)
        east = ring(down, "gy", -1)
        if r == 3:
            early = pl.pallas_call(
                early_answer_kernel,
                out_shape=sds(512, 128),
                in_specs=[VM] * 4,
                out_specs=VM,
                compiler_params=CP,
                name="early_answers",
            )(hot, *hists)
            west, east, early = lax.optimization_barrier((west, east, early))
        ins = (edge, top, bot, north, south, west, east, prev, lam, mu2, q)
        if r < 3:
            top, bot, prev, hist = pl.pallas_call(
                round_kernel,
                out_shape=[half, half, u1s, sds(512, 128)],
                in_specs=[SM] + [VM] * 10,
                out_specs=[VM] * 4,
                scratch_shapes=[ue, ss, hh, mz],
                compiler_params=CP,
                name="wave_round",
            )(*ins)
        else:
            now, before, hist = pl.pallas_call(
                last_kernel,
                out_shape=[sds(3, 16, 32, 128)] * 2 + [sds(512, 128)],
                in_specs=[SM] + [VM] * 10,
                out_specs=[VM] * 3,
                scratch_shapes=[ue, ss, hh, mz, pltpu.VMEM((3, 24, YR, 128), F32)],
                compiler_params=CP,
                name="wave_last",
            )(*ins)
        hists.append(hist)

    answers = pl.pallas_call(
        answer_kernel,
        out_shape=sds(128, 4, 128),
        in_specs=[VM] * 3,
        out_specs=VM,
        compiler_params=CP,
        name="answers",
    )(hot, early, hists[3])
    returned = lax.all_to_all(answers, ("gx", "gy"), 0, 0, tiled=True)
    disp, vel, hyst = pl.pallas_call(
        building_kernel,
        out_shape=[sds(3, 64, 1024)] * 3,
        in_specs=[VM] * 10,
        out_specs=[HB] * 3,
        scratch_shapes=[
            pltpu.VMEM((32, 1024), F32),
            pltpu.VMEM((3, 3, 64, 1024), F32),
            pltpu.SemaphoreType.DMA((9,)),
        ],
        compiler_params=CP,
        name="buildings",
    )(returned, key, kmod, cnt.reshape(1, 1024), *starts)
    return now, before, disp, vel, hyst


def solution(mesh):
    grid = P(None, "gx", "gy", None)
    cells = P("gx", "gy", None)
    both = ("gx", "gy")
    b3 = P(None, None, both)
    b2 = P(None, both)
    b1 = P(both)
    return jax.shard_map(
        local,
        mesh=mesh,
        in_specs=(grid, grid, cells, cells, cells, b3, b3, b3, b3, b2, b2, b2, b1, P(both, None), b1),
        out_specs=(grid, grid, b3, b3, b3),
        check_vma=False,
    )
```

time: 254 us -> 187 us (0.74)
  Pallas kernels: 108 us -> 49.5 us
  blocking collectives: 20.8 us -> 39 us
  starting transfers between devices: 38.1 us -> 22.4 us
  waiting for transfers between devices: 73 us -> 67.2 us
  local copies, waits for them, and re-layouts: 10.4 us -> 7.07 us
    pallas_call x2, Pallas kernels: 37.8 us -> 14.9 us  [local(): pl.pallas_call(round_kernel, out_shape=[half, half, u1s, sds(512, 128)],...]
    all_to_all x0 -> x1, blocking collectives: none -> 21.8 us  [local(): incoming = lax.all_to_all(req, ('gx', 'gy'), 0, 0, tiled=True)]
    pallas_call x1, Pallas kernels: 21 us -> 10.1 us  [local(): pl.pallas_call(first_round_kernel, out_shape=[half, half, u1s, sds(28, YR...]
    pallas_call x1, Pallas kernels: 18.6 us -> 8.36 us  [local(): pl.pallas_call(last_kernel, out_shape=[sds(3, 16, 32, 128)] * 2 + [sds(51...]
    all_to_all x1 -> x0, starting transfers between devices: 8.1 us -> none  [local(): incoming = lax.all_to_all(req, ('gx', 'gy'), 0, 0, tiled=True)]
    ppermute x16, starting transfers between devices: 30 us -> 22.4 us  [ring(): return lax.ppermute(x, axis, [(i, (i + step) % n) for i in range(n)])]
    pallas_call x3, Pallas kernels: 6.86 us -> 0.23 us  [local(): pl.pallas_call(pack_round_kernel, out_shape=[sds(3, 32, 8, 128)] * 2, in_...]
    ppermute x16, waiting for transfers between devices: 73 us -> 67.2 us  [ring(): return lax.ppermute(x, axis, [(i, (i + step) % n) for i in range(n)])]
  transfers between devices with their start and end apart: 17 -> 16, of which waited for: 10 -> 14; matrix products, arithmetic and copies ran while one was open for 1% -> 0% of each run, Pallas kernels for 8% -> 2%
where the time goes in v2:
time: 187 us; the launch traced here: 186 us
  waiting for transfers between devices  67.2 us (36%)
  Pallas kernels  49.5 us (26%)
  blocking collectives  39 us (21%)
  starting transfers between devices  22.4 us (12%)
  local copies, waits for them, and re-layouts  7.07 us (4%)
    ppermute x16, waiting for transfers between devices, ring(): return lax.ppermute(x, axis, [(i, (i + step) % n) for i in range(n)])  67.2 us
    ppermute x16, starting transfers between devices, ring(): return lax.ppermute(x, axis, [(i, (i + step) % n) for i in range(n)])  22.4 us
    all_to_all x1, blocking collectives, local(): incoming = lax.all_to_all(req, ('gx', 'gy'), 0, 0, tiled=True)  21.8 us
    all_to_all x1, blocking collectives, local(): returned = lax.all_to_all(answers, ('gx', 'gy'), 0, 0, tiled=True)  17.2 us
    pallas_call x2, Pallas kernels, local(): pl.pallas_call(round_kernel, out_shape=[half, half, u1s, sds(512, 128)],...  14.9 us
    pallas_call x1, Pallas kernels, local(): pl.pallas_call(first_round_kernel, out_shape=[half, half, u1s, sds(28, YR...  10.1 us
    pallas_call x1, Pallas kernels, local(): pl.pallas_call(last_kernel, out_shape=[sds(3, 16, 32, 128)] * 2 + [sds(51...  8.36 us
    unnamed x42, local copies, waits for them, and re-layouts  7.07 us
  transfers between devices with their start and end apart: 16, of which 14 were waited for; matrix products, arithmetic and copies ran while one was open for 0% of the time, Pallas kernels for 2%

profile of v2, /device:TPU:1, one launch (start us, length us, event | category | flops | bytes accessed | tf_op | source)
XLA Modules:
  0.0 186.4 jit_solution(9685836186674890311)
XLA Ops:
  5.8 2.4 %pack_x.1 = (f32[52,32,128]{2,1,0:T(8,128)S(1)}, f32[52,32,128]{2,1,0:T(8,128)S(1)}) custom-call(f32[3,16,32,128]{3,2,1,0:T(8,128)S(1)} %copy-done, f32[3,16,32,128]{3,2,1,0:T(8,128)S(1)} %copy-done.2, f32[16,32,128]{2,1,0:T(8,128)S(1)} %copy-done.4, f32[16,32,128]{2,1,0:T(8,128)S(1)} %copy-done.6, f32[16,32,128]{2,1,0:T(8,128)S(1)} %copy-done.8), custom_call_target="tpu_custom_call" | custom-call | tf_op jit(solution)/shard_map/pack_x/pallas_call | solution.py:482
  8.1 2.5 %collective-permute-start = (f32[52,32,128]{2,1,0:T(8,128)S(1)}, f32[52,32,128]{2,1,0:T(8,128)S(1)}, u32[]{:S(2)}, u32[]{:S(2)}) collective-permute-start(f32[52,32,128]{2,1,0:T(8,128)S(1)} %get-tuple-element.60), channel_id=1, source_target_pairs={{0,8},{8,16},{16,24},{24,32},{32,40},{40,48},{48,56},{56,64},{64,7... | collective-permute-start | bytes 2555912 | tf_op jit(solution)/shard_map/ppermute | solution.py:32
  10.7 4.7 %collective-permute-start.1 = (f32[52,32,128]{2,1,0:T(8,128)S(1)}, f32[52,32,128]{2,1,0:T(8,128)S(1)}, u32[]{:S(2)}, u32[]{:S(2)}) collective-permute-start(f32[52,32,128]{2,1,0:T(8,128)S(1)} %get-tuple-element.61), channel_id=1, source_target_pairs={{0,120},{8,0},{16,8},{24,16},{32,24},{40,32},{48,40},{56,48},{64,5... | collective-permute-start | bytes 2555912 | tf_op jit(solution)/shard_map/ppermute | solution.py:32
  16.5 21.8 %all_to_all.10.inc = f32[128,4,128]{2,1,0:T(4,128)} all-to-all(f32[128,4,128]{2,1,0:T(4,128)S(1)} %get-tuple-element.62), channel_id=1, replica_groups=mesh['gx'=16,'gy'=8] {'gx','gy'}, dimensions={0} | all-to-all | bytes 524288 | tf_op jit(solution)/shard_map/all_to_all | solution.py:503
  38.3 1.8 pack_y.1
  40.1 1.5 collective-permute-start.2
  41.7 11.6 %collective-permute-done.2.west = f32[248,8,128]{2,1,0:T(8,128)} collective-permute-done((f32[248,8,128]{2,1,0:T(8,128)}, f32[248,8,128]{2,1,0:T(8,128)}, u32[]{:S(2)}, u32[]{:S(2)}) %collective-permute-start.2) | collective-permute-done | bytes 1015840 | tf_op jit(solution)/shard_map/ppermute | solution.py:32
  53.3 2.5 %collective-permute-done.3.east = f32[248,8,128]{2,1,0:T(8,128)} collective-permute-done((f32[248,8,128]{2,1,0:T(8,128)}, f32[248,8,128]{2,1,0:T(8,128)}, u32[]{:S(2)}, u32[]{:S(2)}) %collective-permute-start.3) | collective-permute-done | bytes 1015840 | tf_op jit(solution)/shard_map/ppermute | solution.py:32
  57.8 10.1 %wave_first.1 = (f32[3,8,32,128]{3,2,1,0:T(8,128)S(1)}, f32[3,8,32,128]{3,2,1,0:T(8,128)S(1)}, f32[3,24,56,128]{3,2,1,0:T(8,128)S(1)}, f32[28,56,128]{2,1,0:T(8,...) custom-call(f32[1,4]{1,0:T(1,128)S(1)} %add_convert_fusion.flags, ...), custom_call_target="tpu_custom_call" | custom-call | tf_op jit(solution)/shard_map/wave_first/pallas_call | solution.py:524
  67.8 4.6 %collective-permute-start.5 = (f32[3,8,32,128]{3,2,1,0:T(8,128)S(1)}, f32[3,8,32,128]{3,2,1,0:T(8,128)S(1)}, u32[]{:S(2)}, u32[]{:S(2)}) collective-permute-start(f32[3,8,32,128]{3,2,1,0:T(8,128)S(1)} %get-tuple-element.67.top), channel_id=1, source_target_pairs={{0,120},{8,0},{16,8},{24,16},{32,24},{40,32},{48,40},{56,48},{64,5... | collective-permute-start | bytes 1179656 | tf_op jit(solution)/shard_map/ppermute | solution.py:32
  72.5 1.4 building_start.1
  74.6 6.4 %collective-permute-done.5.south = f32[3,8,32,128]{3,2,1,0:T(8,128)S(1)} collective-permute-done((f32[3,8,32,128]{3,2,1,0:T(8,128)S(1)}, f32[3,8,32,128]{3,2,1,0:T(8,128)S(1)}, u32[]{:S(2)}, u32[]{:S(2)}) %collective-permute-start.5) | collective-permute-done | bytes 393248 | tf_op jit(solution)/shard_map/ppermute | solution.py:32
  81.0 5.2 %collective-permute-done.4.north = f32[3,8,32,128]{3,2,1,0:T(8,128)S(1)} collective-permute-done((f32[3,8,32,128]{3,2,1,0:T(8,128)S(1)}, f32[3,8,32,128]{3,2,1,0:T(8,128)S(1)}, u32[]{:S(2)}, u32[]{:S(2)}) %collective-permute-start.4) | collective-permute-done | bytes 393248 | tf_op jit(solution)/shard_map/ppermute | solution.py:32
  86.3 1.5 collective-permute-start.6
  87.8 4.7 %collective-permute-done.6.west = f32[3,32,8,128]{3,2,1,0:T(8,128)S(1)} collective-permute-done((f32[3,32,8,128]{3,2,1,0:T(8,128)S(1)}, f32[3,32,8,128]{3,2,1,0:T(8,128)S(1)}, u32[]{:S(2)}, u32[]{:S(2)}) %collective-permute-start.6) | collective-permute-done | bytes 393248 | tf_op jit(solution)/shard_map/ppermute | solution.py:32
  92.5 2.8 %collective-permute-done.7.east = f32[3,32,8,128]{3,2,1,0:T(8,128)S(1)} collective-permute-done((f32[3,32,8,128]{3,2,1,0:T(8,128)S(1)}, f32[3,32,8,128]{3,2,1,0:T(8,128)S(1)}, u32[]{:S(2)}, u32[]{:S(2)}) %collective-permute-start.7) | collective-permute-done | bytes 393248 | tf_op jit(solution)/shard_map/ppermute | solution.py:32
  95.3 7.4 %wave_round.2 = (f32[3,8,32,128]{3,2,1,0:T(8,128)S(1)}, f32[3,8,32,128]{3,2,1,0:T(8,128)S(1)}, f32[3,24,56,128]{3,2,1,0:T(8,128)S(1)}, f32[512,128]{1,0:T(8,128)S(1)}) custom-call(f32[1,4]{1,0:T(1,128)S(1)} %add_convert_fusion.flags, f32[3,8,32,128]{3,2,1,0:T(8,128)S(1)} %get-tuple-element.67.top, f32[3,8,32,128]{3,2,1,0:T(8,128)S(1)} %get-tuple-element.68.bot, ...), custom_call_target="tpu_custom_call" | custom-call | tf_op jit(solution)/shard_map/wave_round/pallas_call | solution.py:570
  102.8 1.5 collective-permute-start.8
  104.3 8.7 %collective-permute-done.9.south = f32[3,8,32,128]{3,2,1,0:T(8,128)S(1)} collective-permute-done((f32[3,8,32,128]{3,2,1,0:T(8,128)S(1)}, f32[3,8,32,128]{3,2,1,0:T(8,128)S(1)}, u32[]{:S(2)}, u32[]{:S(2)}) %collective-permute-start.9) | collective-permute-done | bytes 393248 | tf_op jit(solution)/shard_map/ppermute | solution.py:32
  112.9 3.2 %collective-permute-done.8.north = f32[3,8,32,128]{3,2,1,0:T(8,128)S(1)} collective-permute-done((f32[3,8,32,128]{3,2,1,0:T(8,128)S(1)}, f32[3,8,32,128]{3,2,1,0:T(8,128)S(1)}, u32[]{:S(2)}, u32[]{:S(2)}) %collective-permute-start.8) | collective-permute-done | bytes 393248 | tf_op jit(solution)/shard_map/ppermute | solution.py:32
  117.8 3.7 %collective-permute-done.10.west = f32[3,32,8,128]{3,2,1,0:T(8,128)S(1)} collective-permute-done((f32[3,32,8,128]{3,2,1,0:T(8,128)S(1)}, f32[3,32,8,128]{3,2,1,0:T(8,128)S(1)}, u32[]{:S(2)}, u32[]{:S(2)}) %collective-permute-start.10) | collective-permute-done | bytes 393248 | tf_op jit(solution)/shard_map/ppermute | solution.py:32
  121.6 2.8 %collective-permute-done.11.east = f32[3,32,8,128]{3,2,1,0:T(8,128)S(1)} collective-permute-done((f32[3,32,8,128]{3,2,1,0:T(8,128)S(1)}, f32[3,32,8,128]{3,2,1,0:T(8,128)S(1)}, u32[]{:S(2)}, u32[]{:S(2)}) %collective-permute-start.11) | collective-permute-done | bytes 393248 | tf_op jit(solution)/shard_map/ppermute | solution.py:32
  124.3 7.4 %wave_round.3 = (f32[3,8,32,128]{3,2,1,0:T(8,128)S(1)}, f32[3,8,32,128]{3,2,1,0:T(8,128)S(1)}, f32[3,24,56,128]{3,2,1,0:T(8,128)S(1)}, f32[512,128]{1,0:T(8,128)S(1)}) custom-call(f32[1,4]{1,0:T(1,128)S(1)} %add_convert_fusion.flags, f32[3,8,32,128]{3,2,1,0:T(8,128)S(1)} %get-tuple-element.84.top, f32[3,8,32,128]{3,2,1,0:T(8,128)S(1)} %get-tuple-element.85.bot, ...), custom_call_target="tpu_custom_call" | custom-call | tf_op jit(solution)/shard_map/wave_round/pallas_call | solution.py:570
  131.9 1.5 collective-permute-start.12
  133.3 7.2 %collective-permute-done.13.south = f32[3,8,32,128]{3,2,1,0:T(8,128)S(1)} collective-permute-done((f32[3,8,32,128]{3,2,1,0:T(8,128)S(1)}, f32[3,8,32,128]{3,2,1,0:T(8,128)S(1)}, u32[]{:S(2)}, u32[]{:S(2)}) %collective-permute-start.13) | collective-permute-done | bytes 393248 | tf_op jit(solution)/shard_map/ppermute | solution.py:32
  140.6 3.6 %collective-permute-done.12.north = f32[3,8,32,128]{3,2,1,0:T(8,128)S(1)} collective-permute-done((f32[3,8,32,128]{3,2,1,0:T(8,128)S(1)}, f32[3,8,32,128]{3,2,1,0:T(8,128)S(1)}, u32[]{:S(2)}, u32[]{:S(2)}) %collective-permute-start.12) | collective-permute-done | bytes 393248 | tf_op jit(solution)/shard_map/ppermute | solution.py:32
  144.9 2.2 %collective-permute-start.15 = (f32[3,32,8,128]{3,2,1,0:T(8,128)S(1)}, f32[3,32,8,128]{3,2,1,0:T(8,128)S(1)}, u32[]{:S(2)}, u32[]{:S(2)}) collective-permute-start(f32[3,32,8,128]{3,2,1,0:T(8,128)S(1)} %get-tuple-element.92), channel_id=1, source_target_pairs={{0,7},{1,0},{2,1},{3,2},{4,3},{5,4},{6,5},{7,6},{8,15},{9,8},{10,9... | collective-permute-start | bytes 1179656 | tf_op jit(solution)/shard_map/ppermute | solution.py:32
  148.0 1.7 collective-permute-done.14.west
  149.6 3.2 %collective-permute-done.15.east = f32[3,32,8,128]{3,2,1,0:T(8,128)S(1)} collective-permute-done((f32[3,32,8,128]{3,2,1,0:T(8,128)S(1)}, f32[3,32,8,128]{3,2,1,0:T(8,128)S(1)}, u32[]{:S(2)}, u32[]{:S(2)}) %collective-permute-start.15) | collective-permute-done | bytes 393248 | tf_op jit(solution)/shard_map/ppermute | solution.py:32
  152.8 8.4 %wave_last.1 = (f32[3,16,32,128]{3,2,1,0:T(8,128)}, f32[3,16,32,128]{3,2,1,0:T(8,128)}, f32[512,128]{1,0:T(8,128)S(1)}) custom-call(f32[1,4]{1,0:T(1,128)S(1)} %add_convert_fusion.flags, f32[3,8,32,128]{3,2,1,0:T(8,128)S(1)} %get-tuple-element.89.top, f32[3,8,32,128]{3,2,1,0:T(8,128)S(1)} %get-tuple-element.90.bot, ...), custom_call_target="tpu_custom_call" | custom-call | tf_op jit(solution)/shard_map/wave_last/pallas_call | solution.py:580
  162.0 17.2 %all_to_all.11.ret = f32[128,4,128]{2,1,0:T(4,128)S(1)} all-to-all(f32[128,4,128]{2,1,0:T(4,128)S(1)} %answers.1), channel_id=1, replica_groups=mesh['gx'=16,'gy'=8] {'gx','gy'}, dimensions={0} | all-to-all | bytes 524288 | tf_op jit(solution)/shard_map/all_to_all | solution.py:599
  179.2 7.0 %buildings.1 = (f32[3,64,1024]{2,1,0:T(8,128)}, f32[3,64,1024]{2,1,0:T(8,128)}, f32[3,64,1024]{2,1,0:T(8,128)}) custom-call(f32[128,4,128]{2,1,0:T(4,128)S(1)} %all_to_all.11.ret, f32[8,128]{1,0:T(8,128)S(1)} %get-tuple-element.104.key, f32[8,128]{1,0:T(8,128)S(1)} %get-tuple-element.105.kmod, s32[1,1024]{1,0:T(1,128)S(1)} %bitcast.10, ...), custom_call_target="tpu_custom_call" | custom-call | tf_op jit(solution)/shard_map/buildings/pallas_call | solution.py:600
  (62 shorter events, 13.3 us)
Async XLA Ops:
  0.6 1.1 copy-start
  1.8 1.1 copy-start.2
  5.8 9.6 %copy-start.19 = (s32[1024,1]{0,1:T(1,128)S(1)}, s32[1024,1]{0,1:T(1,128)}, u32[]{:S(2)}) copy-start(s32[1024,1]{0,1:T(1,128)} %param.28) | copy-start | bytes 12292
  5.8 9.6 %copy-start.20 = (s32[1024]{0:T(1024)S(1)}, s32[1024]{0:T(1024)}, u32[]{:S(2)}) copy-start(s32[1024]{0:T(1024)} %param.29) | copy-start | bytes 12292
  5.8 32.5 %copy-start.1 = (f32[3,16,32,128]{3,2,1,0:T(8,128)S(1)}, f32[3,16,32,128]{3,2,1,0:T(8,128)}, u32[]{:S(2)}) copy-start(f32[3,16,32,128]{3,2,1,0:T(8,128)} %u.5) | copy-start | bytes 2359300
  8.1 30.1 %collective-permute-start = (f32[52,32,128]{2,1,0:T(8,128)S(1)}, f32[52,32,128]{2,1,0:T(8,128)S(1)}, u32[]{:S(2)}, u32[]{:S(2)}) collective-permute-start(f32[52,32,128]{2,1,0:T(8,128)S(1)} %get-tuple-element.60), channel_id=1, source_target_pairs={{0,8},{8,16},{16,24},{24,32},{32,40},{40,48},{48,56},{56,64},{64,7... | collective-permute-start | bytes 2555912 | tf_op jit(solution)/shard_map/ppermute | solution.py:32
  10.7 27.6 %collective-permute-start.1 = (f32[52,32,128]{2,1,0:T(8,128)S(1)}, f32[52,32,128]{2,1,0:T(8,128)S(1)}, u32[]{:S(2)}, u32[]{:S(2)}) collective-permute-start(f32[52,32,128]{2,1,0:T(8,128)S(1)} %get-tuple-element.61), channel_id=1, source_target_pairs={{0,120},{8,0},{16,8},{24,16},{32,24},{40,32},{48,40},{56,48},{64,5... | collective-permute-start | bytes 2555912 | tf_op jit(solution)/shard_map/ppermute | solution.py:32
  38.3 17.5 %copy-start.3 = (f32[3,16,32,128]{3,2,1,0:T(8,128)S(1)}, f32[3,16,32,128]{3,2,1,0:T(8,128)}, u32[]{:S(2)}) copy-start(f32[3,16,32,128]{3,2,1,0:T(8,128)} %p.5) | copy-start | bytes 2359300
  38.3 17.5 %copy-start.5 = (f32[16,32,128]{2,1,0:T(8,128)S(1)}, f32[16,32,128]{2,1,0:T(8,128)}, u32[]{:S(2)}) copy-start(f32[16,32,128]{2,1,0:T(8,128)} %la.5) | copy-start | bytes 786436
  40.1 13.2 %collective-permute-start.2 = (f32[248,8,128]{2,1,0:T(8,128)}, f32[248,8,128]{2,1,0:T(8,128)}, u32[]{:S(2)}, u32[]{:S(2)}) collective-permute-start(f32[248,8,128]{2,1,0:T(8,128)} %get-tuple-element.65), channel_id=1, source_target_pairs={{0,1},{1,2},{2,3},{3,4},{4,5},{5,6},{6,7},{7,0},{8,9},{9,10},{10,1... | collective-permute-start | bytes 3047432 | tf_op jit(solution)/shard_map/ppermute | solution.py:32
  41.6 14.2 %collective-permute-start.3 = (f32[248,8,128]{2,1,0:T(8,128)}, f32[248,8,128]{2,1,0:T(8,128)}, u32[]{:S(2)}, u32[]{:S(2)}) collective-permute-start(f32[248,8,128]{2,1,0:T(8,128)} %get-tuple-element.66), channel_id=1, source_target_pairs={{0,7},{1,0},{2,1},{3,2},{4,3},{5,4},{6,5},{7,6},{8,15},{9,8},{10,9... | collective-permute-start | bytes 3047432 | tf_op jit(solution)/shard_map/ppermute | solution.py:32
  57.7 14.8 %copy-start.11 = (f32[3,64,1024]{2,1,0:T(8,128)S(1)}, f32[3,64,1024]{2,1,0:T(8,128)}, u32[]{:S(2)}) copy-start(f32[3,64,1024]{2,1,0:T(8,128)} %d_in.1) | copy-start | bytes 2359300
  57.7 14.8 %copy-start.12 = (f32[3,64,1024]{2,1,0:T(8,128)S(1)}, f32[3,64,1024]{2,1,0:T(8,128)}, u32[]{:S(2)}) copy-start(f32[3,64,1024]{2,1,0:T(8,128)} %v_in.1) | copy-start | bytes 2359300
  57.7 14.8 %copy-start.13 = (f32[3,64,1024]{2,1,0:T(8,128)S(1)}, f32[3,64,1024]{2,1,0:T(8,128)}, u32[]{:S(2)}) copy-start(f32[3,64,1024]{2,1,0:T(8,128)} %hf.1) | copy-start | bytes 2359300
  57.7 14.8 %copy-start.14 = (s32[3,64,1024]{2,1,0:T(8,128)S(1)}, s32[3,64,1024]{2,1,0:T(8,128)}, u32[]{:S(2)}) copy-start(s32[3,64,1024]{2,1,0:T(8,128)} %br.1) | copy-start | bytes 2359300
  57.7 14.8 %copy-start.15 = (f32[64,1024]{1,0:T(8,128)S(1)}, f32[64,1024]{1,0:T(8,128)}, u32[]{:S(2)}) copy-start(f32[64,1024]{1,0:T(8,128)} %st.1) | copy-start | bytes 786436
  57.7 14.8 %copy-start.16 = (f32[64,1024]{1,0:T(8,128)S(1)}, f32[64,1024]{1,0:T(8,128)}, u32[]{:S(2)}) copy-start(f32[64,1024]{1,0:T(8,128)} %ms.1) | copy-start | bytes 786436
  57.8 14.8 %copy-start.17 = (f32[64,1024]{1,0:T(8,128)S(1)}, f32[64,1024]{1,0:T(8,128)}, u32[]{:S(2)}) copy-start(f32[64,1024]{1,0:T(8,128)} %yd.1) | copy-start | bytes 786436
  57.8 14.8 %copy-start.18 = (s32[1024]{0:T(1024)S(1)}, s32[1024]{0:T(1024)}, u32[]{:S(2)}) copy-start(s32[1024]{0:T(1024)} %param.27) | copy-start | bytes 12292
  67.8 6.1 %copy-start.10 = (f32[128,4,128]{2,1,0:T(4,128)S(1)}, f32[128,4,128]{2,1,0:T(4,128)}, u32[]{:S(2)}) copy-start(f32[128,4,128]{2,1,0:T(4,128)} %all_to_all.10.inc) | copy-start | bytes 786436
  67.8 13.1 %collective-permute-start.5 = (f32[3,8,32,128]{3,2,1,0:T(8,128)S(1)}, f32[3,8,32,128]{3,2,1,0:T(8,128)S(1)}, u32[]{:S(2)}, u32[]{:S(2)}) collective-permute-start(f32[3,8,32,128]{3,2,1,0:T(8,128)S(1)} %get-tuple-element.67.top), channel_id=1, source_target_pairs={{0,120},{8,0},{16,8},{24,16},{32,24},{40,32},{48,40},{56,48},{64,5... | collective-permute-start | bytes 1179656 | tf_op jit(solution)/shard_map/ppermute | solution.py:32
  72.5 13.7 %collective-permute-start.4 = (f32[3,8,32,128]{3,2,1,0:T(8,128)S(1)}, f32[3,8,32,128]{3,2,1,0:T(8,128)S(1)}, u32[]{:S(2)}, u32[]{:S(2)}) collective-permute-start(f32[3,8,32,128]{3,2,1,0:T(8,128)S(1)} %get-tuple-element.68.bot), channel_id=1, source_target_pairs={{0,8},{8,16},{16,24},{24,32},{32,40},{40,48},{48,56},{56,64},{64,7... | collective-permute-start | bytes 1179656 | tf_op jit(solution)/shard_map/ppermute | solution.py:32
  86.3 6.3 %collective-permute-start.6 = (f32[3,32,8,128]{3,2,1,0:T(8,128)S(1)}, f32[3,32,8,128]{3,2,1,0:T(8,128)S(1)}, u32[]{:S(2)}, u32[]{:S(2)}) collective-permute-start(f32[3,32,8,128]{3,2,1,0:T(8,128)S(1)} %get-tuple-element.78), channel_id=1, source_target_pairs={{0,1},{1,2},{2,3},{3,4},{4,5},{5,6},{6,7},{7,0},{8,9},{9,10},{10,1... | collective-permute-start | bytes 1179656 | tf_op jit(solution)/shard_map/ppermute | solution.py:32
  87.8 7.5 %collective-permute-start.7 = (f32[3,32,8,128]{3,2,1,0:T(8,128)S(1)}, f32[3,32,8,128]{3,2,1,0:T(8,128)S(1)}, u32[]{:S(2)}, u32[]{:S(2)}) collective-permute-start(f32[3,32,8,128]{3,2,1,0:T(8,128)S(1)} %get-tuple-element.79), channel_id=1, source_target_pairs={{0,7},{1,0},{2,1},{3,2},{4,3},{5,4},{6,5},{7,6},{8,15},{9,8},{10,9... | collective-permute-start | bytes 1179656 | tf_op jit(solution)/shard_map/ppermute | solution.py:32
  102.7 10.2 %collective-permute-start.9 = (f32[3,8,32,128]{3,2,1,0:T(8,128)S(1)}, f32[3,8,32,128]{3,2,1,0:T(8,128)S(1)}, u32[]{:S(2)}, u32[]{:S(2)}) collective-permute-start(f32[3,8,32,128]{3,2,1,0:T(8,128)S(1)} %get-tuple-element.84.top), channel_id=1, source_target_pairs={{0,120},{8,0},{16,8},{24,16},{32,24},{40,32},{48,40},{56,48},{64,5... | collective-permute-start | bytes 1179656 | tf_op jit(solution)/shard_map/ppermute | solution.py:32
  102.8 13.3 %collective-permute-start.8 = (f32[3,8,32,128]{3,2,1,0:T(8,128)S(1)}, f32[3,8,32,128]{3,2,1,0:T(8,128)S(1)}, u32[]{:S(2)}, u32[]{:S(2)}) collective-permute-start(f32[3,8,32,128]{3,2,1,0:T(8,128)S(1)} %get-tuple-element.85.bot), channel_id=1, source_target_pairs={{0,8},{8,16},{16,24},{24,32},{32,40},{40,48},{48,56},{56,64},{64,7... | collective-permute-start | bytes 1179656 | tf_op jit(solution)/shard_map/ppermute | solution.py:32
  116.2 5.4 %collective-permute-start.10 = (f32[3,32,8,128]{3,2,1,0:T(8,128)S(1)}, f32[3,32,8,128]{3,2,1,0:T(8,128)S(1)}, u32[]{:S(2)}, u32[]{:S(2)}) collective-permute-start(f32[3,32,8,128]{3,2,1,0:T(8,128)S(1)} %get-tuple-element.86), channel_id=1, source_target_pairs={{0,1},{1,2},{2,3},{3,4},{4,5},{5,6},{6,7},{7,0},{8,9},{9,10},{10,1... | collective-permute-start | bytes 1179656 | tf_op jit(solution)/shard_map/ppermute | solution.py:32
  116.8 7.5 %collective-permute-start.11 = (f32[3,32,8,128]{3,2,1,0:T(8,128)S(1)}, f32[3,32,8,128]{3,2,1,0:T(8,128)S(1)}, u32[]{:S(2)}, u32[]{:S(2)}) collective-permute-start(f32[3,32,8,128]{3,2,1,0:T(8,128)S(1)} %get-tuple-element.87), channel_id=1, source_target_pairs={{0,7},{1,0},{2,1},{3,2},{4,3},{5,4},{6,5},{7,6},{8,15},{9,8},{10,9... | collective-permute-start | bytes 1179656 | tf_op jit(solution)/shard_map/ppermute | solution.py:32
  131.8 8.8 %collective-permute-start.13 = (f32[3,8,32,128]{3,2,1,0:T(8,128)S(1)}, f32[3,8,32,128]{3,2,1,0:T(8,128)S(1)}, u32[]{:S(2)}, u32[]{:S(2)}) collective-permute-start(f32[3,8,32,128]{3,2,1,0:T(8,128)S(1)} %get-tuple-element.89.top), channel_id=1, source_target_pairs={{0,120},{8,0},{16,8},{24,16},{32,24},{40,32},{48,40},{56,48},{64,5... | collective-permute-start | bytes 1179656 | tf_op jit(solution)/shard_map/ppermute | solution.py:32
  131.9 12.3 %collective-permute-start.12 = (f32[3,8,32,128]{3,2,1,0:T(8,128)S(1)}, f32[3,8,32,128]{3,2,1,0:T(8,128)S(1)}, u32[]{:S(2)}, u32[]{:S(2)}) collective-permute-start(f32[3,8,32,128]{3,2,1,0:T(8,128)S(1)} %get-tuple-element.90.bot), channel_id=1, source_target_pairs={{0,8},{8,16},{16,24},{24,32},{32,40},{40,48},{48,56},{56,64},{64,7... | collective-permute-start | bytes 1179656 | tf_op jit(solution)/shard_map/ppermute | solution.py:32
  144.2 5.4 %collective-permute-start.14 = (f32[3,32,8,128]{3,2,1,0:T(8,128)S(1)}, f32[3,32,8,128]{3,2,1,0:T(8,128)S(1)}, u32[]{:S(2)}, u32[]{:S(2)}) collective-permute-start(f32[3,32,8,128]{3,2,1,0:T(8,128)S(1)} %get-tuple-element.91), channel_id=1, source_target_pairs={{0,1},{1,2},{2,3},{3,4},{4,5},{5,6},{6,7},{7,0},{8,9},{9,10},{10,1... | collective-permute-start | bytes 1179656 | tf_op jit(solution)/shard_map/ppermute | solution.py:32
  144.9 7.9 %collective-permute-start.15 = (f32[3,32,8,128]{3,2,1,0:T(8,128)S(1)}, f32[3,32,8,128]{3,2,1,0:T(8,128)S(1)}, u32[]{:S(2)}, u32[]{:S(2)}) collective-permute-start(f32[3,32,8,128]{3,2,1,0:T(8,128)S(1)} %get-tuple-element.92), channel_id=1, source_target_pairs={{0,7},{1,0},{2,1},{3,2},{4,3},{5,4},{6,5},{7,6},{8,15},{9,8},{10,9... | collective-permute-start | bytes 1179656 | tf_op jit(solution)/shard_map/ppermute | solution.py:32
  (5 other events, 4.8 us)

commit v3 on v2

v3 whole, which is shorter than its diff:
```python
import jax
import jax.numpy as jnp
from jax import lax
from jax.experimental import pallas as pl
from jax.experimental.pallas import tpu as pltpu
from jax.sharding import PartitionSpec as P

STEPS = 8
DT = 0.35
POST = 0.1
DAMP = 0.05
F32 = jnp.float32
BF16 = jnp.bfloat16
VM = pl.BlockSpec(memory_space=pltpu.VMEM)
SM = pl.BlockSpec(memory_space=pltpu.SMEM)
HB = pl.BlockSpec(memory_space=pltpu.HBM)
CP = pltpu.CompilerParams(vmem_limit_bytes=12 << 20)
YR = 56

XPARTS = ((0, 3, 8), (1, 3, 4), (2, 1, 6), (3, 1, 6), (4, 1, 4))
XPLANES = sum(c * w for _, c, w in XPARTS)


def sds(*shape):
    return jax.ShapeDtypeStruct(shape, F32)


def ring(x, axis, step):
    n = lax.axis_size(axis)
    return lax.ppermute(x, axis, [(i, (i + step) % n) for i in range(n)])


def split3(x):
    hi = x.astype(BF16)
    rest = x - hi.astype(F32)
    mid = rest.astype(BF16)
    low = (rest - mid.astype(F32)).astype(BF16)
    return hi, mid, low


def at_comp(ref, comps, c, rows, cols):
    return ref.at[c, rows, cols] if comps == 3 else ref.at[rows, cols]


def pack_first_kernel(u, p, la, mu, de, up, down, right, left, sem):
    args = (u, p, la, mu, de)
    copies = []
    off = 0
    row = 0
    for a, comps, w in XPARTS:
        for c in range(comps):
            full = pl.ds(0, 32)
            every = pl.ds(0, 16)
            for src, dst in (
                (at_comp(args[a], comps, c, pl.ds(16 - w, w), full), up.at[pl.ds(off, w)]),
                (at_comp(args[a], comps, c, pl.ds(0, w), full), down.at[pl.ds(off, w)]),
                (at_comp(args[a], comps, c, every, pl.ds(24, 8)), right.at[pl.ds(row, 16)]),
                (at_comp(args[a], comps, c, every, pl.ds(0, 8)), left.at[pl.ds(row, 16)]),
            ):
                cp = pltpu.make_async_copy(src, dst, sem.at[len(copies)])
                cp.start()
                copies.append(cp)
            off += w
            row += 16
    for cp in copies:
        cp.wait()


def pack_corner_kernel(north, south, right, left):
    for dst, col in ((right, 24), (left, 0)):
        dst[0] = north[:, col : col + 8]
        dst[1] = south[:, col : col + 8]


def z_matrix():
    i = lax.broadcasted_iota(jnp.int32, (256, 128), 0)
    j = lax.broadcasted_iota(jnp.int32, (256, 128), 1)
    d = jnp.where(i < 128, i, i - 128) - j
    one = jnp.ones((256, 128), F32)
    near = jnp.where(d == 1, 8.0 * one, 0.0) - jnp.where(d == -1, 8.0 * one, 0.0)
    far = jnp.where(d == 2, one, 0.0) - jnp.where(d == -2, one, 0.0)
    return (near - far).astype(BF16)


def pieces2(f):
    hi = f.astype(BF16)
    lo = (f - hi.astype(F32)).astype(BF16)
    return jnp.concatenate([hi, lo], axis=1)


def dz_all(fields, mz):
    n = fields[0].shape[0]
    lhs = pieces2(jnp.concatenate(fields, axis=0))
    out = jnp.dot(lhs, mz, preferred_element_type=F32)
    return [out[n * k : n * k + n] for k in range(len(fields))]


def dx(rows, k):
    return 8.0 * (rows[k + 3] - rows[k + 1]) - (rows[k + 4] - rows[k])


def dy(ref, c, x, y, n):
    near = ref[c, x, pl.ds(y + 1, n)] - ref[c, x, pl.ds(y - 1, n)]
    far = ref[c, x, pl.ds(y + 2, n)] - ref[c, x, pl.ds(y - 2, n)]
    return 8.0 * near - far


def for_x(count, fn):
    def body(i, carry):
        fn(i)
        return carry

    lax.fori_loop(0, count, body, 0)


def stress_rows(u, ux, s, sx, lam, mu, mz, blocks, m, n):
    rows = []
    fields = []
    for g0, y in blocks:
        r = [[u[c, g0 - ux - 2 + j, pl.ds(y, n)] for j in range(m + 4)] for c in range(3)]
        rows.append(r)
        fields += [r[c][k + 2] for k in range(m) for c in range(3)]
    zs = dz_all(fields, mz[...])
    for (g0, y), r in zip(blocks, rows):
        ys = pl.ds(y, n)
        for k in range(m):
            gx = g0 + k
            x = gx - ux
            z0, z1, z2 = zs[:3]
            zs = zs[3:]
            mm = mu[gx - 2, ys]
            g00 = dx(r[0], k)
            g11 = dy(u, 1, x, y, n)
            lt = lam[gx - 2, ys] * (g00 + g11 + z2)
            m2 = mm + mm
            s[0, gx - sx, ys] = lt + m2 * g00
            s[1, gx - sx, ys] = lt + m2 * g11
            s[2, gx - sx, ys] = lt + m2 * z2
            s[3, gx - sx, ys] = mm * (dy(u, 0, x, y, n) + dx(r[1], k))
            s[4, gx - sx, ys] = mm * (z0 + dx(r[2], k))
            s[5, gx - sx, ys] = mm * (z1 + dy(u, 2, x, y, n))


def forces(s, sx, q, mz, blocks, m, n):
    rows = []
    fields = []
    for g0, y in blocks:
        ys = pl.ds(y, n)
        r = [[s[c, g0 - sx - 2 + j, ys] for j in range(m + 4)] for c in (0, 3, 4)]
        rows.append(r)
        for k in range(m):
            fields += [r[2][k + 2], s[5, g0 - sx + k, ys], s[2, g0 - sx + k, ys]]
    zs = dz_all(fields, mz[...])
    out = []
    for (g0, y), r in zip(blocks, rows):
        mine = []
        for k in range(m):
            x = g0 + k
            z0, z1, z2 = zs[:3]
            zs = zs[3:]
            qk = q[x - 4, pl.ds(y, n)]
            mine.append(
                (
                    qk * (dx(r[0], k) + dy(s, 3, x - sx, y, n) + z0),
                    qk * (dx(r[1], k) + dy(s, 1, x - sx, y, n) + z1),
                    qk * (dx(r[2], k) + dy(s, 5, x - sx, y, n) + z2),
                )
            )
        out.append(mine)
    return out


def surface(fs, slot, old):
    lane = lax.broadcasted_iota(jnp.int32, fs[0].shape, 1)
    for c, f in enumerate(fs):
        v = pltpu.roll(f, slot + c, 1) if slot + c else f
        old = jnp.where(lane == slot + c, v, old)
    return old


def first_rows(ue, prev, q, s, hs, mz, u1, blocks, m, n, seen):
    for (i0, y), fr in zip(blocks, forces(s, 2, q, mz, [(i0 + 4, y) for i0, y in blocks], m, n)):
        ys = pl.ds(y, n)
        for k, fs in enumerate(fr):
            i = i0 + k
            if k in seen(i0):
                hs[i - 4, pl.ds(y - 4, n)] = surface(fs, 0, jnp.zeros((n, 128), F32))
            for c in range(3):
                now = ue[c, i + 4, ys]
                u1[c, i, ys] = (now - prev[c, i, ys]) + (now + fs[c])


def second_rows(ue, q, s, hs, mz, u1, hist, blocks, m, n):
    places = [(j0 + 8 * part + 8, y) for _, j0, part, y, _ in blocks]
    for (out, j0, part, y, side), fr in zip(blocks, forces(s, 6, q, mz, places, m, n)):
        ys = pl.ds(y, n)
        for k, fs in enumerate(fr):
            i = j0 + 8 * part + k
            r = pl.multiple_of(i * 32 + y - 8, 8)
            hist[pl.ds(r, n)] = surface(fs, 3, hs[i, pl.ds(y - 4, n)])
            for c in range(3):
                now = u1[c, i + 4, ys]
                v = (now - ue[c, i + 8, ys]) + (now + fs[c])
                out[c, j0 + k, pl.ds(y - 8, n)] = v
                if side is not None:
                    side[c, i] = v


def two_steps(prev, lam, mu, q, ue, s, s2, hs, u1, top, bot, hist, mz):
    mz[...] = z_matrix()
    none = lambda i0: ()
    every = lambda i0: range(4)
    for_x(7, lambda i: stress_rows(ue, 0, s, 2, lam, mu, mz, [(4 * i + 2, 2)], 4, 48))
    for_x(2, lambda i: first_rows(ue, prev, q, s, hs, mz, u1, [(20 * i, 4)], 4, 48, none))
    for_x(4, lambda i: first_rows(ue, prev, q, s, hs, mz, u1, [(4 * i + 4, 4)], 4, 48, every))
    for_x(5, lambda i: stress_rows(u1, 4, s2, 6, lam, mu, mz, [(4 * i + 6, 6)], 4, 48))
    for part, out in enumerate((top, bot)):
        for_x(2, lambda i: second_rows(ue, q, s2, hs, mz, u1, hist, [(out, 4 * i, part, 8, None)], 4, 32))


def patch_two_steps(prev, lam, mu, q, ue, s, s2, hs, u1, top, bot, hist, right, left, mz):
    mz[...] = z_matrix()
    stress_rows(ue, 0, s, 2, lam, mu, mz, [(x, y) for x in (2, 22) for y in (2, 38)], 8, 8)
    seen = lambda i0: range(4, 8) if i0 == 0 else range(4)
    first_rows(ue, prev, q, s, hs, mz, u1, [(i, y) for i in (0, 16) for y in (4, 36)], 8, 8, seen)
    stress_rows(u1, 4, s2, 6, lam, mu, mz, [(x, y) for x in (6, 18) for y in (6, 34)], 8, 8)
    blocks = [(o, 0, part, y, side) for part, o in enumerate((top, bot)) for y, side in ((8, left), (32, right))]
    second_rows(ue, q, s2, hs, mz, u1, hist, blocks, 8, 8)


def first_round_kernel(flags, u, p, la, mu, de, north, south, west, east, ue, s, s2, hs, u1, top, bot, hist, pe, lam, muo, q, mz, sem):
    fn, fs, fw, fe = [flags[0, k] for k in range(4)]
    copies = []
    args = (u, p, la, mu, de)
    exts = (ue, pe, lam, muo, q)
    off = 0
    row = 0
    for a, comps, w in XPARTS:
        for c in range(comps):
            ref = exts[a].at[c] if comps == 3 else exts[a]
            arg = args[a].at[c] if comps == 3 else args[a]
            cp = pltpu.make_async_copy(arg, ref.at[pl.ds(w, 16), pl.ds(8, 32)], sem.at[len(copies)])
            cp.start()
            copies.append(cp)
            none = jnp.zeros((8, 128), F32)
            for i in range(w):
                for x, strip, f in ((i, north, fn), (16 + w + i, south, fs)):
                    ref[x, 0:8] = none
                    ref[x, 8:40] = strip[off + i] * f
                    ref[x, 40:48] = none

            def mid(i, ref=ref, row=row, w=w):
                ref[w + i, 0:8] = west[row + i] * fw
                ref[w + i, 40:48] = east[row + i] * fe

            for_x(16, mid)
            off += w
            row += 16

    for cp in copies:
        cp.wait()

    def scale(i):
        lam[i, 0:48] = lam[i, 0:48] * (1.0 / 12.0)
        muo[i, 0:48] = muo[i, 0:48] * (1.0 / 12.0)

    for_x(28, scale)

    def invert(i):
        q[i, 0:48] = inverse_density(q[i, 0:48])

    for_x(24, invert)
    two_steps(pe, lam, muo, q, ue, s, s2, hs, u1, top, bot, hist, mz)


def inverse_density(d):
    return jnp.where(d > 0.0, (DT * DT / 12.0) / jnp.where(d > 0.0, d, 1.0), 0.0)


def first_patch_kernel(*refs):
    flags, wc, ec = refs[:3]
    ue, s, s2, hs, u1, top, bot, hist, pe, lam, mu, q, right, left, mz = refs[15:]
    fn, fs, fw, fe = [flags[0, k] for k in range(4)]
    exts = (ue, pe, lam, mu, q)
    off = 0
    for a, comps, w in XPARTS:
        for c in range(comps):
            ref = exts[a].at[c] if comps == 3 else exts[a]
            for i in range(w):
                for half, x, f in ((0, i, fn), (1, 16 + w + i, fs)):
                    for strip, y, g in ((wc, 0, fw), (ec, 40, fe)):
                        v = strip[half, off + i] * (f * g)
                        if a in (2, 3):
                            v = v * (1.0 / 12.0)
                        ref[x, y : y + 8] = inverse_density(v) if a == 4 else v
            off += w
    patch_two_steps(pe, lam, mu, q, ue, s, s2, hs, u1, top, bot, hist, right, left, mz)


def round_kernel(flags, top, bot, north, south, west, east, prev, lam, mu, q, ue, s, s2, hs, u1, top2, bot2, hist, mz):
    fn, fs, fw, fe = [flags[0, k] for k in range(4)]
    none = jnp.zeros((8, 128), F32)
    for c in range(3):

        def rows(i, c=c):
            for x, strip, f in ((i, north, fn), (24 + i, south, fs)):
                ue[c, x, 0:8] = none
                ue[c, x, 8:40] = strip[8 * c + i] * f
                ue[c, x, 40:48] = none
            for x, strip in ((i, top), (8 + i, bot)):
                ue[c, 8 + x, 0:8] = west[c, x] * fw
                ue[c, 8 + x, 8:40] = strip[c, i]
                ue[c, 8 + x, 40:48] = east[c, x] * fe

        for_x(8, rows)
    two_steps(prev, lam, mu, q, ue, s, s2, hs, u1, top2, bot2, hist, mz)


def fill_corners(flags, wc, ec, ue):
    fn, fs, fw, fe = [flags[0, k] for k in range(4)]
    for c in range(3):

        def rows(i, c=c):
            for half, x, f in ((0, i, fn), (1, 24 + i, fs)):
                ue[c, x, 0:8] = wc[half, 8 * c + i] * (f * fw)
                ue[c, x, 40:48] = ec[half, 8 * c + i] * (f * fe)

        for_x(8, rows)


def patch_kernel(*refs):
    flags, wc, ec, prev, lam, mu, q = refs[:7]
    ue, s, s2, hs, u1, top, bot, hist, right, left, mz = refs[15:]
    fill_corners(flags, wc, ec, ue)
    patch_two_steps(prev, lam, mu, q, ue, s, s2, hs, u1, top, bot, hist, right, left, mz)


def last_patch_kernel(*refs):
    flags, wc, ec, prev, lam, mu, q = refs[:7]
    ue, s, s2, hs, u1, top, bot, hist, now, before, right, left, mz = refs[15:]
    fill_corners(flags, wc, ec, ue)
    patch_two_steps(prev, lam, mu, q, ue, s, s2, hs, u1, top, bot, hist, right, left, mz)
    for c in range(3):

        def rows(i, c=c):
            now[c, i] = top[c, i]
            now[c, 8 + i] = bot[c, i]
            before[c, i] = u1[c, i + 4, 8:40]
            before[c, 8 + i] = u1[c, i + 12, 8:40]

        for_x(8, rows)


def request_kernel(tile, cell, req, key, kmod, a_ref, bhi, blo):
    ones = jnp.ones((128, 128), F32)
    sub = lax.broadcasted_iota(jnp.int32, (128, 128), 0)
    lan = lax.broadcasted_iota(jnp.int32, (128, 128), 1)
    cols = [(ones * tile[i : i + 1, :]).T for i in range(8)]
    row512 = lax.broadcasted_iota(jnp.int32, (512, 128), 0).astype(F32)
    subf = sub.astype(F32)
    for j in range(8):
        mine = tile[j : j + 1, :]
        acc = jnp.where((cols[j] == mine) & (sub < lan), 1.0, 0.0)
        for i in range(j):
            acc = acc + jnp.where(cols[i] == mine, 1.0, 0.0)
        rank = jnp.sum(acc, axis=0, keepdims=True)
        quarter = jnp.floor(rank * 0.25)
        kj = mine * 4.0 + quarter
        mj = rank - 4.0 * quarter
        key[j : j + 1, :] = kj
        kmod[j : j + 1, :] = mj
        lanes = pl.ds(128 * j, 128)
        a_ref[:, lanes] = jnp.where(row512 == kj, 1.0, 0.0).astype(BF16)
        cj = cell[j : j + 1, :]
        hi = jnp.floor(cj * (1.0 / 32.0))
        hit = subf == mj
        bhi[:, lanes] = jnp.where(hit, hi, 0.0).astype(BF16)
        blo[:, lanes] = jnp.where(hit, cj - 32.0 * hi, 0.0).astype(BF16)
    dims = (((1,), (1,)), ((), ()))
    top = lax.dot_general(a_ref[...], bhi[...], dims, preferred_element_type=F32)
    low = lax.dot_general(a_ref[...], blo[...], dims, preferred_element_type=F32)
    req[...] = (32.0 * top + low).reshape(128, 4, 128)


def hot_kernel(inc, hot):
    cells = inc[...].reshape(512, 128)
    lane = lax.broadcasted_iota(jnp.int32, (512, 512), 1).astype(F32)
    for k in range(4):
        hot[k] = jnp.where(lane == cells[:, k : k + 1], 1.0, 0.0).astype(BF16)


def pick(h, hot):
    acc = jnp.zeros((512, 128), F32)
    for k in range(4):
        hk = pltpu.roll(h, 32 * k, 1) if k else h
        hi = hk.astype(BF16)
        mid = (hk - hi.astype(F32)).astype(BF16)
        both = jnp.dot(hot[k], jnp.concatenate([hi, mid], axis=1), preferred_element_type=F32)
        acc = acc + (both[:, :128] + both[:, 128:])
    return acc


def early_answer_kernel(hot, h0, h1, h2, out):
    h = h0[...] + pltpu.roll(h1[...], 6, 1) + pltpu.roll(h2[...], 12, 1)
    out[...] = pick(h, hot)


def answer_kernel(hot, early, h3, out):
    out[...] = (early[...] + pick(pltpu.roll(h3[...], 18, 1), hot)).reshape(128, 4, 128)


def building_start_kernel(d_in, v_in, hf, br, st, ms, yd, cnt, disp, vel, hyst, stiff, yld, gain):
    level = lax.broadcasted_iota(jnp.int32, (64, 128), 0)
    mask = jnp.where(level < cnt[0], 1.0, 0.0)
    y = yd[...] * mask
    stiff[...] = st[...] * mask
    yld[...] = y
    gain[...] = DT / ms[...]
    for c in range(3):
        disp[c] = d_in[c] * mask
        vel[c] = v_in[c] * mask
        flag = br[c]
        hyst[c] = jnp.where(flag == 1, y, jnp.where(flag == 2, -y, hf[c] * y))


def building_kernel(ret, key, kmod, cnt, d_in, v_in, h_in, st, yd, gn, d_out, v_out, h_out, ground, bufs, sem):
    pieces = split3(ret[...].reshape(512, 128).T)[:2]
    row512 = lax.broadcasted_iota(jnp.int32, (512, 128), 0).astype(F32)
    for j in range(8):
        lanes = pl.ds(128 * j, 128)
        hot = jnp.where(row512 == key[j : j + 1, :], 1.0, 0.0).astype(BF16)
        g = jnp.dot(pieces[0], hot, preferred_element_type=F32)
        g = g + jnp.dot(pieces[1], hot, preferred_element_type=F32)
        km = kmod[j : j + 1, :]
        acc = jnp.zeros((32, 128), F32)
        for k in range(4):
            acc = acc + jnp.where(km == k, g[32 * k : 32 * k + 32], 0.0)
        ground[:, lanes] = acc * (1.0 / DT)
    outs = (d_out, v_out, h_out)
    copies = []
    for c in range(3):

        def chunk(j, carry, c=c):
            lanes = pl.ds(pl.multiple_of(j * 128, 128), 128)
            level = lax.broadcasted_iota(jnp.int32, (64, 128), 0)
            first_row = level == 0
            last_row = level == 63
            mask = jnp.where(level < cnt[0:1, lanes], 1.0, 0.0)

            def drift_of(x):
                return x - jnp.where(first_row, 0.0, pltpu.roll(x, 1, 0))

            stiff = st[:, lanes]
            yld = yd[:, lanes]
            gain = gn[:, lanes]
            disp = d_in[c, :, lanes]
            vel = v_in[c, :, lanes]
            hyst = h_in[c, :, lanes]
            drift = drift_of(disp)
            for t in range(STEPS):
                spring = stiff * (POST * drift + (1.0 - POST) * hyst)
                above = jnp.where(last_row, 0.0, pltpu.roll(spring, 63, 0))
                row = ground[3 * t + c : 3 * t + c + 1, lanes]
                vel = vel * (1.0 - DT * DAMP) + (gain * (above - spring) - mask * row)
                disp = disp + DT * vel
                new = drift_of(disp)
                hyst = jnp.minimum(jnp.maximum(hyst + new - drift, -yld), yld)
                drift = new
            bufs[0, c, :, lanes] = disp
            bufs[1, c, :, lanes] = vel
            bufs[2, c, :, lanes] = hyst
            return carry

        lax.fori_loop(0, 8, chunk, 0)
        for n in range(3):
            cp = pltpu.make_async_copy(bufs.at[n, c], outs[n].at[c], sem.at[3 * c + n])
            cp.start()
            copies.append(cp)
    for cp in copies:
        cp.wait()


def building_start(sd, sv, hf, br, st, ms, yd, cnt):
    lanes3 = pl.BlockSpec((3, 64, 128), lambda i: (0, 0, i))
    lanes2 = pl.BlockSpec((64, 128), lambda i: (0, i))
    rows = pl.BlockSpec((1, 1, 128), lambda i: (i, 0, 0))
    return pl.pallas_call(
        building_start_kernel,
        out_shape=[sds(3, 64, 1024)] * 3 + [sds(64, 1024)] * 3,
        grid=(8,),
        in_specs=[lanes3] * 4 + [lanes2] * 3 + [rows],
        out_specs=[lanes3] * 3 + [lanes2] * 3,
        compiler_params=CP,
        name="building_start",
    )(sd, sv, hf, br, st, ms, yd, cnt.reshape(8, 1, 128))


def local(u, p, de, mu, la, sd, sv, hf, br, st, ms, yd, cnt, tile, cell):
    ix = lax.axis_index("gx")
    iy = lax.axis_index("gy")
    nx = lax.axis_size("gx")
    ny = lax.axis_size("gy")
    edge = jnp.stack([ix > 0, ix < nx - 1, iy > 0, iy < ny - 1]).astype(F32).reshape(1, 4)

    hbm = [pltpu.with_memory_space_constraint(x, pltpu.HBM) for x in (u, p, la, mu, de)]
    up, down, right, left = pl.pallas_call(
        pack_first_kernel,
        out_shape=[sds(XPLANES, 32, 128)] * 2 + [sds(144, 8, 128)] * 2,
        in_specs=[HB] * 5,
        out_specs=[VM] * 4,
        scratch_shapes=[pltpu.SemaphoreType.DMA((36,))],
        compiler_params=CP,
        name="pack_first",
    )(*hbm)
    north, south = ring(up, "gx", 1), ring(down, "gx", -1)
    west, east = ring(right, "gy", 1), ring(left, "gy", -1)

    req, key, kmod = pl.pallas_call(
        request_kernel,
        out_shape=[sds(128, 4, 128), sds(8, 128), sds(8, 128)],
        in_specs=[VM] * 2,
        out_specs=[VM] * 3,
        scratch_shapes=[pltpu.VMEM((512, 1024), BF16), pltpu.VMEM((128, 1024), BF16), pltpu.VMEM((128, 1024), BF16)],
        compiler_params=CP,
        name="requests",
    )(tile.reshape(8, 128).astype(F32), cell.reshape(8, 128).astype(F32))
    incoming = lax.all_to_all(req, ("gx", "gy"), 0, 0, tiled=True)
    north, south, west, east, incoming = lax.optimization_barrier((north, south, west, east, incoming))

    def corners(north, south):
        n = north.shape[0]
        right, left = pl.pallas_call(
            pack_corner_kernel,
            out_shape=[sds(2, n, 8, 128)] * 2,
            in_specs=[VM] * 2,
            out_specs=[VM] * 2,
            compiler_params=CP,
            name="pack_corner",
        )(north, south)
        return ring(right, "gy", 1), ring(left, "gy", -1)

    half = sds(3, 8, 32, 128)
    side = sds(3, 16, 8, 128)
    band = pltpu.VMEM((256, 128), BF16)
    work = [sds(3, 32, YR, 128), sds(6, 28, YR, 128), sds(6, 20, YR, 128), sds(16, 48, 128), sds(3, 24, YR, 128), half, half, sds(512, 128)]
    mats = [sds(3, 24, YR, 128), sds(28, YR, 128), sds(28, YR, 128), sds(24, YR, 128)]
    wc, ec = corners(north, south)
    state = pl.pallas_call(
        first_round_kernel,
        out_shape=work + mats,
        in_specs=[SM] + [HB] * 5 + [VM] * 4,
        out_specs=[VM] * 12,
        scratch_shapes=[band, pltpu.SemaphoreType.DMA((9,))],
        compiler_params=CP,
        name="wave_first",
    )(edge, *hbm, north, south, west, east)
    state = pl.pallas_call(
        first_patch_kernel,
        out_shape=work + mats + [side, side],
        in_specs=[SM] + [VM] * 14,
        out_specs=[VM] * 14,
        input_output_aliases={3 + n: n for n in range(12)},
        scratch_shapes=[band],
        compiler_params=CP,
        name="patch_first",
    )(edge, wc, ec, *state)
    prev, top, bot, hist = state[4:8]
    lam, mu2, q = state[9:12]
    right, left = state[12:14]
    hists = [hist]
    for r in range(1, 4):
        north, south = ring(bot.reshape(24, 32, 128), "gx", 1), ring(top.reshape(24, 32, 128), "gx", -1)
        west, east = ring(right, "gy", 1), ring(left, "gy", -1)
        if r == 1:
            starts = building_start(sd, sv, hf, br, st, ms, yd, cnt)
            hot = pl.pallas_call(
                hot_kernel,
                out_shape=jax.ShapeDtypeStruct((4, 512, 512), BF16),
                in_specs=[VM],
                out_specs=VM,
                compiler_params=CP,
                name="hot",
            )(incoming)
            north, south, hot, starts = lax.optimization_barrier((north, south, hot, starts))
        if r == 3:
            early = pl.pallas_call(
                early_answer_kernel,
                out_shape=sds(512, 128),
                in_specs=[VM] * 4,
                out_specs=VM,
                compiler_params=CP,
                name="early_answers",
            )(hot, *hists)
            north, south, early = lax.optimization_barrier((north, south, early))
        wc, ec = corners(north, south)
        consts = (prev, lam, mu2, q)
        state = pl.pallas_call(
            round_kernel,
            out_shape=work,
            in_specs=[SM] + [VM] * 10,
            out_specs=[VM] * 8,
            scratch_shapes=[band],
            compiler_params=CP,
            name="wave_round",
        )(edge, top, bot, north, south, west, east, *consts)
        last = r == 3
        state = pl.pallas_call(
            last_patch_kernel if last else patch_kernel,
            out_shape=work + ([sds(3, 16, 32, 128)] * 2 if last else [side, side]),
            in_specs=[SM] + [VM] * 14,
            out_specs=[VM] * 10,
            input_output_aliases={7 + n: n for n in range(8)},
            scratch_shapes=([pltpu.VMEM((3, 16, 8, 128), F32)] * 2 if last else []) + [band],
            compiler_params=CP,
            name="patch_last" if last else "patch_round",
        )(edge, wc, ec, *consts, *state)
        prev, top, bot, hist, right, left = state[4:10]
        hists.append(hist)
    now, before = right, left

    answers = pl.pallas_call(
        answer_kernel,
        out_shape=sds(128, 4, 128),
        in_specs=[VM] * 3,
        out_specs=VM,
        compiler_params=CP,
        name="answers",
    )(hot, early, hists[3])
    returned = lax.all_to_all(answers, ("gx", "gy"), 0, 0, tiled=True)
    disp, vel, hyst = pl.pallas_call(
        building_kernel,
        out_shape=[sds(3, 64, 1024)] * 3,
        in_specs=[VM] * 10,
        out_specs=[HB] * 3,
        scratch_shapes=[
            pltpu.VMEM((32, 1024), F32),
            pltpu.VMEM((3, 3, 64, 1024), F32),
            pltpu.SemaphoreType.DMA((9,)),
        ],
        compiler_params=CP,
        name="buildings",
    )(returned, key, kmod, cnt.reshape(1, 1024), *starts)
    return now, before, disp, vel, hyst


def solution(mesh):
    grid = P(None, "gx", "gy", None)
    cells = P("gx", "gy", None)
    both = ("gx", "gy")
    b3 = P(None, None, both)
    b2 = P(None, both)
    b1 = P(both)
    return jax.shard_map(
        local,
        mesh=mesh,
        in_specs=(grid, grid, cells, cells, cells, b3, b3, b3, b3, b2, b2, b2, b1, P(both, None), b1),
        out_specs=(grid, grid, b3, b3, b3),
        check_vma=False,
    )
```

time: 187 us -> 154 us (0.82)
  waiting for transfers between devices: 67.2 us -> 12.3 us
  starting transfers between devices: 22.4 us -> 42.9 us
  Pallas kernels: 49.5 us -> 58.5 us
  local copies, waits for them, and re-layouts: 7.07 us -> 0.05 us
    ppermute x16 -> x24, waiting for transfers between devices: 67.2 us -> 12.3 us  [ring(): return lax.ppermute(x, axis, [(i, (i + step) % n) for i in range(n)])]
    ppermute x16 -> x24, starting transfers between devices: 22.4 us -> 42.9 us  [ring(): return lax.ppermute(x, axis, [(i, (i + step) % n) for i in range(n)])]
    pallas_call x9 -> x13, Pallas kernels: 37.7 us -> 46.7 us  [the longest x3 23.1 us: local(): pl.pallas_call(round_kernel, out_shape=work, in_specs=[SM] + [VM] * 10, o...]
    unnamed x42 -> x16, local copies, waits for them, and re-layouts: 7.07 us -> 0.05 us
    all_to_all x1, blocking collectives: 21.8 us -> 17.8 us  [local(): incoming = lax.all_to_all(req, ('gx', 'gy'), 0, 0, tiled=True)]
    all_to_all x1, blocking collectives: 17.2 us -> 19.9 us  [local(): returned = lax.all_to_all(answers, ('gx', 'gy'), 0, 0, tiled=True)]
  transfers between devices with their start and end apart: 16 -> 24, of which waited for: 14 -> 3; matrix products, arithmetic and copies ran while one was open for 0% -> 1% of each run, Pallas kernels for 2% -> 24%
where the time goes in v3:
time: 154 us
  Pallas kernels  58.5 us (38%)
  starting transfers between devices  42.9 us (28%)
  blocking collectives  37.7 us (24%)
  waiting for transfers between devices  12.3 us (8%)
    ppermute x24, starting transfers between devices, ring(): return lax.ppermute(x, axis, [(i, (i + step) % n) for i in range(n)])  42.9 us
    pallas_call x3, Pallas kernels, local(): pl.pallas_call(round_kernel, out_shape=work, in_specs=[SM] + [VM] * 10, o...  23.1 us
    all_to_all x1, blocking collectives, local(): returned = lax.all_to_all(answers, ('gx', 'gy'), 0, 0, tiled=True)  19.9 us
    all_to_all x1, blocking collectives, local(): incoming = lax.all_to_all(req, ('gx', 'gy'), 0, 0, tiled=True)  17.8 us
    ppermute x24, waiting for transfers between devices, ring(): return lax.ppermute(x, axis, [(i, (i + step) % n) for i in range(n)])  12.3 us
    pallas_call x1, Pallas kernels, local(): pl.pallas_call(first_round_kernel, out_shape=work + mats, in_specs=[SM] +...  10.3 us
    pallas_call x3, Pallas kernels, local(): pl.pallas_call(last_patch_kernel if last else patch_kernel, out_shape=wor...  7.43 us
    pallas_call x1, Pallas kernels, local(): pl.pallas_call(building_kernel, out_shape=[sds(3, 64, 1024)] * 3, in_spec...  6.97 us
  transfers between devices with their start and end apart: 24, of which 3 were waited for; matrix products, arithmetic and copies ran while one was open for 1% of the time, Pallas kernels for 24%

profile of v3, /device:TPU:1, one launch (start us, length us, event | category | flops | bytes accessed | tf_op | source)
XLA Modules:
  0.0 154.1 jit_solution(2334786381371859381)
XLA Ops:
  0.6 2.1 %pack_first.1 = (f32[52,32,128]{2,1,0:T(8,128)S(1)}, f32[52,32,128]{2,1,0:T(8,128)S(1)}, f32[144,8,128]{2,1,0:T(8,128)S(1)}, f32[144,8,128]{2,1,0:T(8,128)S(1)}) custom-call(f32[3,16,32,128]{3,2,1,0:T(8,128)} %u.3, f32[3,16,32,128]{3,2,1,0:T(8,128)} %p.3, f32[16,32,128]{2,1,0:T(8,128)} %la.3, f32[16,32,128]{2,1,0:T(8,128)} %mu.3, f32[16,32,128]{2,1,0:T(8,128)} %de.3), custom_call_target="tpu_custom_call" | custom-call | tf_op jit(solution)/shard_map/pack_first/pallas_call | solution.py:506
  2.8 2.5 %collective-permute-start = (f32[52,32,128]{2,1,0:T(8,128)S(1)}, f32[52,32,128]{2,1,0:T(8,128)S(1)}, u32[]{:S(2)}, u32[]{:S(2)}) collective-permute-start(f32[52,32,128]{2,1,0:T(8,128)S(1)} %get-tuple-element.106), channel_id=1, source_target_pairs={{0,8},{8,16},{16,24},{24,32},{32,40},{40,48},{48,56},{56,64},{64,7... | collective-permute-start | bytes 2555912 | tf_op jit(solution)/shard_map/ppermute | solution.py:30
  5.3 4.7 %collective-permute-start.1 = (f32[52,32,128]{2,1,0:T(8,128)S(1)}, f32[52,32,128]{2,1,0:T(8,128)S(1)}, u32[]{:S(2)}, u32[]{:S(2)}) collective-permute-start(f32[52,32,128]{2,1,0:T(8,128)S(1)} %get-tuple-element.107), channel_id=1, source_target_pairs={{0,120},{8,0},{16,8},{24,16},{32,24},{40,32},{48,40},{56,48},{64,5... | collective-permute-start | bytes 2555912 | tf_op jit(solution)/shard_map/ppermute | solution.py:30
  9.9 2.1 %collective-permute-start.2 = (f32[144,8,128]{2,1,0:T(8,128)S(1)}, f32[144,8,128]{2,1,0:T(8,128)S(1)}, u32[]{:S(2)}, u32[]{:S(2)}) collective-permute-start(f32[144,8,128]{2,1,0:T(8,128)S(1)} %get-tuple-element.108), channel_id=1, source_target_pairs={{0,1},{1,2},{2,3},{3,4},{4,5},{5,6},{6,7},{7,0},{8,9},{9,10},{10,1... | collective-permute-start | bytes 1769480 | tf_op jit(solution)/shard_map/ppermute | solution.py:30
  13.4 1.1 requests.1
  14.5 17.8 %all_to_all.10.inc = f32[128,4,128]{2,1,0:T(4,128)S(1)} all-to-all(f32[128,4,128]{2,1,0:T(4,128)S(1)} %get-tuple-element.110), channel_id=1, replica_groups=mesh['gx'=16,'gy'=8] {'gx','gy'}, dimensions={0} | all-to-all | bytes 524288 | tf_op jit(solution)/shard_map/all_to_all | solution.py:527
  32.3 1.0 pack_corner.4
  33.3 1.6 %collective-permute-start.4 = (f32[2,52,8,128]{3,2,1,0:T(8,128)}, f32[2,52,8,128]{3,2,1,0:T(8,128)}, u32[]{:S(2)}, u32[]{:S(2)}) collective-permute-start(f32[2,52,8,128]{3,2,1,0:T(8,128)} %get-tuple-element.113), channel_id=1, source_target_pairs={{0,1},{1,2},{2,3},{3,4},{4,5},{5,6},{6,7},{7,0},{8,9},{9,10},{10,1... | collective-permute-start | bytes 1277960 | tf_op jit(solution)/shard_map/ppermute | solution.py:30
  35.0 10.3 %wave_first.1 = (f32[3,32,56,128]{3,2,1,0:T(8,128)S(1)}, f32[6,28,56,128]{3,2,1,0:T(8,128)S(1)}, f32[6,20,56,128]{3,2,1,0:T(8,128)S(1)}, f32[16,48,128]{2,1,0:T(...) custom-call(f32[1,4]{1,0:T(1,128)S(1)} %add_convert_fusion.flags.ref, ...), custom_call_target="tpu_custom_call" | custom-call | tf_op jit(solution)/shard_map/wave_first/pallas_call | solution.py:548
  45.4 2.7 %patch_first.1 = (f32[3,32,56,128]{3,2,1,0:T(8,128)S(1)}, f32[6,28,56,128]{3,2,1,0:T(8,128)S(1)}, f32[6,20,56,128]{3,2,1,0:T(8,128)S(1)}, f32[16,48,128]{2,1,0:T...) custom-call(f32[1,4]{1,0:T(1,128)S(1)} %add_convert_fusion.flags.ref, ...), custom_call_target="tpu_custom_call", output_to_operand_aliasing={{0}: (3, {}), {1}: (4, {}), {2}: (5, {}), {3}: (6, {}), {4}... | custom-call | tf_op jit(solution)/shard_map/patch_first/pallas_call | solution.py:557
  48.8 4.4 %collective-permute-start.7 = (f32[24,32,128]{2,1,0:T(8,128)S(1)}, f32[24,32,128]{2,1,0:T(8,128)S(1)}, u32[]{:S(2)}, u32[]{:S(2)}) collective-permute-start(f32[24,32,128]{2,1,0:T(8,128)S(1)} %bitcast.15), channel_id=1, source_target_pairs={{0,120},{8,0},{16,8},{24,16},{32,24},{40,32},{48,40},{56,48},{64,5... | collective-permute-start | bytes 1179656 | tf_op jit(solution)/shard_map/ppermute | solution.py:30
  53.2 1.4 building_start.1
  55.3 2.1 %collective-permute-start.10 = (f32[3,16,8,128]{3,2,1,0:T(8,128)S(1)}, f32[3,16,8,128]{3,2,1,0:T(8,128)S(1)}, u32[]{:S(2)}, u32[]{:S(2)}) collective-permute-start(f32[3,16,8,128]{3,2,1,0:T(8,128)S(1)} %get-tuple-element.146), channel_id=1, source_target_pairs={{0,1},{1,2},{2,3},{3,4},{4,5},{5,6},{6,7},{7,0},{8,9},{9,10},{10,1... | collective-permute-start | bytes 589832 | tf_op jit(solution)/shard_map/ppermute | solution.py:30
  57.4 3.3 %collective-permute-done.6.north = f32[24,32,128]{2,1,0:T(8,128)S(1)} collective-permute-done((f32[24,32,128]{2,1,0:T(8,128)S(1)}, f32[24,32,128]{2,1,0:T(8,128)S(1)}, u32[]{:S(2)}, u32[]{:S(2)}) %collective-permute-start.6) | collective-permute-done | bytes 393248 | tf_op jit(solution)/shard_map/ppermute | solution.py:30
  60.7 3.8 %collective-permute-start.8 = (f32[2,24,8,128]{3,2,1,0:T(8,128)S(1)}, f32[2,24,8,128]{3,2,1,0:T(8,128)S(1)}, u32[]{:S(2)}, u32[]{:S(2)}) collective-permute-start(f32[2,24,8,128]{3,2,1,0:T(8,128)S(1)} %get-tuple-element.140), channel_id=1, source_target_pairs={{0,1},{1,2},{2,3},{3,4},{4,5},{5,6},{6,7},{7,0},{8,9},{9,10},{10,1... | collective-permute-start | bytes 589832 | tf_op jit(solution)/shard_map/ppermute | solution.py:30
  64.5 7.7 %wave_round.3 = (f32[3,32,56,128]{3,2,1,0:T(8,128)S(1)}, f32[6,28,56,128]{3,2,1,0:T(8,128)S(1)}, f32[6,20,56,128]{3,2,1,0:T(8,128)S(1)}, f32[16,48,128]{2,1,0:T(...) custom-call(f32[1,4]{1,0:T(1,128)S(1)} %add_convert_fusion.flags.ref, ...), custom_call_target="tpu_custom_call" | custom-call | tf_op jit(solution)/shard_map/wave_round/pallas_call | solution.py:597
  72.2 2.0 %patch_round.2 = (f32[3,32,56,128]{3,2,1,0:T(8,128)S(1)}, f32[6,28,56,128]{3,2,1,0:T(8,128)S(1)}, f32[6,20,56,128]{3,2,1,0:T(8,128)S(1)}, f32[16,48,128]{2,1,0:T...) custom-call(f32[1,4]{1,0:T(1,128)S(1)} %add_convert_fusion.flags.ref, ...), custom_call_target="tpu_custom_call", output_to_operand_aliasing={{0}: (7, {}), {1}: (8, {}), {2}: (9, {}), {3}: (10, {}), {4... | custom-call | tf_op jit(solution)/shard_map/patch_round/pallas_call | solution.py:607
  74.3 5.1 %collective-permute-start.13 = (f32[24,32,128]{2,1,0:T(8,128)S(1)}, f32[24,32,128]{2,1,0:T(8,128)S(1)}, u32[]{:S(2)}, u32[]{:S(2)}) collective-permute-start(f32[24,32,128]{2,1,0:T(8,128)S(1)} %bitcast.17), channel_id=1, source_target_pairs={{0,120},{8,0},{16,8},{24,16},{32,24},{40,32},{48,40},{56,48},{64,5... | collective-permute-start | bytes 1179656 | tf_op jit(solution)/shard_map/ppermute | solution.py:30
  79.4 2.0 %collective-permute-start.16 = (f32[3,16,8,128]{3,2,1,0:T(8,128)S(1)}, f32[3,16,8,128]{3,2,1,0:T(8,128)S(1)}, u32[]{:S(2)}, u32[]{:S(2)}) collective-permute-start(f32[3,16,8,128]{3,2,1,0:T(8,128)S(1)} %get-tuple-element.161), channel_id=1, source_target_pairs={{0,1},{1,2},{2,3},{3,4},{4,5},{5,6},{6,7},{7,0},{8,9},{9,10},{10,1... | collective-permute-start | bytes 589832 | tf_op jit(solution)/shard_map/ppermute | solution.py:30
  81.4 5.2 %collective-permute-done.12.north = f32[24,32,128]{2,1,0:T(8,128)S(1)} collective-permute-done((f32[24,32,128]{2,1,0:T(8,128)S(1)}, f32[24,32,128]{2,1,0:T(8,128)S(1)}, u32[]{:S(2)}, u32[]{:S(2)}) %collective-permute-start.12) | collective-permute-done | bytes 393248 | tf_op jit(solution)/shard_map/ppermute | solution.py:30
  86.7 3.3 %collective-permute-start.14 = (f32[2,24,8,128]{3,2,1,0:T(8,128)S(1)}, f32[2,24,8,128]{3,2,1,0:T(8,128)S(1)}, u32[]{:S(2)}, u32[]{:S(2)}) collective-permute-start(f32[2,24,8,128]{3,2,1,0:T(8,128)S(1)} %get-tuple-element.158), channel_id=1, source_target_pairs={{0,1},{1,2},{2,3},{3,4},{4,5},{5,6},{6,7},{7,0},{8,9},{9,10},{10,1... | collective-permute-start | bytes 589832 | tf_op jit(solution)/shard_map/ppermute | solution.py:30
  90.0 7.7 %wave_round.4 = (f32[3,32,56,128]{3,2,1,0:T(8,128)S(1)}, f32[6,28,56,128]{3,2,1,0:T(8,128)S(1)}, f32[6,20,56,128]{3,2,1,0:T(8,128)S(1)}, f32[16,48,128]{2,1,0:T(...) custom-call(f32[1,4]{1,0:T(1,128)S(1)} %add_convert_fusion.flags.ref, ...), custom_call_target="tpu_custom_call" | custom-call | tf_op jit(solution)/shard_map/wave_round/pallas_call | solution.py:597
  97.8 2.0 %patch_round.3 = (f32[3,32,56,128]{3,2,1,0:T(8,128)S(1)}, f32[6,28,56,128]{3,2,1,0:T(8,128)S(1)}, f32[6,20,56,128]{3,2,1,0:T(8,128)S(1)}, f32[16,48,128]{2,1,0:T...) custom-call(f32[1,4]{1,0:T(1,128)S(1)} %add_convert_fusion.flags.ref, ...), custom_call_target="tpu_custom_call", output_to_operand_aliasing={{0}: (7, {}), {1}: (8, {}), {2}: (9, {}), {3}: (10, {}), {4... | custom-call | tf_op jit(solution)/shard_map/patch_round/pallas_call | solution.py:607
  99.9 5.1 %collective-permute-start.19 = (f32[24,32,128]{2,1,0:T(8,128)S(1)}, f32[24,32,128]{2,1,0:T(8,128)S(1)}, u32[]{:S(2)}, u32[]{:S(2)}) collective-permute-start(f32[24,32,128]{2,1,0:T(8,128)S(1)} %bitcast.19), channel_id=1, source_target_pairs={{0,120},{8,0},{16,8},{24,16},{32,24},{40,32},{48,40},{56,48},{64,5... | collective-permute-start | bytes 1179656 | tf_op jit(solution)/shard_map/ppermute | solution.py:30
  105.0 2.0 %collective-permute-start.22 = (f32[3,16,8,128]{3,2,1,0:T(8,128)S(1)}, f32[3,16,8,128]{3,2,1,0:T(8,128)S(1)}, u32[]{:S(2)}, u32[]{:S(2)}) collective-permute-start(f32[3,16,8,128]{3,2,1,0:T(8,128)S(1)} %get-tuple-element.182), channel_id=1, source_target_pairs={{0,1},{1,2},{2,3},{3,4},{4,5},{5,6},{6,7},{7,0},{8,9},{9,10},{10,1... | collective-permute-start | bytes 589832 | tf_op jit(solution)/shard_map/ppermute | solution.py:30
  107.5 0.9 early_answers.1.early
  108.3 3.8 %collective-permute-done.18.north = f32[24,32,128]{2,1,0:T(8,128)S(1)} collective-permute-done((f32[24,32,128]{2,1,0:T(8,128)S(1)}, f32[24,32,128]{2,1,0:T(8,128)S(1)}, u32[]{:S(2)}, u32[]{:S(2)}) %collective-permute-start.18) | collective-permute-done | bytes 393248 | tf_op jit(solution)/shard_map/ppermute | solution.py:30
  112.1 3.0 %collective-permute-start.20 = (f32[2,24,8,128]{3,2,1,0:T(8,128)S(1)}, f32[2,24,8,128]{3,2,1,0:T(8,128)S(1)}, u32[]{:S(2)}, u32[]{:S(2)}) collective-permute-start(f32[2,24,8,128]{3,2,1,0:T(8,128)S(1)} %get-tuple-element.179), channel_id=1, source_target_pairs={{0,1},{1,2},{2,3},{3,4},{4,5},{5,6},{6,7},{7,0},{8,9},{9,10},{10,1... | collective-permute-start | bytes 589832 | tf_op jit(solution)/shard_map/ppermute | solution.py:30
  115.1 7.7 %wave_round.5 = (f32[3,32,56,128]{3,2,1,0:T(8,128)S(1)}, f32[6,28,56,128]{3,2,1,0:T(8,128)S(1)}, f32[6,20,56,128]{3,2,1,0:T(8,128)S(1)}, f32[16,48,128]{2,1,0:T(...) custom-call(f32[1,4]{1,0:T(1,128)S(1)} %add_convert_fusion.flags.ref, ...), custom_call_target="tpu_custom_call" | custom-call | tf_op jit(solution)/shard_map/wave_round/pallas_call | solution.py:597
  122.9 3.3 %patch_last.1 = (f32[3,32,56,128]{3,2,1,0:T(8,128)S(1)}, f32[6,28,56,128]{3,2,1,0:T(8,128)S(1)}, f32[6,20,56,128]{3,2,1,0:T(8,128)S(1)}, f32[16,48,128]{2,1,0:T(...) custom-call(f32[1,4]{1,0:T(1,128)S(1)} %add_convert_fusion.flags.ref, ...), custom_call_target="tpu_custom_call", output_to_operand_aliasing={{0}: (7, {}), {1}: (8, {}), {2}: (9, {}), {3}: (10, {}), {4... | custom-call | tf_op jit(solution)/shard_map/patch_last/pallas_call | solution.py:607
  127.1 19.9 %all_to_all.11.ret = f32[128,4,128]{2,1,0:T(4,128)S(1)} all-to-all(f32[128,4,128]{2,1,0:T(4,128)S(1)} %answers.1), channel_id=1, replica_groups=mesh['gx'=16,'gy'=8] {'gx','gy'}, dimensions={0} | all-to-all | bytes 524288 | tf_op jit(solution)/shard_map/all_to_all | solution.py:629
  147.0 7.0 %buildings.1 = (f32[3,64,1024]{2,1,0:T(8,128)}, f32[3,64,1024]{2,1,0:T(8,128)}, f32[3,64,1024]{2,1,0:T(8,128)}) custom-call(f32[128,4,128]{2,1,0:T(4,128)S(1)} %all_to_all.11.ret, f32[8,128]{1,0:T(8,128)S(1)} %get-tuple-element.196.key, f32[8,128]{1,0:T(8,128)S(1)} %get-tuple-element.197.kmod, s32[1,1024]{1,0:T(1,128)S(1)} %bitcast.22, ...), custom_call_target="tpu_custom_call" | custom-call | tf_op jit(solution)/shard_map/buildings/pallas_call | solution.py:630
  (56 shorter events, 4.5 us)
Async XLA Ops:
  2.8 29.6 %collective-permute-start = (f32[52,32,128]{2,1,0:T(8,128)S(1)}, f32[52,32,128]{2,1,0:T(8,128)S(1)}, u32[]{:S(2)}, u32[]{:S(2)}) collective-permute-start(f32[52,32,128]{2,1,0:T(8,128)S(1)} %get-tuple-element.106), channel_id=1, source_target_pairs={{0,8},{8,16},{16,24},{24,32},{32,40},{40,48},{48,56},{56,64},{64,7... | collective-permute-start | bytes 2555912 | tf_op jit(solution)/shard_map/ppermute | solution.py:30
  5.3 27.0 %collective-permute-start.1 = (f32[52,32,128]{2,1,0:T(8,128)S(1)}, f32[52,32,128]{2,1,0:T(8,128)S(1)}, u32[]{:S(2)}, u32[]{:S(2)}) collective-permute-start(f32[52,32,128]{2,1,0:T(8,128)S(1)} %get-tuple-element.107), channel_id=1, source_target_pairs={{0,120},{8,0},{16,8},{24,16},{32,24},{40,32},{48,40},{56,48},{64,5... | collective-permute-start | bytes 2555912 | tf_op jit(solution)/shard_map/ppermute | solution.py:30
  9.9 22.4 %collective-permute-start.2 = (f32[144,8,128]{2,1,0:T(8,128)S(1)}, f32[144,8,128]{2,1,0:T(8,128)S(1)}, u32[]{:S(2)}, u32[]{:S(2)}) collective-permute-start(f32[144,8,128]{2,1,0:T(8,128)S(1)} %get-tuple-element.108), channel_id=1, source_target_pairs={{0,1},{1,2},{2,3},{3,4},{4,5},{5,6},{6,7},{7,0},{8,9},{9,10},{10,1... | collective-permute-start | bytes 1769480 | tf_op jit(solution)/shard_map/ppermute | solution.py:30
  12.0 20.3 %collective-permute-start.3 = (f32[144,8,128]{2,1,0:T(8,128)S(1)}, f32[144,8,128]{2,1,0:T(8,128)S(1)}, u32[]{:S(2)}, u32[]{:S(2)}) collective-permute-start(f32[144,8,128]{2,1,0:T(8,128)S(1)} %get-tuple-element.109), channel_id=1, source_target_pairs={{0,7},{1,0},{2,1},{3,2},{4,3},{5,4},{6,5},{7,6},{8,15},{9,8},{10,9... | collective-permute-start | bytes 1769480 | tf_op jit(solution)/shard_map/ppermute | solution.py:30
  33.3 11.9 %collective-permute-start.4 = (f32[2,52,8,128]{3,2,1,0:T(8,128)}, f32[2,52,8,128]{3,2,1,0:T(8,128)}, u32[]{:S(2)}, u32[]{:S(2)}) collective-permute-start(f32[2,52,8,128]{3,2,1,0:T(8,128)} %get-tuple-element.113), channel_id=1, source_target_pairs={{0,1},{1,2},{2,3},{3,4},{4,5},{5,6},{6,7},{7,0},{8,9},{9,10},{10,1... | collective-permute-start | bytes 1277960 | tf_op jit(solution)/shard_map/ppermute | solution.py:30
  34.9 10.4 %collective-permute-start.5 = (f32[2,52,8,128]{3,2,1,0:T(8,128)}, f32[2,52,8,128]{3,2,1,0:T(8,128)}, u32[]{:S(2)}, u32[]{:S(2)}) collective-permute-start(f32[2,52,8,128]{3,2,1,0:T(8,128)} %get-tuple-element.114), channel_id=1, source_target_pairs={{0,7},{1,0},{2,1},{3,2},{4,3},{5,4},{6,5},{7,6},{8,15},{9,8},{10,9... | collective-permute-start | bytes 1277960 | tf_op jit(solution)/shard_map/ppermute | solution.py:30
  45.3 7.9 %copy-start = (f32[3,64,1024]{2,1,0:T(8,128)S(1)}, f32[3,64,1024]{2,1,0:T(8,128)}, u32[]{:S(2)}) copy-start(f32[3,64,1024]{2,1,0:T(8,128)} %d_in.1) | copy-start | bytes 2359300
  45.3 7.9 %copy-start.1 = (f32[3,64,1024]{2,1,0:T(8,128)S(1)}, f32[3,64,1024]{2,1,0:T(8,128)}, u32[]{:S(2)}) copy-start(f32[3,64,1024]{2,1,0:T(8,128)} %v_in.1) | copy-start | bytes 2359300
  45.3 7.9 %copy-start.2 = (f32[3,64,1024]{2,1,0:T(8,128)S(1)}, f32[3,64,1024]{2,1,0:T(8,128)}, u32[]{:S(2)}) copy-start(f32[3,64,1024]{2,1,0:T(8,128)} %hf.1) | copy-start | bytes 2359300
  45.3 7.9 %copy-start.3 = (s32[3,64,1024]{2,1,0:T(8,128)S(1)}, s32[3,64,1024]{2,1,0:T(8,128)}, u32[]{:S(2)}) copy-start(s32[3,64,1024]{2,1,0:T(8,128)} %br.1) | copy-start | bytes 2359300
  45.3 7.9 %copy-start.4 = (f32[64,1024]{1,0:T(8,128)S(1)}, f32[64,1024]{1,0:T(8,128)}, u32[]{:S(2)}) copy-start(f32[64,1024]{1,0:T(8,128)} %st.1) | copy-start | bytes 786436
  45.3 7.9 %copy-start.5 = (f32[64,1024]{1,0:T(8,128)S(1)}, f32[64,1024]{1,0:T(8,128)}, u32[]{:S(2)}) copy-start(f32[64,1024]{1,0:T(8,128)} %ms.1) | copy-start | bytes 786436
  45.4 7.9 %copy-start.6 = (f32[64,1024]{1,0:T(8,128)S(1)}, f32[64,1024]{1,0:T(8,128)}, u32[]{:S(2)}) copy-start(f32[64,1024]{1,0:T(8,128)} %yd.1) | copy-start | bytes 786436
  45.4 7.9 %copy-start.7 = (s32[1024]{0:T(1024)S(1)}, s32[1024]{0:T(1024)}, u32[]{:S(2)}) copy-start(s32[1024]{0:T(1024)} %param.27) | copy-start | bytes 12292
  48.1 12.5 %collective-permute-start.6 = (f32[24,32,128]{2,1,0:T(8,128)S(1)}, f32[24,32,128]{2,1,0:T(8,128)S(1)}, u32[]{:S(2)}, u32[]{:S(2)}) collective-permute-start(f32[24,32,128]{2,1,0:T(8,128)S(1)} %bitcast.16), channel_id=1, source_target_pairs={{0,8},{8,16},{16,24},{24,32},{32,40},{40,48},{48,56},{56,64},{64,7... | collective-permute-start | bytes 1179656 | tf_op jit(solution)/shard_map/ppermute | solution.py:30
  48.8 11.8 %collective-permute-start.7 = (f32[24,32,128]{2,1,0:T(8,128)S(1)}, f32[24,32,128]{2,1,0:T(8,128)S(1)}, u32[]{:S(2)}, u32[]{:S(2)}) collective-permute-start(f32[24,32,128]{2,1,0:T(8,128)S(1)} %bitcast.15), channel_id=1, source_target_pairs={{0,120},{8,0},{16,8},{24,16},{32,24},{40,32},{48,40},{56,48},{64,5... | collective-permute-start | bytes 1179656 | tf_op jit(solution)/shard_map/ppermute | solution.py:30
  55.3 9.2 %collective-permute-start.10 = (f32[3,16,8,128]{3,2,1,0:T(8,128)S(1)}, f32[3,16,8,128]{3,2,1,0:T(8,128)S(1)}, u32[]{:S(2)}, u32[]{:S(2)}) collective-permute-start(f32[3,16,8,128]{3,2,1,0:T(8,128)S(1)} %get-tuple-element.146), channel_id=1, source_target_pairs={{0,1},{1,2},{2,3},{3,4},{4,5},{5,6},{6,7},{7,0},{8,9},{9,10},{10,1... | collective-permute-start | bytes 589832 | tf_op jit(solution)/shard_map/ppermute | solution.py:30
  57.4 7.1 %collective-permute-start.11 = (f32[3,16,8,128]{3,2,1,0:T(8,128)S(1)}, f32[3,16,8,128]{3,2,1,0:T(8,128)S(1)}, u32[]{:S(2)}, u32[]{:S(2)}) collective-permute-start(f32[3,16,8,128]{3,2,1,0:T(8,128)S(1)} %get-tuple-element.147), channel_id=1, source_target_pairs={{0,7},{1,0},{2,1},{3,2},{4,3},{5,4},{6,5},{7,6},{8,15},{9,8},{10,9... | collective-permute-start | bytes 589832 | tf_op jit(solution)/shard_map/ppermute | solution.py:30
  60.7 11.5 %collective-permute-start.8 = (f32[2,24,8,128]{3,2,1,0:T(8,128)S(1)}, f32[2,24,8,128]{3,2,1,0:T(8,128)S(1)}, u32[]{:S(2)}, u32[]{:S(2)}) collective-permute-start(f32[2,24,8,128]{3,2,1,0:T(8,128)S(1)} %get-tuple-element.140), channel_id=1, source_target_pairs={{0,1},{1,2},{2,3},{3,4},{4,5},{5,6},{6,7},{7,0},{8,9},{9,10},{10,1... | collective-permute-start | bytes 589832 | tf_op jit(solution)/shard_map/ppermute | solution.py:30
  64.4 7.7 %collective-permute-start.9 = (f32[2,24,8,128]{3,2,1,0:T(8,128)S(1)}, f32[2,24,8,128]{3,2,1,0:T(8,128)S(1)}, u32[]{:S(2)}, u32[]{:S(2)}) collective-permute-start(f32[2,24,8,128]{3,2,1,0:T(8,128)S(1)} %get-tuple-element.141), channel_id=1, source_target_pairs={{0,7},{1,0},{2,1},{3,2},{4,3},{5,4},{6,5},{7,6},{8,15},{9,8},{10,9... | collective-permute-start | bytes 589832 | tf_op jit(solution)/shard_map/ppermute | solution.py:30
  74.2 12.4 %collective-permute-start.12 = (f32[24,32,128]{2,1,0:T(8,128)S(1)}, f32[24,32,128]{2,1,0:T(8,128)S(1)}, u32[]{:S(2)}, u32[]{:S(2)}) collective-permute-start(f32[24,32,128]{2,1,0:T(8,128)S(1)} %bitcast.18), channel_id=1, source_target_pairs={{0,8},{8,16},{16,24},{24,32},{32,40},{40,48},{48,56},{56,64},{64,7... | collective-permute-start | bytes 1179656 | tf_op jit(solution)/shard_map/ppermute | solution.py:30
  74.3 12.4 %collective-permute-start.13 = (f32[24,32,128]{2,1,0:T(8,128)S(1)}, f32[24,32,128]{2,1,0:T(8,128)S(1)}, u32[]{:S(2)}, u32[]{:S(2)}) collective-permute-start(f32[24,32,128]{2,1,0:T(8,128)S(1)} %bitcast.17), channel_id=1, source_target_pairs={{0,120},{8,0},{16,8},{24,16},{32,24},{40,32},{48,40},{56,48},{64,5... | collective-permute-start | bytes 1179656 | tf_op jit(solution)/shard_map/ppermute | solution.py:30
  79.4 10.6 %collective-permute-start.16 = (f32[3,16,8,128]{3,2,1,0:T(8,128)S(1)}, f32[3,16,8,128]{3,2,1,0:T(8,128)S(1)}, u32[]{:S(2)}, u32[]{:S(2)}) collective-permute-start(f32[3,16,8,128]{3,2,1,0:T(8,128)S(1)} %get-tuple-element.161), channel_id=1, source_target_pairs={{0,1},{1,2},{2,3},{3,4},{4,5},{5,6},{6,7},{7,0},{8,9},{9,10},{10,1... | collective-permute-start | bytes 589832 | tf_op jit(solution)/shard_map/ppermute | solution.py:30
  81.4 8.6 %collective-permute-start.17 = (f32[3,16,8,128]{3,2,1,0:T(8,128)S(1)}, f32[3,16,8,128]{3,2,1,0:T(8,128)S(1)}, u32[]{:S(2)}, u32[]{:S(2)}) collective-permute-start(f32[3,16,8,128]{3,2,1,0:T(8,128)S(1)} %get-tuple-element.162), channel_id=1, source_target_pairs={{0,7},{1,0},{2,1},{3,2},{4,3},{5,4},{6,5},{7,6},{8,15},{9,8},{10,9... | collective-permute-start | bytes 589832 | tf_op jit(solution)/shard_map/ppermute | solution.py:30
  86.7 11.0 %collective-permute-start.14 = (f32[2,24,8,128]{3,2,1,0:T(8,128)S(1)}, f32[2,24,8,128]{3,2,1,0:T(8,128)S(1)}, u32[]{:S(2)}, u32[]{:S(2)}) collective-permute-start(f32[2,24,8,128]{3,2,1,0:T(8,128)S(1)} %get-tuple-element.158), channel_id=1, source_target_pairs={{0,1},{1,2},{2,3},{3,4},{4,5},{5,6},{6,7},{7,0},{8,9},{9,10},{10,1... | collective-permute-start | bytes 589832 | tf_op jit(solution)/shard_map/ppermute | solution.py:30
  90.0 7.7 %collective-permute-start.15 = (f32[2,24,8,128]{3,2,1,0:T(8,128)S(1)}, f32[2,24,8,128]{3,2,1,0:T(8,128)S(1)}, u32[]{:S(2)}, u32[]{:S(2)}) collective-permute-start(f32[2,24,8,128]{3,2,1,0:T(8,128)S(1)} %get-tuple-element.159), channel_id=1, source_target_pairs={{0,7},{1,0},{2,1},{3,2},{4,3},{5,4},{6,5},{7,6},{8,15},{9,8},{10,9... | collective-permute-start | bytes 589832 | tf_op jit(solution)/shard_map/ppermute | solution.py:30
  99.8 12.3 %collective-permute-start.18 = (f32[24,32,128]{2,1,0:T(8,128)S(1)}, f32[24,32,128]{2,1,0:T(8,128)S(1)}, u32[]{:S(2)}, u32[]{:S(2)}) collective-permute-start(f32[24,32,128]{2,1,0:T(8,128)S(1)} %bitcast.20), channel_id=1, source_target_pairs={{0,8},{8,16},{16,24},{24,32},{32,40},{40,48},{48,56},{56,64},{64,7... | collective-permute-start | bytes 1179656 | tf_op jit(solution)/shard_map/ppermute | solution.py:30
  99.9 12.2 %collective-permute-start.19 = (f32[24,32,128]{2,1,0:T(8,128)S(1)}, f32[24,32,128]{2,1,0:T(8,128)S(1)}, u32[]{:S(2)}, u32[]{:S(2)}) collective-permute-start(f32[24,32,128]{2,1,0:T(8,128)S(1)} %bitcast.19), channel_id=1, source_target_pairs={{0,120},{8,0},{16,8},{24,16},{32,24},{40,32},{48,40},{56,48},{64,5... | collective-permute-start | bytes 1179656 | tf_op jit(solution)/shard_map/ppermute | solution.py:30
  105.0 10.1 %collective-permute-start.22 = (f32[3,16,8,128]{3,2,1,0:T(8,128)S(1)}, f32[3,16,8,128]{3,2,1,0:T(8,128)S(1)}, u32[]{:S(2)}, u32[]{:S(2)}) collective-permute-start(f32[3,16,8,128]{3,2,1,0:T(8,128)S(1)} %get-tuple-element.182), channel_id=1, source_target_pairs={{0,1},{1,2},{2,3},{3,4},{4,5},{5,6},{6,7},{7,0},{8,9},{9,10},{10,1... | collective-permute-start | bytes 589832 | tf_op jit(solution)/shard_map/ppermute | solution.py:30
  107.0 8.1 %collective-permute-start.23 = (f32[3,16,8,128]{3,2,1,0:T(8,128)S(1)}, f32[3,16,8,128]{3,2,1,0:T(8,128)S(1)}, u32[]{:S(2)}, u32[]{:S(2)}) collective-permute-start(f32[3,16,8,128]{3,2,1,0:T(8,128)S(1)} %get-tuple-element.183), channel_id=1, source_target_pairs={{0,7},{1,0},{2,1},{3,2},{4,3},{5,4},{6,5},{7,6},{8,15},{9,8},{10,9... | collective-permute-start | bytes 589832 | tf_op jit(solution)/shard_map/ppermute | solution.py:30
  112.1 10.7 %collective-permute-start.20 = (f32[2,24,8,128]{3,2,1,0:T(8,128)S(1)}, f32[2,24,8,128]{3,2,1,0:T(8,128)S(1)}, u32[]{:S(2)}, u32[]{:S(2)}) collective-permute-start(f32[2,24,8,128]{3,2,1,0:T(8,128)S(1)} %get-tuple-element.179), channel_id=1, source_target_pairs={{0,1},{1,2},{2,3},{3,4},{4,5},{5,6},{6,7},{7,0},{8,9},{9,10},{10,1... | collective-permute-start | bytes 589832 | tf_op jit(solution)/shard_map/ppermute | solution.py:30
  115.1 7.7 %collective-permute-start.21 = (f32[2,24,8,128]{3,2,1,0:T(8,128)S(1)}, f32[2,24,8,128]{3,2,1,0:T(8,128)S(1)}, u32[]{:S(2)}, u32[]{:S(2)}) collective-permute-start(f32[2,24,8,128]{3,2,1,0:T(8,128)S(1)} %get-tuple-element.180), channel_id=1, source_target_pairs={{0,7},{1,0},{2,1},{3,2},{4,3},{5,4},{6,5},{7,6},{8,15},{9,8},{10,9... | collective-permute-start | bytes 589832 | tf_op jit(solution)/shard_map/ppermute | solution.py:30

commit v4 on v3

--- a/solution.py
+++ b/solution.py
@@ -15,6 +15,7 @@
 SM = pl.BlockSpec(memory_space=pltpu.SMEM)
 HB = pl.BlockSpec(memory_space=pltpu.HBM)
 CP = pltpu.CompilerParams(vmem_limit_bytes=12 << 20)
+BW = 128
 YR = 56
 
 XPARTS = ((0, 3, 8), (1, 3, 4), (2, 1, 6), (3, 1, 6), (4, 1, 4))
@@ -196,7 +197,7 @@
         ys = pl.ds(y, n)
         for k, fs in enumerate(fr):
             i = j0 + 8 * part + k
-            r = pl.multiple_of(i * 32 + y - 8, 8)
+            r = i * 32 + y - 8
             hist[pl.ds(r, n)] = surface(fs, 3, hs[i, pl.ds(y - 4, n)])
             for c in range(3):
                 now = u1[c, i + 4, ys]
@@ -209,13 +210,13 @@
 def two_steps(prev, lam, mu, q, ue, s, s2, hs, u1, top, bot, hist, mz):
     mz[...] = z_matrix()
     none = lambda i0: ()
-    every = lambda i0: range(4)
-    for_x(7, lambda i: stress_rows(ue, 0, s, 2, lam, mu, mz, [(4 * i + 2, 2)], 4, 48))
-    for_x(2, lambda i: first_rows(ue, prev, q, s, hs, mz, u1, [(20 * i, 4)], 4, 48, none))
-    for_x(4, lambda i: first_rows(ue, prev, q, s, hs, mz, u1, [(4 * i + 4, 4)], 4, 48, every))
-    for_x(5, lambda i: stress_rows(u1, 4, s2, 6, lam, mu, mz, [(4 * i + 6, 6)], 4, 48))
+    every = lambda i0: range(8)
+    for_x(2, lambda i: stress_rows(ue, 0, s, 2, lam, mu, mz, [(14 * i + 2, 2)], 14, 48))
+    first_rows(ue, prev, q, s, hs, mz, u1, [(0, 4), (20, 4)], 4, 48, none)
+    for_x(2, lambda i: first_rows(ue, prev, q, s, hs, mz, u1, [(8 * i + 4, 4)], 8, 48, every))
+    for_x(2, lambda i: stress_rows(u1, 4, s2, 6, lam, mu, mz, [(10 * i + 6, 6)], 10, 48))
     for part, out in enumerate((top, bot)):
-        for_x(2, lambda i: second_rows(ue, q, s2, hs, mz, u1, hist, [(out, 4 * i, part, 8, None)], 4, 32))
+        second_rows(ue, q, s2, hs, mz, u1, hist, [(out, 0, part, 8, None)], 8, 32)
 
 
 def patch_two_steps(prev, lam, mu, q, ue, s, s2, hs, u1, top, bot, hist, right, left, mz):
@@ -333,22 +334,6 @@
     ue, s, s2, hs, u1, top, bot, hist, right, left, mz = refs[15:]
     fill_corners(flags, wc, ec, ue)
     patch_two_steps(prev, lam, mu, q, ue, s, s2, hs, u1, top, bot, hist, right, left, mz)
-
-
-def last_patch_kernel(*refs):
-    flags, wc, ec, prev, lam, mu, q = refs[:7]
-    ue, s, s2, hs, u1, top, bot, hist, now, before, right, left, mz = refs[15:]
-    fill_corners(flags, wc, ec, ue)
-    patch_two_steps(prev, lam, mu, q, ue, s, s2, hs, u1, top, bot, hist, right, left, mz)
-    for c in range(3):
-
-        def rows(i, c=c):
-            now[c, i] = top[c, i]
-            now[c, 8 + i] = bot[c, i]
-            before[c, i] = u1[c, i + 4, 8:40]
-            before[c, 8 + i] = u1[c, i + 12, 8:40]
-
-        for_x(8, rows)
 
 
 def request_kernel(tile, cell, req, key, kmod, a_ref, bhi, blo):
@@ -400,7 +385,10 @@
     return acc
 
 
-def early_answer_kernel(hot, h0, h1, h2, out):
+def early_answer_kernel(hot, h0, h1, h2, key, out, hots):
+    row512 = lax.broadcasted_iota(jnp.int32, (512, 128), 0).astype(F32)
+    for j in range(8):
+        hots[:, 128 * j : 128 * j + 128] = jnp.where(row512 == key[j : j + 1, :], 1.0, 0.0).astype(BF16)
     h = h0[...] + pltpu.roll(h1[...], 6, 1) + pltpu.roll(h2[...], 12, 1)
     out[...] = pick(h, hot)
 
@@ -409,73 +397,101 @@
     out[...] = (early[...] + pick(pltpu.roll(h3[...], 18, 1), hot)).reshape(128, 4, 128)
 
 
-def building_start_kernel(d_in, v_in, hf, br, st, ms, yd, cnt, disp, vel, hyst, stiff, yld, gain):
-    level = lax.broadcasted_iota(jnp.int32, (64, 128), 0)
-    mask = jnp.where(level < cnt[0], 1.0, 0.0)
-    y = yd[...] * mask
-    stiff[...] = st[...] * mask
-    yld[...] = y
-    gain[...] = DT / ms[...]
-    for c in range(3):
-        disp[c] = d_in[c] * mask
-        vel[c] = v_in[c] * mask
-        flag = br[c]
-        hyst[c] = jnp.where(flag == 1, y, jnp.where(flag == 2, -y, hf[c] * y))
-
-
-def building_kernel(ret, key, kmod, cnt, d_in, v_in, h_in, st, yd, gn, d_out, v_out, h_out, ground, bufs, sem):
-    pieces = split3(ret[...].reshape(512, 128).T)[:2]
-    row512 = lax.broadcasted_iota(jnp.int32, (512, 128), 0).astype(F32)
+def building_start_kernel(d_in, v_in, hf, br, st, ms, yd, cnt, disp, vel, hyst, weak, stiff, yld, gain):
+    low = lax.broadcasted_iota(jnp.int32, (8, 128), 0) * 8
+    for v in range(8):
+        src = pl.ds(v, 8, stride=8)
+        dst = pl.ds(8 * v, 8)
+        mask = jnp.where(low + v < cnt[0], 1.0, 0.0)
+        y = yd[src] * mask
+        k = st[src] * mask
+        weak[dst] = POST * k
+        stiff[dst] = (1.0 - POST) * k
+        yld[dst] = y
+        gain[dst] = DT * DT / ms[src]
+        for c in range(3):
+            disp[c, dst] = d_in[c, src] * mask
+            vel[c, dst] = v_in[c, src] * (DT * mask)
+            flag = br[c, src]
+            hyst[c, dst] = jnp.where(flag == 1, y, jnp.where(flag == 2, -y, hf[c, src] * y))
+
+
+def building_kernel(*refs):
+    top, bot, u1, ret, hots, kmod, cnt, d_in, v_in, h_in, wk, st, yd, gn = refs[:14]
+    now, before, d_out, v_out, h_out, ground, bufs, sem, field_sem = refs[14:]
+    copies = []
+    for n, (src, dst) in enumerate(
+        (
+            (top, now.at[pl.ds(0, 3), pl.ds(0, 8)]),
+            (bot, now.at[pl.ds(0, 3), pl.ds(8, 8)]),
+            (u1.at[pl.ds(0, 3), pl.ds(4, 16), pl.ds(8, 32)], before),
+        )
+    ):
+        cp = pltpu.make_async_copy(src, dst, field_sem.at[n])
+        cp.start()
+        copies.append(cp)
+    turned = ret[...].reshape(512, 128).T
+    high = turned.astype(BF16)
+    low = (turned - high.astype(F32)).astype(BF16)
+    both = jnp.dot(jnp.concatenate([high, low], axis=0), hots[...], preferred_element_type=F32)
+    gathered = both[:128] + both[128:]
     for j in range(8):
-        lanes = pl.ds(128 * j, 128)
-        hot = jnp.where(row512 == key[j : j + 1, :], 1.0, 0.0).astype(BF16)
-        g = jnp.dot(pieces[0], hot, preferred_element_type=F32)
-        g = g + jnp.dot(pieces[1], hot, preferred_element_type=F32)
+        g = gathered[:, 128 * j : 128 * j + 128]
         km = kmod[j : j + 1, :]
         acc = jnp.zeros((32, 128), F32)
         for k in range(4):
             acc = acc + jnp.where(km == k, g[32 * k : 32 * k + 32], 0.0)
-        ground[:, lanes] = acc * (1.0 / DT)
+        ground[:, 128 * j : 128 * j + 128] = acc
     outs = (d_out, v_out, h_out)
-    copies = []
+    eight = range(8)
     for c in range(3):
 
-        def chunk(j, carry, c=c):
-            lanes = pl.ds(pl.multiple_of(j * 128, 128), 128)
-            level = lax.broadcasted_iota(jnp.int32, (64, 128), 0)
-            first_row = level == 0
-            last_row = level == 63
-            mask = jnp.where(level < cnt[0:1, lanes], 1.0, 0.0)
+        def chunk(j, c=c):
+            lanes = pl.ds(pl.multiple_of(j * BW, BW), BW)
+            row = lax.broadcasted_iota(jnp.int32, (8, BW), 0)
+            first_row = row == 0
+            last_row = row == 7
+            count = cnt[0:1, lanes]
+            part = [pl.ds(8 * v, 8) for v in eight]
 
             def drift_of(x):
-                return x - jnp.where(first_row, 0.0, pltpu.roll(x, 1, 0))
-
-            stiff = st[:, lanes]
-            yld = yd[:, lanes]
-            gain = gn[:, lanes]
-            disp = d_in[c, :, lanes]
-            vel = v_in[c, :, lanes]
-            hyst = h_in[c, :, lanes]
+                below = jnp.where(first_row, 0.0, pltpu.roll(x[7], 1, 0))
+                return [x[0] - below] + [x[v] - x[v - 1] for v in range(1, 8)]
+
+            mask = [jnp.where(row * 8 + v < count, 1.0, 0.0) for v in eight]
+            disp = [d_in[c, part[v], lanes] for v in eight]
+            vel = [v_in[c, part[v], lanes] for v in eight]
+            hyst = [h_in[c, part[v], lanes] for v in eight]
             drift = drift_of(disp)
             for t in range(STEPS):
-                spring = stiff * (POST * drift + (1.0 - POST) * hyst)
-                above = jnp.where(last_row, 0.0, pltpu.roll(spring, 63, 0))
-                row = ground[3 * t + c : 3 * t + c + 1, lanes]
-                vel = vel * (1.0 - DT * DAMP) + (gain * (above - spring) - mask * row)
-                disp = disp + DT * vel
+                spring = [wk[part[v], lanes] * drift[v] + st[part[v], lanes] * hyst[v] for v in eight]
+                above = spring[1:] + [jnp.where(last_row, 0.0, pltpu.roll(spring[0], 7, 0))]
+                quake = ground[3 * t + c : 3 * t + c + 1, lanes]
+                for v in eight:
+                    push = gn[part[v], lanes] * (above[v] - spring[v]) - mask[v] * quake
+                    vel[v] = vel[v] * (1.0 - DT * DAMP) + push
+                    disp[v] = disp[v] + vel[v]
                 new = drift_of(disp)
-                hyst = jnp.minimum(jnp.maximum(hyst + new - drift, -yld), yld)
+                for v in eight:
+                    y = yd[part[v], lanes]
+                    hyst[v] = jnp.minimum(jnp.maximum(hyst[v] + (new[v] - drift[v]), -y), y)
                 drift = new
-            bufs[0, c, :, lanes] = disp
-            bufs[1, c, :, lanes] = vel
-            bufs[2, c, :, lanes] = hyst
-            return carry
-
-        lax.fori_loop(0, 8, chunk, 0)
+            for v in eight:
+                dst = pl.ds(v, 8, stride=8)
+                speed = vel[v] * (1.0 / DT)
+                for h in range(BW // 128):
+                    cut = slice(128 * h, 128 * h + 128)
+                    bufs[0, c, j * (BW // 128) + h, dst] = disp[v][:, cut]
+                    bufs[1, c, j * (BW // 128) + h, dst] = speed[:, cut]
+                    bufs[2, c, j * (BW // 128) + h, dst] = hyst[v][:, cut]
+
+        for_x(1024 // BW, chunk)
         for n in range(3):
-            cp = pltpu.make_async_copy(bufs.at[n, c], outs[n].at[c], sem.at[3 * c + n])
-            cp.start()
-            copies.append(cp)
+            for j in range(8):
+                dst = outs[n].at[c, pl.ds(0, 64), pl.ds(128 * j, 128)]
+                cp = pltpu.make_async_copy(bufs.at[n, c, j], dst, sem.at[24 * c + 8 * n + j])
+                cp.start()
+                copies.append(cp)
     for cp in copies:
         cp.wait()
 
@@ -486,10 +502,10 @@
     rows = pl.BlockSpec((1, 1, 128), lambda i: (i, 0, 0))
     return pl.pallas_call(
         building_start_kernel,
-        out_shape=[sds(3, 64, 1024)] * 3 + [sds(64, 1024)] * 3,
+        out_shape=[sds(3, 64, 1024)] * 3 + [sds(64, 1024)] * 4,
         grid=(8,),
         in_specs=[lanes3] * 4 + [lanes2] * 3 + [rows],
-        out_specs=[lanes3] * 3 + [lanes2] * 3,
+        out_specs=[lanes3] * 3 + [lanes2] * 4,
         compiler_params=CP,
         name="building_start",
     )(sd, sv, hf, br, st, ms, yd, cnt.reshape(8, 1, 128))
@@ -502,6 +518,11 @@
     ny = lax.axis_size("gy")
     edge = jnp.stack([ix > 0, ix < nx - 1, iy > 0, iy < ny - 1]).astype(F32).reshape(1, 4)
 
+    half = sds(3, 8, 32, 128)
+    side = sds(3, 16, 8, 128)
+    band = pltpu.VMEM((256, 128), BF16)
+    work = [sds(3, 32, YR, 128), sds(6, 28, YR, 128), sds(6, 20, YR, 128), sds(16, 48, 128), sds(3, 24, YR, 128), half, half, sds(512, 128)]
+    mats = [sds(3, 24, YR, 128), sds(28, YR, 128), sds(28, YR, 128), sds(24, YR, 128)]
     hbm = [pltpu.with_memory_space_constraint(x, pltpu.HBM) for x in (u, p, la, mu, de)]
     up, down, right, left = pl.pallas_call(
         pack_first_kernel,
@@ -520,7 +541,7 @@
         out_shape=[sds(128, 4, 128), sds(8, 128), sds(8, 128)],
         in_specs=[VM] * 2,
         out_specs=[VM] * 3,
-        scratch_shapes=[pltpu.VMEM((512, 1024), BF16), pltpu.VMEM((128, 1024), BF16), pltpu.VMEM((128, 1024), BF16)],
+        scratch_shapes=[pltpu.VMEM((512, 1024), BF16)] + [pltpu.VMEM((128, 1024), BF16)] * 2,
         compiler_params=CP,
         name="requests",
     )(tile.reshape(8, 128).astype(F32), cell.reshape(8, 128).astype(F32))
@@ -539,11 +560,6 @@
         )(north, south)
         return ring(right, "gy", 1), ring(left, "gy", -1)
 
-    half = sds(3, 8, 32, 128)
-    side = sds(3, 16, 8, 128)
-    band = pltpu.VMEM((256, 128), BF16)
-    work = [sds(3, 32, YR, 128), sds(6, 28, YR, 128), sds(6, 20, YR, 128), sds(16, 48, 128), sds(3, 24, YR, 128), half, half, sds(512, 128)]
-    mats = [sds(3, 24, YR, 128), sds(28, YR, 128), sds(28, YR, 128), sds(24, YR, 128)]
     wc, ec = corners(north, south)
     state = pl.pallas_call(
         first_round_kernel,
@@ -583,15 +599,15 @@
             )(incoming)
             north, south, hot, starts = lax.optimization_barrier((north, south, hot, starts))
         if r == 3:
-            early = pl.pallas_call(
+            early, hots = pl.pallas_call(
                 early_answer_kernel,
-                out_shape=sds(512, 128),
-                in_specs=[VM] * 4,
-                out_specs=VM,
+                out_shape=[sds(512, 128), jax.ShapeDtypeStruct((512, 1024), BF16)],
+                in_specs=[VM] * 5,
+                out_specs=[VM] * 2,
                 compiler_params=CP,
                 name="early_answers",
-            )(hot, *hists)
-            north, south, early = lax.optimization_barrier((north, south, early))
+            )(hot, *hists, key)
+            north, south, early, hots = lax.optimization_barrier((north, south, early, hots))
         wc, ec = corners(north, south)
         consts = (prev, lam, mu2, q)
         state = pl.pallas_call(
@@ -603,20 +619,18 @@
             compiler_params=CP,
             name="wave_round",
         )(edge, top, bot, north, south, west, east, *consts)
-        last = r == 3
         state = pl.pallas_call(
-            last_patch_kernel if last else patch_kernel,
-            out_shape=work + ([sds(3, 16, 32, 128)] * 2 if last else [side, side]),
+            patch_kernel,
+            out_shape=work + [side, side],
             in_specs=[SM] + [VM] * 14,
             out_specs=[VM] * 10,
             input_output_aliases={7 + n: n for n in range(8)},
-            scratch_shapes=([pltpu.VMEM((3, 16, 8, 128), F32)] * 2 if last else []) + [band],
+            scratch_shapes=[band],
             compiler_params=CP,
-            name="patch_last" if last else "patch_round",
+            name="patch_round",
         )(edge, wc, ec, *consts, *state)
         prev, top, bot, hist, right, left = state[4:10]
         hists.append(hist)
-    now, before = right, left
 
     answers = pl.pallas_call(
         answer_kernel,
@@ -627,19 +641,20 @@
         name="answers",
     )(hot, early, hists[3])
     returned = lax.all_to_all(answers, ("gx", "gy"), 0, 0, tiled=True)
-    disp, vel, hyst = pl.pallas_call(
+    now, before, disp, vel, hyst = pl.pallas_call(
         building_kernel,
-        out_shape=[sds(3, 64, 1024)] * 3,
-        in_specs=[VM] * 10,
-        out_specs=[HB] * 3,
+        out_shape=[sds(3, 16, 32, 128)] * 2 + [sds(3, 64, 1024)] * 3,
+        in_specs=[VM] * 14,
+        out_specs=[HB] * 5,
         scratch_shapes=[
             pltpu.VMEM((32, 1024), F32),
-            pltpu.VMEM((3, 3, 64, 1024), F32),
-            pltpu.SemaphoreType.DMA((9,)),
+            pltpu.VMEM((3, 3, 8, 64, 128), F32),
+            pltpu.SemaphoreType.DMA((72,)),
+            pltpu.SemaphoreType.DMA((3,)),
         ],
         compiler_params=CP,
         name="buildings",
-    )(returned, key, kmod, cnt.reshape(1, 1024), *starts)
+    )(top, bot, prev, returned, hots, kmod, cnt.reshape(1, 1024), *starts)
     return now, before, disp, vel, hyst
 
 

time: 154 us -> 147 us (0.955)
  Pallas kernels: 58.5 us -> 51.7 us
    pallas_call x3, Pallas kernels: 23.1 us -> 18.3 us  [local(): pl.pallas_call(round_kernel, out_shape=work, in_specs=[SM] + [VM] * 10, o...]
    pallas_call x1, Pallas kernels: 10.3 us -> 8.66 us  [local(): pl.pallas_call(first_round_kernel, out_shape=work + mats, in_specs=[SM] +...]
  transfers between devices with their start and end apart: 24 -> 24, of which waited for: 3 -> 3; matrix products, arithmetic and copies ran while one was open for 1% -> 1% of each run, Pallas kernels for 24% -> 22%
where the time goes in v4:
time: 147 us
  Pallas kernels  51.7 us (35%)
  starting transfers between devices  43.1 us (29%)
  blocking collectives  38.6 us (26%)
  waiting for transfers between devices  11.1 us (8%)
    ppermute x24, starting transfers between devices, ring(): return lax.ppermute(x, axis, [(i, (i + step) % n) for i in range(n)])  43.1 us
    all_to_all x1, blocking collectives, local(): returned = lax.all_to_all(answers, ('gx', 'gy'), 0, 0, tiled=True)  20.8 us
    pallas_call x3, Pallas kernels, local(): pl.pallas_call(round_kernel, out_shape=work, in_specs=[SM] + [VM] * 10, o...  18.3 us
    all_to_all x1, blocking collectives, local(): incoming = lax.all_to_all(req, ('gx', 'gy'), 0, 0, tiled=True)  17.8 us
    ppermute x24, waiting for transfers between devices, ring(): return lax.ppermute(x, axis, [(i, (i + step) % n) for i in range(n)])  11.1 us
    pallas_call x1, Pallas kernels, local(): pl.pallas_call(first_round_kernel, out_shape=work + mats, in_specs=[SM] +...  8.66 us
    pallas_call x3, Pallas kernels, local(): pl.pallas_call(patch_kernel, out_shape=work + [side, side], in_specs=[SM]...  6.8 us
    pallas_call x1, Pallas kernels, local(): pl.pallas_call(building_kernel, out_shape=[sds(3, 16, 32, 128)] * 2 + [sd...  6.12 us
  transfers between devices with their start and end apart: 24, of which 3 were waited for; matrix products, arithmetic and copies ran while one was open for 1% of the time, Pallas kernels for 22%

profile of v4, /device:TPU:1, one launch (start us, length us, event | category | flops | bytes accessed | tf_op | source)
XLA Modules:
  0.0 147.2 jit_solution(2201921857494889762)
XLA Ops:
  0.6 2.1 %pack_first.1 = (f32[52,32,128]{2,1,0:T(8,128)S(1)}, f32[52,32,128]{2,1,0:T(8,128)S(1)}, f32[144,8,128]{2,1,0:T(8,128)S(1)}, f32[144,8,128]{2,1,0:T(8,128)S(1)}) custom-call(f32[3,16,32,128]{3,2,1,0:T(8,128)} %u.3, f32[3,16,32,128]{3,2,1,0:T(8,128)} %p.3, f32[16,32,128]{2,1,0:T(8,128)} %la.3, f32[16,32,128]{2,1,0:T(8,128)} %mu.3, f32[16,32,128]{2,1,0:T(8,128)} %de.3), custom_call_target="tpu_custom_call" | custom-call | tf_op jit(solution)/shard_map/pack_first/pallas_call | solution.py:527
  2.8 2.5 %collective-permute-start = (f32[52,32,128]{2,1,0:T(8,128)S(1)}, f32[52,32,128]{2,1,0:T(8,128)S(1)}, u32[]{:S(2)}, u32[]{:S(2)}) collective-permute-start(f32[52,32,128]{2,1,0:T(8,128)S(1)} %get-tuple-element.109), channel_id=1, source_target_pairs={{0,8},{8,16},{16,24},{24,32},{32,40},{40,48},{48,56},{56,64},{64,7... | collective-permute-start | bytes 2555912 | tf_op jit(solution)/shard_map/ppermute | solution.py:31
  5.3 4.7 %collective-permute-start.1 = (f32[52,32,128]{2,1,0:T(8,128)S(1)}, f32[52,32,128]{2,1,0:T(8,128)S(1)}, u32[]{:S(2)}, u32[]{:S(2)}) collective-permute-start(f32[52,32,128]{2,1,0:T(8,128)S(1)} %get-tuple-element.110), channel_id=1, source_target_pairs={{0,120},{8,0},{16,8},{24,16},{32,24},{40,32},{48,40},{56,48},{64,5... | collective-permute-start | bytes 2555912 | tf_op jit(solution)/shard_map/ppermute | solution.py:31
  9.9 2.1 %collective-permute-start.2 = (f32[144,8,128]{2,1,0:T(8,128)S(1)}, f32[144,8,128]{2,1,0:T(8,128)S(1)}, u32[]{:S(2)}, u32[]{:S(2)}) collective-permute-start(f32[144,8,128]{2,1,0:T(8,128)S(1)} %get-tuple-element.111), channel_id=1, source_target_pairs={{0,1},{1,2},{2,3},{3,4},{4,5},{5,6},{6,7},{7,0},{8,9},{9,10},{10,1... | collective-permute-start | bytes 1769480 | tf_op jit(solution)/shard_map/ppermute | solution.py:31
  13.4 1.1 requests.1
  14.5 17.8 %all_to_all.10.inc = f32[128,4,128]{2,1,0:T(4,128)S(1)} all-to-all(f32[128,4,128]{2,1,0:T(4,128)S(1)} %get-tuple-element.113), channel_id=1, replica_groups=mesh['gx'=16,'gy'=8] {'gx','gy'}, dimensions={0} | all-to-all | bytes 524288 | tf_op jit(solution)/shard_map/all_to_all | solution.py:548
  32.3 1.0 pack_corner.4
  33.3 1.6 %collective-permute-start.4 = (f32[2,52,8,128]{3,2,1,0:T(8,128)}, f32[2,52,8,128]{3,2,1,0:T(8,128)}, u32[]{:S(2)}, u32[]{:S(2)}) collective-permute-start(f32[2,52,8,128]{3,2,1,0:T(8,128)} %get-tuple-element.116), channel_id=1, source_target_pairs={{0,1},{1,2},{2,3},{3,4},{4,5},{5,6},{6,7},{7,0},{8,9},{9,10},{10,1... | collective-permute-start | bytes 1277960 | tf_op jit(solution)/shard_map/ppermute | solution.py:31
  35.0 8.7 %wave_first.1 = (f32[3,32,56,128]{3,2,1,0:T(8,128)S(1)}, f32[6,28,56,128]{3,2,1,0:T(8,128)S(1)}, f32[6,20,56,128]{3,2,1,0:T(8,128)S(1)}, f32[16,48,128]{2,1,0:T(...) custom-call(f32[1,4]{1,0:T(1,128)S(1)} %add_convert_fusion.flags.ref, ...), custom_call_target="tpu_custom_call" | custom-call | tf_op jit(solution)/shard_map/wave_first/pallas_call | solution.py:564
  43.8 2.7 %patch_first.1 = (f32[3,32,56,128]{3,2,1,0:T(8,128)S(1)}, f32[6,28,56,128]{3,2,1,0:T(8,128)S(1)}, f32[6,20,56,128]{3,2,1,0:T(8,128)S(1)}, f32[16,48,128]{2,1,0:T...) custom-call(f32[1,4]{1,0:T(1,128)S(1)} %add_convert_fusion.flags.ref, ...), custom_call_target="tpu_custom_call", output_to_operand_aliasing={{0}: (3, {}), {1}: (4, {}), {2}: (5, {}), {3}: (6, {}), {4}... | custom-call | tf_op jit(solution)/shard_map/patch_first/pallas_call | solution.py:573
  47.2 4.5 %collective-permute-start.7 = (f32[24,32,128]{2,1,0:T(8,128)S(1)}, f32[24,32,128]{2,1,0:T(8,128)S(1)}, u32[]{:S(2)}, u32[]{:S(2)}) collective-permute-start(f32[24,32,128]{2,1,0:T(8,128)S(1)} %bitcast.15), channel_id=1, source_target_pairs={{0,120},{8,0},{16,8},{24,16},{32,24},{40,32},{48,40},{56,48},{64,5... | collective-permute-start | bytes 1179656 | tf_op jit(solution)/shard_map/ppermute | solution.py:31
  51.8 2.1 %building_start.1 = (f32[3,64,1024]{2,1,0:T(8,128)S(1)}, f32[3,64,1024]{2,1,0:T(8,128)S(1)}, f32[3,64,1024]{2,1,0:T(8,128)S(1)}, f32[64,1024]{1,0:T(8,128)S(1)},...) custom-call(f32[3,64,1024]{2,1,0:T(8,128)S(1)} %copy-done, f32[3,64,1024]{2,1,0:T(8,128)S(1)} %copy-done.1, ...), custom_call_target="tpu_custom_call" | custom-call | tf_op jit(solution)/shard_map/building_start/pallas_call | solution.py:503
  54.6 2.0 %collective-permute-start.10 = (f32[3,16,8,128]{3,2,1,0:T(8,128)S(1)}, f32[3,16,8,128]{3,2,1,0:T(8,128)S(1)}, u32[]{:S(2)}, u32[]{:S(2)}) collective-permute-start(f32[3,16,8,128]{3,2,1,0:T(8,128)S(1)} %get-tuple-element.150), channel_id=1, source_target_pairs={{0,1},{1,2},{2,3},{3,4},{4,5},{5,6},{6,7},{7,0},{8,9},{9,10},{10,1... | collective-permute-start | bytes 589832 | tf_op jit(solution)/shard_map/ppermute | solution.py:31
  56.6 2.5 %collective-permute-done.6.north = f32[24,32,128]{2,1,0:T(8,128)S(1)} collective-permute-done((f32[24,32,128]{2,1,0:T(8,128)S(1)}, f32[24,32,128]{2,1,0:T(8,128)S(1)}, u32[]{:S(2)}, u32[]{:S(2)}) %collective-permute-start.6) | collective-permute-done | bytes 393248 | tf_op jit(solution)/shard_map/ppermute | solution.py:31
  59.1 3.7 %collective-permute-start.8 = (f32[2,24,8,128]{3,2,1,0:T(8,128)S(1)}, f32[2,24,8,128]{3,2,1,0:T(8,128)S(1)}, u32[]{:S(2)}, u32[]{:S(2)}) collective-permute-start(f32[2,24,8,128]{3,2,1,0:T(8,128)S(1)} %get-tuple-element.144), channel_id=1, source_target_pairs={{0,1},{1,2},{2,3},{3,4},{4,5},{5,6},{6,7},{7,0},{8,9},{9,10},{10,1... | collective-permute-start | bytes 589832 | tf_op jit(solution)/shard_map/ppermute | solution.py:31
  62.9 6.1 %wave_round.3 = (f32[3,32,56,128]{3,2,1,0:T(8,128)S(1)}, f32[6,28,56,128]{3,2,1,0:T(8,128)S(1)}, f32[6,20,56,128]{3,2,1,0:T(8,128)S(1)}, f32[16,48,128]{2,1,0:T(...) custom-call(f32[1,4]{1,0:T(1,128)S(1)} %add_convert_fusion.flags.ref, ...), custom_call_target="tpu_custom_call" | custom-call | tf_op jit(solution)/shard_map/wave_round/pallas_call | solution.py:613
  69.0 2.0 %patch_round.3 = (f32[3,32,56,128]{3,2,1,0:T(8,128)S(1)}, f32[6,28,56,128]{3,2,1,0:T(8,128)S(1)}, f32[6,20,56,128]{3,2,1,0:T(8,128)S(1)}, f32[16,48,128]{2,1,0:T...) custom-call(f32[1,4]{1,0:T(1,128)S(1)} %add_convert_fusion.flags.ref, ...), custom_call_target="tpu_custom_call", output_to_operand_aliasing={{0}: (7, {}), {1}: (8, {}), {2}: (9, {}), {3}: (10, {}), {4... | custom-call | tf_op jit(solution)/shard_map/patch_round/pallas_call | solution.py:622
  71.1 5.1 %collective-permute-start.13 = (f32[24,32,128]{2,1,0:T(8,128)S(1)}, f32[24,32,128]{2,1,0:T(8,128)S(1)}, u32[]{:S(2)}, u32[]{:S(2)}) collective-permute-start(f32[24,32,128]{2,1,0:T(8,128)S(1)} %bitcast.17), channel_id=1, source_target_pairs={{0,120},{8,0},{16,8},{24,16},{32,24},{40,32},{48,40},{56,48},{64,5... | collective-permute-start | bytes 1179656 | tf_op jit(solution)/shard_map/ppermute | solution.py:31
  76.2 2.0 %collective-permute-start.16 = (f32[3,16,8,128]{3,2,1,0:T(8,128)S(1)}, f32[3,16,8,128]{3,2,1,0:T(8,128)S(1)}, u32[]{:S(2)}, u32[]{:S(2)}) collective-permute-start(f32[3,16,8,128]{3,2,1,0:T(8,128)S(1)} %get-tuple-element.165), channel_id=1, source_target_pairs={{0,1},{1,2},{2,3},{3,4},{4,5},{5,6},{6,7},{7,0},{8,9},{9,10},{10,1... | collective-permute-start | bytes 589832 | tf_op jit(solution)/shard_map/ppermute | solution.py:31
  78.2 5.6 %collective-permute-done.12.north = f32[24,32,128]{2,1,0:T(8,128)S(1)} collective-permute-done((f32[24,32,128]{2,1,0:T(8,128)S(1)}, f32[24,32,128]{2,1,0:T(8,128)S(1)}, u32[]{:S(2)}, u32[]{:S(2)}) %collective-permute-start.12) | collective-permute-done | bytes 393248 | tf_op jit(solution)/shard_map/ppermute | solution.py:31
  83.9 3.1 %collective-permute-start.14 = (f32[2,24,8,128]{3,2,1,0:T(8,128)S(1)}, f32[2,24,8,128]{3,2,1,0:T(8,128)S(1)}, u32[]{:S(2)}, u32[]{:S(2)}) collective-permute-start(f32[2,24,8,128]{3,2,1,0:T(8,128)S(1)} %get-tuple-element.162), channel_id=1, source_target_pairs={{0,1},{1,2},{2,3},{3,4},{4,5},{5,6},{6,7},{7,0},{8,9},{9,10},{10,1... | collective-permute-start | bytes 589832 | tf_op jit(solution)/shard_map/ppermute | solution.py:31
  87.0 6.1 %wave_round.4 = (f32[3,32,56,128]{3,2,1,0:T(8,128)S(1)}, f32[6,28,56,128]{3,2,1,0:T(8,128)S(1)}, f32[6,20,56,128]{3,2,1,0:T(8,128)S(1)}, f32[16,48,128]{2,1,0:T(...) custom-call(f32[1,4]{1,0:T(1,128)S(1)} %add_convert_fusion.flags.ref, ...), custom_call_target="tpu_custom_call" | custom-call | tf_op jit(solution)/shard_map/wave_round/pallas_call | solution.py:613
  93.2 2.0 %patch_round.4 = (f32[3,32,56,128]{3,2,1,0:T(8,128)S(1)}, f32[6,28,56,128]{3,2,1,0:T(8,128)S(1)}, f32[6,20,56,128]{3,2,1,0:T(8,128)S(1)}, f32[16,48,128]{2,1,0:T...) custom-call(f32[1,4]{1,0:T(1,128)S(1)} %add_convert_fusion.flags.ref, ...), custom_call_target="tpu_custom_call", output_to_operand_aliasing={{0}: (7, {}), {1}: (8, {}), {2}: (9, {}), {3}: (10, {}), {4... | custom-call | tf_op jit(solution)/shard_map/patch_round/pallas_call | solution.py:622
  95.3 5.1 %collective-permute-start.19 = (f32[24,32,128]{2,1,0:T(8,128)S(1)}, f32[24,32,128]{2,1,0:T(8,128)S(1)}, u32[]{:S(2)}, u32[]{:S(2)}) collective-permute-start(f32[24,32,128]{2,1,0:T(8,128)S(1)} %bitcast.19), channel_id=1, source_target_pairs={{0,120},{8,0},{16,8},{24,16},{32,24},{40,32},{48,40},{56,48},{64,5... | collective-permute-start | bytes 1179656 | tf_op jit(solution)/shard_map/ppermute | solution.py:31
  100.4 2.0 %collective-permute-start.22 = (f32[3,16,8,128]{3,2,1,0:T(8,128)S(1)}, f32[3,16,8,128]{3,2,1,0:T(8,128)S(1)}, u32[]{:S(2)}, u32[]{:S(2)}) collective-permute-start(f32[3,16,8,128]{3,2,1,0:T(8,128)S(1)} %get-tuple-element.189), channel_id=1, source_target_pairs={{0,1},{1,2},{2,3},{3,4},{4,5},{5,6},{6,7},{7,0},{8,9},{9,10},{10,1... | collective-permute-start | bytes 589832 | tf_op jit(solution)/shard_map/ppermute | solution.py:31
  102.9 1.2 early_answers.1
  104.1 3.0 %collective-permute-done.18.north = f32[24,32,128]{2,1,0:T(8,128)S(1)} collective-permute-done((f32[24,32,128]{2,1,0:T(8,128)S(1)}, f32[24,32,128]{2,1,0:T(8,128)S(1)}, u32[]{:S(2)}, u32[]{:S(2)}) %collective-permute-start.18) | collective-permute-done | bytes 393248 | tf_op jit(solution)/shard_map/ppermute | solution.py:31
  107.2 3.2 %collective-permute-start.20 = (f32[2,24,8,128]{3,2,1,0:T(8,128)S(1)}, f32[2,24,8,128]{3,2,1,0:T(8,128)S(1)}, u32[]{:S(2)}, u32[]{:S(2)}) collective-permute-start(f32[2,24,8,128]{3,2,1,0:T(8,128)S(1)} %get-tuple-element.186), channel_id=1, source_target_pairs={{0,1},{1,2},{2,3},{3,4},{4,5},{5,6},{6,7},{7,0},{8,9},{9,10},{10,1... | collective-permute-start | bytes 589832 | tf_op jit(solution)/shard_map/ppermute | solution.py:31
  110.4 6.1 %wave_round.5 = (f32[3,32,56,128]{3,2,1,0:T(8,128)S(1)}, f32[6,28,56,128]{3,2,1,0:T(8,128)S(1)}, f32[6,20,56,128]{3,2,1,0:T(8,128)S(1)}, f32[16,48,128]{2,1,0:T(...) custom-call(f32[1,4]{1,0:T(1,128)S(1)} %add_convert_fusion.flags.ref, ...), custom_call_target="tpu_custom_call" | custom-call | tf_op jit(solution)/shard_map/wave_round/pallas_call | solution.py:613
  116.5 2.7 %patch_round.5 = (f32[3,32,56,128]{3,2,1,0:T(8,128)S(1)}, f32[6,28,56,128]{3,2,1,0:T(8,128)S(1)}, f32[6,20,56,128]{3,2,1,0:T(8,128)S(1)}, f32[16,48,128]{2,1,0:T...) custom-call(f32[1,4]{1,0:T(1,128)S(1)} %add_convert_fusion.flags.ref, ...), custom_call_target="tpu_custom_call", output_to_operand_aliasing={{0}: (7, {}), {1}: (8, {}), {2}: (9, {}), {3}: (10, {}), {4... | custom-call | tf_op jit(solution)/shard_map/patch_round/pallas_call | solution.py:622
  120.1 20.8 %all_to_all.11.refs_3_ = f32[128,4,128]{2,1,0:T(4,128)S(1)} all-to-all(f32[128,4,128]{2,1,0:T(4,128)S(1)} %answers.1), channel_id=1, replica_groups=mesh['gx'=16,'gy'=8] {'gx','gy'}, dimensions={0} | all-to-all | bytes 524288 | tf_op jit(solution)/shard_map/all_to_all | solution.py:643
  140.9 6.1 %buildings.1 = (f32[3,16,32,128]{3,2,1,0:T(8,128)}, f32[3,16,32,128]{3,2,1,0:T(8,128)}, f32[3,64,1024]{2,1,0:T(8,128)}, f32[3,64,1024]{2,1,0:T(8,128)}, f32[3,64,1024]{2,1,0:T(8,128)}) custom-call(f32[3,8,32,128]{3,2,1,0:T(8,128)S(1)} %get-tuple-element.199.refs_0_, f32[3,8,32,128]{3,2,1,0:T(8,128)S(1)} %get-tuple-element.200.refs_1_, ...), custom_call_target="tpu_custom_call" | custom-call | tf_op jit(solution)/shard_map/buildings/pallas_call | solution.py:644
  (56 shorter events, 4.5 us)
Async XLA Ops:
  2.8 29.6 %collective-permute-start = (f32[52,32,128]{2,1,0:T(8,128)S(1)}, f32[52,32,128]{2,1,0:T(8,128)S(1)}, u32[]{:S(2)}, u32[]{:S(2)}) collective-permute-start(f32[52,32,128]{2,1,0:T(8,128)S(1)} %get-tuple-element.109), channel_id=1, source_target_pairs={{0,8},{8,16},{16,24},{24,32},{32,40},{40,48},{48,56},{56,64},{64,7... | collective-permute-start | bytes 2555912 | tf_op jit(solution)/shard_map/ppermute | solution.py:31
  5.3 27.0 %collective-permute-start.1 = (f32[52,32,128]{2,1,0:T(8,128)S(1)}, f32[52,32,128]{2,1,0:T(8,128)S(1)}, u32[]{:S(2)}, u32[]{:S(2)}) collective-permute-start(f32[52,32,128]{2,1,0:T(8,128)S(1)} %get-tuple-element.110), channel_id=1, source_target_pairs={{0,120},{8,0},{16,8},{24,16},{32,24},{40,32},{48,40},{56,48},{64,5... | collective-permute-start | bytes 2555912 | tf_op jit(solution)/shard_map/ppermute | solution.py:31
  9.9 22.4 %collective-permute-start.2 = (f32[144,8,128]{2,1,0:T(8,128)S(1)}, f32[144,8,128]{2,1,0:T(8,128)S(1)}, u32[]{:S(2)}, u32[]{:S(2)}) collective-permute-start(f32[144,8,128]{2,1,0:T(8,128)S(1)} %get-tuple-element.111), channel_id=1, source_target_pairs={{0,1},{1,2},{2,3},{3,4},{4,5},{5,6},{6,7},{7,0},{8,9},{9,10},{10,1... | collective-permute-start | bytes 1769480 | tf_op jit(solution)/shard_map/ppermute | solution.py:31
  12.0 20.3 %collective-permute-start.3 = (f32[144,8,128]{2,1,0:T(8,128)S(1)}, f32[144,8,128]{2,1,0:T(8,128)S(1)}, u32[]{:S(2)}, u32[]{:S(2)}) collective-permute-start(f32[144,8,128]{2,1,0:T(8,128)S(1)} %get-tuple-element.112), channel_id=1, source_target_pairs={{0,7},{1,0},{2,1},{3,2},{4,3},{5,4},{6,5},{7,6},{8,15},{9,8},{10,9... | collective-permute-start | bytes 1769480 | tf_op jit(solution)/shard_map/ppermute | solution.py:31
  33.3 10.3 %collective-permute-start.4 = (f32[2,52,8,128]{3,2,1,0:T(8,128)}, f32[2,52,8,128]{3,2,1,0:T(8,128)}, u32[]{:S(2)}, u32[]{:S(2)}) collective-permute-start(f32[2,52,8,128]{3,2,1,0:T(8,128)} %get-tuple-element.116), channel_id=1, source_target_pairs={{0,1},{1,2},{2,3},{3,4},{4,5},{5,6},{6,7},{7,0},{8,9},{9,10},{10,1... | collective-permute-start | bytes 1277960 | tf_op jit(solution)/shard_map/ppermute | solution.py:31
  34.9 8.8 %collective-permute-start.5 = (f32[2,52,8,128]{3,2,1,0:T(8,128)}, f32[2,52,8,128]{3,2,1,0:T(8,128)}, u32[]{:S(2)}, u32[]{:S(2)}) collective-permute-start(f32[2,52,8,128]{3,2,1,0:T(8,128)} %get-tuple-element.117), channel_id=1, source_target_pairs={{0,7},{1,0},{2,1},{3,2},{4,3},{5,4},{6,5},{7,6},{8,15},{9,8},{10,9... | collective-permute-start | bytes 1277960 | tf_op jit(solution)/shard_map/ppermute | solution.py:31
  43.7 8.1 %copy-start = (f32[3,64,1024]{2,1,0:T(8,128)S(1)}, f32[3,64,1024]{2,1,0:T(8,128)}, u32[]{:S(2)}) copy-start(f32[3,64,1024]{2,1,0:T(8,128)} %d_in.1) | copy-start | bytes 2359300
  43.7 8.1 %copy-start.1 = (f32[3,64,1024]{2,1,0:T(8,128)S(1)}, f32[3,64,1024]{2,1,0:T(8,128)}, u32[]{:S(2)}) copy-start(f32[3,64,1024]{2,1,0:T(8,128)} %v_in.1) | copy-start | bytes 2359300
  43.7 8.1 %copy-start.2 = (f32[3,64,1024]{2,1,0:T(8,128)S(1)}, f32[3,64,1024]{2,1,0:T(8,128)}, u32[]{:S(2)}) copy-start(f32[3,64,1024]{2,1,0:T(8,128)} %hf.1) | copy-start | bytes 2359300
  43.7 8.1 %copy-start.3 = (s32[3,64,1024]{2,1,0:T(8,128)S(1)}, s32[3,64,1024]{2,1,0:T(8,128)}, u32[]{:S(2)}) copy-start(s32[3,64,1024]{2,1,0:T(8,128)} %br.1) | copy-start | bytes 2359300
  43.7 8.1 %copy-start.4 = (f32[64,1024]{1,0:T(8,128)S(1)}, f32[64,1024]{1,0:T(8,128)}, u32[]{:S(2)}) copy-start(f32[64,1024]{1,0:T(8,128)} %st.1) | copy-start | bytes 786436
  43.7 8.1 %copy-start.5 = (f32[64,1024]{1,0:T(8,128)S(1)}, f32[64,1024]{1,0:T(8,128)}, u32[]{:S(2)}) copy-start(f32[64,1024]{1,0:T(8,128)} %ms.1) | copy-start | bytes 786436
  43.8 8.1 %copy-start.6 = (f32[64,1024]{1,0:T(8,128)S(1)}, f32[64,1024]{1,0:T(8,128)}, u32[]{:S(2)}) copy-start(f32[64,1024]{1,0:T(8,128)} %yd.1) | copy-start | bytes 786436
  43.8 8.1 %copy-start.7 = (s32[1024]{0:T(1024)S(1)}, s32[1024]{0:T(1024)}, u32[]{:S(2)}) copy-start(s32[1024]{0:T(1024)} %param.27) | copy-start | bytes 12292
  46.5 12.6 %collective-permute-start.6 = (f32[24,32,128]{2,1,0:T(8,128)S(1)}, f32[24,32,128]{2,1,0:T(8,128)S(1)}, u32[]{:S(2)}, u32[]{:S(2)}) collective-permute-start(f32[24,32,128]{2,1,0:T(8,128)S(1)} %bitcast.16), channel_id=1, source_target_pairs={{0,8},{8,16},{16,24},{24,32},{32,40},{40,48},{48,56},{56,64},{64,7... | collective-permute-start | bytes 1179656 | tf_op jit(solution)/shard_map/ppermute | solution.py:31
  47.2 11.8 %collective-permute-start.7 = (f32[24,32,128]{2,1,0:T(8,128)S(1)}, f32[24,32,128]{2,1,0:T(8,128)S(1)}, u32[]{:S(2)}, u32[]{:S(2)}) collective-permute-start(f32[24,32,128]{2,1,0:T(8,128)S(1)} %bitcast.15), channel_id=1, source_target_pairs={{0,120},{8,0},{16,8},{24,16},{32,24},{40,32},{48,40},{56,48},{64,5... | collective-permute-start | bytes 1179656 | tf_op jit(solution)/shard_map/ppermute | solution.py:31
  54.6 8.3 %collective-permute-start.10 = (f32[3,16,8,128]{3,2,1,0:T(8,128)S(1)}, f32[3,16,8,128]{3,2,1,0:T(8,128)S(1)}, u32[]{:S(2)}, u32[]{:S(2)}) collective-permute-start(f32[3,16,8,128]{3,2,1,0:T(8,128)S(1)} %get-tuple-element.150), channel_id=1, source_target_pairs={{0,1},{1,2},{2,3},{3,4},{4,5},{5,6},{6,7},{7,0},{8,9},{9,10},{10,1... | collective-permute-start | bytes 589832 | tf_op jit(solution)/shard_map/ppermute | solution.py:31
  56.6 6.2 %collective-permute-start.11 = (f32[3,16,8,128]{3,2,1,0:T(8,128)S(1)}, f32[3,16,8,128]{3,2,1,0:T(8,128)S(1)}, u32[]{:S(2)}, u32[]{:S(2)}) collective-permute-start(f32[3,16,8,128]{3,2,1,0:T(8,128)S(1)} %get-tuple-element.151), channel_id=1, source_target_pairs={{0,7},{1,0},{2,1},{3,2},{4,3},{5,4},{6,5},{7,6},{8,15},{9,8},{10,9... | collective-permute-start | bytes 589832 | tf_op jit(solution)/shard_map/ppermute | solution.py:31
  59.1 9.9 %collective-permute-start.8 = (f32[2,24,8,128]{3,2,1,0:T(8,128)S(1)}, f32[2,24,8,128]{3,2,1,0:T(8,128)S(1)}, u32[]{:S(2)}, u32[]{:S(2)}) collective-permute-start(f32[2,24,8,128]{3,2,1,0:T(8,128)S(1)} %get-tuple-element.144), channel_id=1, source_target_pairs={{0,1},{1,2},{2,3},{3,4},{4,5},{5,6},{6,7},{7,0},{8,9},{9,10},{10,1... | collective-permute-start | bytes 589832 | tf_op jit(solution)/shard_map/ppermute | solution.py:31
  62.8 6.1 %collective-permute-start.9 = (f32[2,24,8,128]{3,2,1,0:T(8,128)S(1)}, f32[2,24,8,128]{3,2,1,0:T(8,128)S(1)}, u32[]{:S(2)}, u32[]{:S(2)}) collective-permute-start(f32[2,24,8,128]{3,2,1,0:T(8,128)S(1)} %get-tuple-element.145), channel_id=1, source_target_pairs={{0,7},{1,0},{2,1},{3,2},{4,3},{5,4},{6,5},{7,6},{8,15},{9,8},{10,9... | collective-permute-start | bytes 589832 | tf_op jit(solution)/shard_map/ppermute | solution.py:31
  71.0 12.8 %collective-permute-start.12 = (f32[24,32,128]{2,1,0:T(8,128)S(1)}, f32[24,32,128]{2,1,0:T(8,128)S(1)}, u32[]{:S(2)}, u32[]{:S(2)}) collective-permute-start(f32[24,32,128]{2,1,0:T(8,128)S(1)} %bitcast.18), channel_id=1, source_target_pairs={{0,8},{8,16},{16,24},{24,32},{32,40},{40,48},{48,56},{56,64},{64,7... | collective-permute-start | bytes 1179656 | tf_op jit(solution)/shard_map/ppermute | solution.py:31
  71.1 12.7 %collective-permute-start.13 = (f32[24,32,128]{2,1,0:T(8,128)S(1)}, f32[24,32,128]{2,1,0:T(8,128)S(1)}, u32[]{:S(2)}, u32[]{:S(2)}) collective-permute-start(f32[24,32,128]{2,1,0:T(8,128)S(1)} %bitcast.17), channel_id=1, source_target_pairs={{0,120},{8,0},{16,8},{24,16},{32,24},{40,32},{48,40},{56,48},{64,5... | collective-permute-start | bytes 1179656 | tf_op jit(solution)/shard_map/ppermute | solution.py:31
  76.2 10.8 %collective-permute-start.16 = (f32[3,16,8,128]{3,2,1,0:T(8,128)S(1)}, f32[3,16,8,128]{3,2,1,0:T(8,128)S(1)}, u32[]{:S(2)}, u32[]{:S(2)}) collective-permute-start(f32[3,16,8,128]{3,2,1,0:T(8,128)S(1)} %get-tuple-element.165), channel_id=1, source_target_pairs={{0,1},{1,2},{2,3},{3,4},{4,5},{5,6},{6,7},{7,0},{8,9},{9,10},{10,1... | collective-permute-start | bytes 589832 | tf_op jit(solution)/shard_map/ppermute | solution.py:31
  78.2 8.8 %collective-permute-start.17 = (f32[3,16,8,128]{3,2,1,0:T(8,128)S(1)}, f32[3,16,8,128]{3,2,1,0:T(8,128)S(1)}, u32[]{:S(2)}, u32[]{:S(2)}) collective-permute-start(f32[3,16,8,128]{3,2,1,0:T(8,128)S(1)} %get-tuple-element.166), channel_id=1, source_target_pairs={{0,7},{1,0},{2,1},{3,2},{4,3},{5,4},{6,5},{7,6},{8,15},{9,8},{10,9... | collective-permute-start | bytes 589832 | tf_op jit(solution)/shard_map/ppermute | solution.py:31
  83.9 9.3 %collective-permute-start.14 = (f32[2,24,8,128]{3,2,1,0:T(8,128)S(1)}, f32[2,24,8,128]{3,2,1,0:T(8,128)S(1)}, u32[]{:S(2)}, u32[]{:S(2)}) collective-permute-start(f32[2,24,8,128]{3,2,1,0:T(8,128)S(1)} %get-tuple-element.162), channel_id=1, source_target_pairs={{0,1},{1,2},{2,3},{3,4},{4,5},{5,6},{6,7},{7,0},{8,9},{9,10},{10,1... | collective-permute-start | bytes 589832 | tf_op jit(solution)/shard_map/ppermute | solution.py:31
  87.0 6.1 %collective-permute-start.15 = (f32[2,24,8,128]{3,2,1,0:T(8,128)S(1)}, f32[2,24,8,128]{3,2,1,0:T(8,128)S(1)}, u32[]{:S(2)}, u32[]{:S(2)}) collective-permute-start(f32[2,24,8,128]{3,2,1,0:T(8,128)S(1)} %get-tuple-element.163), channel_id=1, source_target_pairs={{0,7},{1,0},{2,1},{3,2},{4,3},{5,4},{6,5},{7,6},{8,15},{9,8},{10,9... | collective-permute-start | bytes 589832 | tf_op jit(solution)/shard_map/ppermute | solution.py:31
  95.2 12.0 %collective-permute-start.18 = (f32[24,32,128]{2,1,0:T(8,128)S(1)}, f32[24,32,128]{2,1,0:T(8,128)S(1)}, u32[]{:S(2)}, u32[]{:S(2)}) collective-permute-start(f32[24,32,128]{2,1,0:T(8,128)S(1)} %bitcast.20), channel_id=1, source_target_pairs={{0,8},{8,16},{16,24},{24,32},{32,40},{40,48},{48,56},{56,64},{64,7... | collective-permute-start | bytes 1179656 | tf_op jit(solution)/shard_map/ppermute | solution.py:31
  95.3 11.9 %collective-permute-start.19 = (f32[24,32,128]{2,1,0:T(8,128)S(1)}, f32[24,32,128]{2,1,0:T(8,128)S(1)}, u32[]{:S(2)}, u32[]{:S(2)}) collective-permute-start(f32[24,32,128]{2,1,0:T(8,128)S(1)} %bitcast.19), channel_id=1, source_target_pairs={{0,120},{8,0},{16,8},{24,16},{32,24},{40,32},{48,40},{56,48},{64,5... | collective-permute-start | bytes 1179656 | tf_op jit(solution)/shard_map/ppermute | solution.py:31
  100.4 9.9 %collective-permute-start.22 = (f32[3,16,8,128]{3,2,1,0:T(8,128)S(1)}, f32[3,16,8,128]{3,2,1,0:T(8,128)S(1)}, u32[]{:S(2)}, u32[]{:S(2)}) collective-permute-start(f32[3,16,8,128]{3,2,1,0:T(8,128)S(1)} %get-tuple-element.189), channel_id=1, source_target_pairs={{0,1},{1,2},{2,3},{3,4},{4,5},{5,6},{6,7},{7,0},{8,9},{9,10},{10,1... | collective-permute-start | bytes 589832 | tf_op jit(solution)/shard_map/ppermute | solution.py:31
  102.4 7.9 %collective-permute-start.23 = (f32[3,16,8,128]{3,2,1,0:T(8,128)S(1)}, f32[3,16,8,128]{3,2,1,0:T(8,128)S(1)}, u32[]{:S(2)}, u32[]{:S(2)}) collective-permute-start(f32[3,16,8,128]{3,2,1,0:T(8,128)S(1)} %get-tuple-element.190), channel_id=1, source_target_pairs={{0,7},{1,0},{2,1},{3,2},{4,3},{5,4},{6,5},{7,6},{8,15},{9,8},{10,9... | collective-permute-start | bytes 589832 | tf_op jit(solution)/shard_map/ppermute | solution.py:31
  107.2 9.3 %collective-permute-start.20 = (f32[2,24,8,128]{3,2,1,0:T(8,128)S(1)}, f32[2,24,8,128]{3,2,1,0:T(8,128)S(1)}, u32[]{:S(2)}, u32[]{:S(2)}) collective-permute-start(f32[2,24,8,128]{3,2,1,0:T(8,128)S(1)} %get-tuple-element.186), channel_id=1, source_target_pairs={{0,1},{1,2},{2,3},{3,4},{4,5},{5,6},{6,7},{7,0},{8,9},{9,10},{10,1... | collective-permute-start | bytes 589832 | tf_op jit(solution)/shard_map/ppermute | solution.py:31
  110.4 6.1 %collective-permute-start.21 = (f32[2,24,8,128]{3,2,1,0:T(8,128)S(1)}, f32[2,24,8,128]{3,2,1,0:T(8,128)S(1)}, u32[]{:S(2)}, u32[]{:S(2)}) collective-permute-start(f32[2,24,8,128]{3,2,1,0:T(8,128)S(1)} %get-tuple-element.187), channel_id=1, source_target_pairs={{0,7},{1,0},{2,1},{3,2},{4,3},{5,4},{6,5},{7,6},{8,15},{9,8},{10,9... | collective-permute-start | bytes 589832 | tf_op jit(solution)/shard_map/ppermute | solution.py:31

commit v5 on v4

--- a/solution.py
+++ b/solution.py
@@ -243,34 +243,21 @@
             cp = pltpu.make_async_copy(arg, ref.at[pl.ds(w, 16), pl.ds(8, 32)], sem.at[len(copies)])
             cp.start()
             copies.append(cp)
-            none = jnp.zeros((8, 128), F32)
-            for i in range(w):
-                for x, strip, f in ((i, north, fn), (16 + w + i, south, fs)):
-                    ref[x, 0:8] = none
-                    ref[x, 8:40] = strip[off + i] * f
-                    ref[x, 40:48] = none
-
-            def mid(i, ref=ref, row=row, w=w):
-                ref[w + i, 0:8] = west[row + i] * fw
-                ref[w + i, 40:48] = east[row + i] * fe
-
-            for_x(16, mid)
+            none = jnp.zeros((w, 8, 128), F32)
+            for x, strip, f in ((0, north, fn), (16 + w, south, fs)):
+                ref[x : x + w, 0:8] = none
+                ref[x : x + w, 8:40] = strip[off : off + w] * f
+                ref[x : x + w, 40:48] = none
+            ref[w : w + 16, 0:8] = west[row : row + 16] * fw
+            ref[w : w + 16, 40:48] = east[row : row + 16] * fe
             off += w
             row += 16
-
     for cp in copies:
         cp.wait()
 
-    def scale(i):
-        lam[i, 0:48] = lam[i, 0:48] * (1.0 / 12.0)
-        muo[i, 0:48] = muo[i, 0:48] * (1.0 / 12.0)
-
-    for_x(28, scale)
-
-    def invert(i):
-        q[i, 0:48] = inverse_density(q[i, 0:48])
-
-    for_x(24, invert)
+    lam[:, 0:48] = lam[:, 0:48] * (1.0 / 12.0)
+    muo[:, 0:48] = muo[:, 0:48] * (1.0 / 12.0)
+    q[:, 0:48] = inverse_density(q[:, 0:48])
     two_steps(pe, lam, muo, q, ue, s, s2, hs, u1, top, bot, hist, mz)
 
 
@@ -287,46 +274,37 @@
     for a, comps, w in XPARTS:
         for c in range(comps):
             ref = exts[a].at[c] if comps == 3 else exts[a]
-            for i in range(w):
-                for half, x, f in ((0, i, fn), (1, 16 + w + i, fs)):
-                    for strip, y, g in ((wc, 0, fw), (ec, 40, fe)):
-                        v = strip[half, off + i] * (f * g)
-                        if a in (2, 3):
-                            v = v * (1.0 / 12.0)
-                        ref[x, y : y + 8] = inverse_density(v) if a == 4 else v
+            for half, x, f in ((0, 0, fn), (1, 16 + w, fs)):
+                for strip, y, g in ((wc, 0, fw), (ec, 40, fe)):
+                    v = strip[half, off : off + w] * (f * g)
+                    if a in (2, 3):
+                        v = v * (1.0 / 12.0)
+                    ref[x : x + w, y : y + 8] = inverse_density(v) if a == 4 else v
             off += w
     patch_two_steps(pe, lam, mu, q, ue, s, s2, hs, u1, top, bot, hist, right, left, mz)
 
 
 def round_kernel(flags, top, bot, north, south, west, east, prev, lam, mu, q, ue, s, s2, hs, u1, top2, bot2, hist, mz):
     fn, fs, fw, fe = [flags[0, k] for k in range(4)]
-    none = jnp.zeros((8, 128), F32)
+    none = jnp.zeros((8, 8, 128), F32)
     for c in range(3):
-
-        def rows(i, c=c):
-            for x, strip, f in ((i, north, fn), (24 + i, south, fs)):
-                ue[c, x, 0:8] = none
-                ue[c, x, 8:40] = strip[8 * c + i] * f
-                ue[c, x, 40:48] = none
-            for x, strip in ((i, top), (8 + i, bot)):
-                ue[c, 8 + x, 0:8] = west[c, x] * fw
-                ue[c, 8 + x, 8:40] = strip[c, i]
-                ue[c, 8 + x, 40:48] = east[c, x] * fe
-
-        for_x(8, rows)
+        for x, strip, f in ((0, north, fn), (24, south, fs)):
+            ue[c, x : x + 8, 0:8] = none
+            ue[c, x : x + 8, 8:40] = strip[8 * c : 8 * c + 8] * f
+            ue[c, x : x + 8, 40:48] = none
+        ue[c, 8:24, 0:8] = west[c] * fw
+        ue[c, 8:16, 8:40] = top[c]
+        ue[c, 16:24, 8:40] = bot[c]
+        ue[c, 8:24, 40:48] = east[c] * fe
     two_steps(prev, lam, mu, q, ue, s, s2, hs, u1, top2, bot2, hist, mz)
 
 
 def fill_corners(flags, wc, ec, ue):
     fn, fs, fw, fe = [flags[0, k] for k in range(4)]
     for c in range(3):
-
-        def rows(i, c=c):
-            for half, x, f in ((0, i, fn), (1, 24 + i, fs)):
-                ue[c, x, 0:8] = wc[half, 8 * c + i] * (f * fw)
-                ue[c, x, 40:48] = ec[half, 8 * c + i] * (f * fe)
-
-        for_x(8, rows)
+        for half, x, f in ((0, 0, fn), (1, 24, fs)):
+            ue[c, x : x + 8, 0:8] = wc[half, 8 * c : 8 * c + 8] * (f * fw)
+            ue[c, x : x + 8, 40:48] = ec[half, 8 * c : 8 * c + 8] * (f * fe)
 
 
 def patch_kernel(*refs):

time: 147 us -> 146 us (level)
  Pallas kernels: 51.7 us -> 50 us
  transfers between devices with their start and end apart: 24 -> 24, of which waited for: 3 -> 3; matrix products, arithmetic and copies ran while one was open for 1% -> 1% of each run, Pallas kernels for 22% -> 21%
where the time goes in v5:
time: 146 us; the launch traced here: 145 us
  Pallas kernels  50 us (34%)
  starting transfers between devices  44 us (30%)
  blocking collectives  37.8 us (26%)
  waiting for transfers between devices  11.1 us (8%)
  other arithmetic  1.46 us (1%)
    ppermute x24, starting transfers between devices, ring(): return lax.ppermute(x, axis, [(i, (i + step) % n) for i in range(n)])  44 us
    all_to_all x1, blocking collectives, local(): returned = lax.all_to_all(answers, ('gx', 'gy'), 0, 0, tiled=True)  19.9 us
    pallas_call x3, Pallas kernels, local(): pl.pallas_call(round_kernel, out_shape=work, in_specs=[SM] + [VM] * 10, o...  18 us
    all_to_all x1, blocking collectives, local(): incoming = lax.all_to_all(req, ('gx', 'gy'), 0, 0, tiled=True)  17.8 us
    ppermute x24, waiting for transfers between devices, ring(): return lax.ppermute(x, axis, [(i, (i + step) % n) for i in range(n)])  11.1 us
    pallas_call x1, Pallas kernels, local(): pl.pallas_call(first_round_kernel, out_shape=work + mats, in_specs=[SM] +...  7.79 us
    pallas_call x3, Pallas kernels, local(): pl.pallas_call(patch_kernel, out_shape=work + [side, side], in_specs=[SM]...  6.33 us
    pallas_call x1, Pallas kernels, local(): pl.pallas_call(building_kernel, out_shape=[sds(3, 16, 32, 128)] * 2 + [sd...  6.12 us
  transfers between devices with their start and end apart: 24, of which 3 were waited for; matrix products, arithmetic and copies ran while one was open for 1% of the time, Pallas kernels for 21%

profile of v5, /device:TPU:1, one launch (start us, length us, event | category | flops | bytes accessed | tf_op | source)
XLA Modules:
  0.0 145.5 jit_solution(17576741363473588248)
XLA Ops:
  0.6 2.1 %pack_first.1 = (f32[52,32,128]{2,1,0:T(8,128)S(1)}, f32[52,32,128]{2,1,0:T(8,128)S(1)}, f32[144,8,128]{2,1,0:T(8,128)S(1)}, f32[144,8,128]{2,1,0:T(8,128)S(1)}) custom-call(f32[3,16,32,128]{3,2,1,0:T(8,128)} %u.3, f32[3,16,32,128]{3,2,1,0:T(8,128)} %p.3, f32[16,32,128]{2,1,0:T(8,128)} %la.3, f32[16,32,128]{2,1,0:T(8,128)} %mu.3, f32[16,32,128]{2,1,0:T(8,128)} %de.3), custom_call_target="tpu_custom_call" | custom-call | tf_op jit(solution)/shard_map/pack_first/pallas_call | solution.py:505
  2.8 2.5 %collective-permute-start = (f32[52,32,128]{2,1,0:T(8,128)S(1)}, f32[52,32,128]{2,1,0:T(8,128)S(1)}, u32[]{:S(2)}, u32[]{:S(2)}) collective-permute-start(f32[52,32,128]{2,1,0:T(8,128)S(1)} %get-tuple-element.109), channel_id=1, source_target_pairs={{0,8},{8,16},{16,24},{24,32},{32,40},{40,48},{48,56},{56,64},{64,7... | collective-permute-start | bytes 2555912 | tf_op jit(solution)/shard_map/ppermute | solution.py:31
  5.3 4.7 %collective-permute-start.1 = (f32[52,32,128]{2,1,0:T(8,128)S(1)}, f32[52,32,128]{2,1,0:T(8,128)S(1)}, u32[]{:S(2)}, u32[]{:S(2)}) collective-permute-start(f32[52,32,128]{2,1,0:T(8,128)S(1)} %get-tuple-element.110), channel_id=1, source_target_pairs={{0,120},{8,0},{16,8},{24,16},{32,24},{40,32},{48,40},{56,48},{64,5... | collective-permute-start | bytes 2555912 | tf_op jit(solution)/shard_map/ppermute | solution.py:31
  9.9 2.1 %collective-permute-start.2 = (f32[144,8,128]{2,1,0:T(8,128)S(1)}, f32[144,8,128]{2,1,0:T(8,128)S(1)}, u32[]{:S(2)}, u32[]{:S(2)}) collective-permute-start(f32[144,8,128]{2,1,0:T(8,128)S(1)} %get-tuple-element.111), channel_id=1, source_target_pairs={{0,1},{1,2},{2,3},{3,4},{4,5},{5,6},{6,7},{7,0},{8,9},{9,10},{10,1... | collective-permute-start | bytes 1769480 | tf_op jit(solution)/shard_map/ppermute | solution.py:31
  13.4 1.1 requests.1
  14.5 17.8 %all_to_all.10.inc = f32[128,4,128]{2,1,0:T(4,128)S(1)} all-to-all(f32[128,4,128]{2,1,0:T(4,128)S(1)} %get-tuple-element.113), channel_id=1, replica_groups=mesh['gx'=16,'gy'=8] {'gx','gy'}, dimensions={0} | all-to-all | bytes 524288 | tf_op jit(solution)/shard_map/all_to_all | solution.py:526
  32.3 1.0 pack_corner.4
  33.3 1.6 %collective-permute-start.4 = (f32[2,52,8,128]{3,2,1,0:T(8,128)}, f32[2,52,8,128]{3,2,1,0:T(8,128)}, u32[]{:S(2)}, u32[]{:S(2)}) collective-permute-start(f32[2,52,8,128]{3,2,1,0:T(8,128)} %get-tuple-element.116), channel_id=1, source_target_pairs={{0,1},{1,2},{2,3},{3,4},{4,5},{5,6},{6,7},{7,0},{8,9},{9,10},{10,1... | collective-permute-start | bytes 1277960 | tf_op jit(solution)/shard_map/ppermute | solution.py:31
  35.0 7.8 %wave_first.1 = (f32[3,32,56,128]{3,2,1,0:T(8,128)S(1)}, f32[6,28,56,128]{3,2,1,0:T(8,128)S(1)}, f32[6,20,56,128]{3,2,1,0:T(8,128)S(1)}, f32[16,48,128]{2,1,0:T(...) custom-call(f32[1,4]{1,0:T(1,128)S(1)} %add_convert_fusion.flags.ref, ...), custom_call_target="tpu_custom_call" | custom-call | tf_op jit(solution)/shard_map/wave_first/pallas_call | solution.py:542
  42.9 2.7 %patch_first.1 = (f32[3,32,56,128]{3,2,1,0:T(8,128)S(1)}, f32[6,28,56,128]{3,2,1,0:T(8,128)S(1)}, f32[6,20,56,128]{3,2,1,0:T(8,128)S(1)}, f32[16,48,128]{2,1,0:T...) custom-call(f32[1,4]{1,0:T(1,128)S(1)} %add_convert_fusion.flags.ref, ...), custom_call_target="tpu_custom_call", output_to_operand_aliasing={{0}: (3, {}), {1}: (4, {}), {2}: (5, {}), {3}: (6, {}), {4}... | custom-call | tf_op jit(solution)/shard_map/patch_first/pallas_call | solution.py:551
  46.4 4.5 %collective-permute-start.7 = (f32[24,32,128]{2,1,0:T(8,128)S(1)}, f32[24,32,128]{2,1,0:T(8,128)S(1)}, u32[]{:S(2)}, u32[]{:S(2)}) collective-permute-start(f32[24,32,128]{2,1,0:T(8,128)S(1)} %bitcast.15), channel_id=1, source_target_pairs={{0,120},{8,0},{16,8},{24,16},{32,24},{40,32},{48,40},{56,48},{64,5... | collective-permute-start | bytes 1179656 | tf_op jit(solution)/shard_map/ppermute | solution.py:31
  51.0 2.1 %building_start.1 = (f32[3,64,1024]{2,1,0:T(8,128)S(1)}, f32[3,64,1024]{2,1,0:T(8,128)S(1)}, f32[3,64,1024]{2,1,0:T(8,128)S(1)}, f32[64,1024]{1,0:T(8,128)S(1)},...) custom-call(f32[3,64,1024]{2,1,0:T(8,128)S(1)} %copy-done, f32[3,64,1024]{2,1,0:T(8,128)S(1)} %copy-done.1, ...), custom_call_target="tpu_custom_call" | custom-call | tf_op jit(solution)/shard_map/building_start/pallas_call | solution.py:481
  53.7 2.0 %collective-permute-start.10 = (f32[3,16,8,128]{3,2,1,0:T(8,128)S(1)}, f32[3,16,8,128]{3,2,1,0:T(8,128)S(1)}, u32[]{:S(2)}, u32[]{:S(2)}) collective-permute-start(f32[3,16,8,128]{3,2,1,0:T(8,128)S(1)} %get-tuple-element.150), channel_id=1, source_target_pairs={{0,1},{1,2},{2,3},{3,4},{4,5},{5,6},{6,7},{7,0},{8,9},{9,10},{10,1... | collective-permute-start | bytes 589832 | tf_op jit(solution)/shard_map/ppermute | solution.py:31
  55.7 2.5 %collective-permute-done.6.north = f32[24,32,128]{2,1,0:T(8,128)S(1)} collective-permute-done((f32[24,32,128]{2,1,0:T(8,128)S(1)}, f32[24,32,128]{2,1,0:T(8,128)S(1)}, u32[]{:S(2)}, u32[]{:S(2)}) %collective-permute-start.6) | collective-permute-done | bytes 393248 | tf_op jit(solution)/shard_map/ppermute | solution.py:31
  58.2 3.7 %collective-permute-start.8 = (f32[2,24,8,128]{3,2,1,0:T(8,128)S(1)}, f32[2,24,8,128]{3,2,1,0:T(8,128)S(1)}, u32[]{:S(2)}, u32[]{:S(2)}) collective-permute-start(f32[2,24,8,128]{3,2,1,0:T(8,128)S(1)} %get-tuple-element.144), channel_id=1, source_target_pairs={{0,1},{1,2},{2,3},{3,4},{4,5},{5,6},{6,7},{7,0},{8,9},{9,10},{10,1... | collective-permute-start | bytes 589832 | tf_op jit(solution)/shard_map/ppermute | solution.py:31
  62.0 6.0 %wave_round.3 = (f32[3,32,56,128]{3,2,1,0:T(8,128)S(1)}, f32[6,28,56,128]{3,2,1,0:T(8,128)S(1)}, f32[6,20,56,128]{3,2,1,0:T(8,128)S(1)}, f32[16,48,128]{2,1,0:T(...) custom-call(f32[1,4]{1,0:T(1,128)S(1)} %add_convert_fusion.flags.ref, ...), custom_call_target="tpu_custom_call" | custom-call | tf_op jit(solution)/shard_map/wave_round/pallas_call | solution.py:591
  68.0 1.9 %patch_round.3 = (f32[3,32,56,128]{3,2,1,0:T(8,128)S(1)}, f32[6,28,56,128]{3,2,1,0:T(8,128)S(1)}, f32[6,20,56,128]{3,2,1,0:T(8,128)S(1)}, f32[16,48,128]{2,1,0:T...) custom-call(f32[1,4]{1,0:T(1,128)S(1)} %add_convert_fusion.flags.ref, ...), custom_call_target="tpu_custom_call", output_to_operand_aliasing={{0}: (7, {}), {1}: (8, {}), {2}: (9, {}), {3}: (10, {}), {4... | custom-call | tf_op jit(solution)/shard_map/patch_round/pallas_call | solution.py:600
  70.0 5.1 %collective-permute-start.13 = (f32[24,32,128]{2,1,0:T(8,128)S(1)}, f32[24,32,128]{2,1,0:T(8,128)S(1)}, u32[]{:S(2)}, u32[]{:S(2)}) collective-permute-start(f32[24,32,128]{2,1,0:T(8,128)S(1)} %bitcast.17), channel_id=1, source_target_pairs={{0,120},{8,0},{16,8},{24,16},{32,24},{40,32},{48,40},{56,48},{64,5... | collective-permute-start | bytes 1179656 | tf_op jit(solution)/shard_map/ppermute | solution.py:31
  75.1 2.0 %collective-permute-start.16 = (f32[3,16,8,128]{3,2,1,0:T(8,128)S(1)}, f32[3,16,8,128]{3,2,1,0:T(8,128)S(1)}, u32[]{:S(2)}, u32[]{:S(2)}) collective-permute-start(f32[3,16,8,128]{3,2,1,0:T(8,128)S(1)} %get-tuple-element.165), channel_id=1, source_target_pairs={{0,1},{1,2},{2,3},{3,4},{4,5},{5,6},{6,7},{7,0},{8,9},{9,10},{10,1... | collective-permute-start | bytes 589832 | tf_op jit(solution)/shard_map/ppermute | solution.py:31
  77.1 5.6 %collective-permute-done.12.north = f32[24,32,128]{2,1,0:T(8,128)S(1)} collective-permute-done((f32[24,32,128]{2,1,0:T(8,128)S(1)}, f32[24,32,128]{2,1,0:T(8,128)S(1)}, u32[]{:S(2)}, u32[]{:S(2)}) %collective-permute-start.12) | collective-permute-done | bytes 393248 | tf_op jit(solution)/shard_map/ppermute | solution.py:31
  82.7 3.1 %collective-permute-start.14 = (f32[2,24,8,128]{3,2,1,0:T(8,128)S(1)}, f32[2,24,8,128]{3,2,1,0:T(8,128)S(1)}, u32[]{:S(2)}, u32[]{:S(2)}) collective-permute-start(f32[2,24,8,128]{3,2,1,0:T(8,128)S(1)} %get-tuple-element.162), channel_id=1, source_target_pairs={{0,1},{1,2},{2,3},{3,4},{4,5},{5,6},{6,7},{7,0},{8,9},{9,10},{10,1... | collective-permute-start | bytes 589832 | tf_op jit(solution)/shard_map/ppermute | solution.py:31
  85.9 6.0 %wave_round.4 = (f32[3,32,56,128]{3,2,1,0:T(8,128)S(1)}, f32[6,28,56,128]{3,2,1,0:T(8,128)S(1)}, f32[6,20,56,128]{3,2,1,0:T(8,128)S(1)}, f32[16,48,128]{2,1,0:T(...) custom-call(f32[1,4]{1,0:T(1,128)S(1)} %add_convert_fusion.flags.ref, ...), custom_call_target="tpu_custom_call" | custom-call | tf_op jit(solution)/shard_map/wave_round/pallas_call | solution.py:591
  91.9 1.9 %patch_round.4 = (f32[3,32,56,128]{3,2,1,0:T(8,128)S(1)}, f32[6,28,56,128]{3,2,1,0:T(8,128)S(1)}, f32[6,20,56,128]{3,2,1,0:T(8,128)S(1)}, f32[16,48,128]{2,1,0:T...) custom-call(f32[1,4]{1,0:T(1,128)S(1)} %add_convert_fusion.flags.ref, ...), custom_call_target="tpu_custom_call", output_to_operand_aliasing={{0}: (7, {}), {1}: (8, {}), {2}: (9, {}), {3}: (10, {}), {4... | custom-call | tf_op jit(solution)/shard_map/patch_round/pallas_call | solution.py:600
  93.8 5.1 %collective-permute-start.19 = (f32[24,32,128]{2,1,0:T(8,128)S(1)}, f32[24,32,128]{2,1,0:T(8,128)S(1)}, u32[]{:S(2)}, u32[]{:S(2)}) collective-permute-start(f32[24,32,128]{2,1,0:T(8,128)S(1)} %bitcast.19), channel_id=1, source_target_pairs={{0,120},{8,0},{16,8},{24,16},{32,24},{40,32},{48,40},{56,48},{64,5... | collective-permute-start | bytes 1179656 | tf_op jit(solution)/shard_map/ppermute | solution.py:31
  99.0 2.0 %collective-permute-start.22 = (f32[3,16,8,128]{3,2,1,0:T(8,128)S(1)}, f32[3,16,8,128]{3,2,1,0:T(8,128)S(1)}, u32[]{:S(2)}, u32[]{:S(2)}) collective-permute-start(f32[3,16,8,128]{3,2,1,0:T(8,128)S(1)} %get-tuple-element.189), channel_id=1, source_target_pairs={{0,1},{1,2},{2,3},{3,4},{4,5},{5,6},{6,7},{7,0},{8,9},{9,10},{10,1... | collective-permute-start | bytes 589832 | tf_op jit(solution)/shard_map/ppermute | solution.py:31
  101.5 1.2 early_answers.1
  102.7 3.0 %collective-permute-done.18.north = f32[24,32,128]{2,1,0:T(8,128)S(1)} collective-permute-done((f32[24,32,128]{2,1,0:T(8,128)S(1)}, f32[24,32,128]{2,1,0:T(8,128)S(1)}, u32[]{:S(2)}, u32[]{:S(2)}) %collective-permute-start.18) | collective-permute-done | bytes 393248 | tf_op jit(solution)/shard_map/ppermute | solution.py:31
  105.7 4.1 %collective-permute-start.20 = (f32[2,24,8,128]{3,2,1,0:T(8,128)S(1)}, f32[2,24,8,128]{3,2,1,0:T(8,128)S(1)}, u32[]{:S(2)}, u32[]{:S(2)}) collective-permute-start(f32[2,24,8,128]{3,2,1,0:T(8,128)S(1)} %get-tuple-element.186), channel_id=1, source_target_pairs={{0,1},{1,2},{2,3},{3,4},{4,5},{5,6},{6,7},{7,0},{8,9},{9,10},{10,1... | collective-permute-start | bytes 589832 | tf_op jit(solution)/shard_map/ppermute | solution.py:31
  109.8 6.0 %wave_round.5 = (f32[3,32,56,128]{3,2,1,0:T(8,128)S(1)}, f32[6,28,56,128]{3,2,1,0:T(8,128)S(1)}, f32[6,20,56,128]{3,2,1,0:T(8,128)S(1)}, f32[16,48,128]{2,1,0:T(...) custom-call(f32[1,4]{1,0:T(1,128)S(1)} %add_convert_fusion.flags.ref, ...), custom_call_target="tpu_custom_call" | custom-call | tf_op jit(solution)/shard_map/wave_round/pallas_call | solution.py:591
  115.8 2.6 %patch_round.5 = (f32[3,32,56,128]{3,2,1,0:T(8,128)S(1)}, f32[6,28,56,128]{3,2,1,0:T(8,128)S(1)}, f32[6,20,56,128]{3,2,1,0:T(8,128)S(1)}, f32[16,48,128]{2,1,0:T...) custom-call(f32[1,4]{1,0:T(1,128)S(1)} %add_convert_fusion.flags.ref, ...), custom_call_target="tpu_custom_call", output_to_operand_aliasing={{0}: (7, {}), {1}: (8, {}), {2}: (9, {}), {3}: (10, {}), {4... | custom-call | tf_op jit(solution)/shard_map/patch_round/pallas_call | solution.py:600
  119.2 19.9 %all_to_all.11.refs_3_ = f32[128,4,128]{2,1,0:T(4,128)S(1)} all-to-all(f32[128,4,128]{2,1,0:T(4,128)S(1)} %answers.1), channel_id=1, replica_groups=mesh['gx'=16,'gy'=8] {'gx','gy'}, dimensions={0} | all-to-all | bytes 524288 | tf_op jit(solution)/shard_map/all_to_all | solution.py:621
  139.2 6.1 %buildings.1 = (f32[3,16,32,128]{3,2,1,0:T(8,128)}, f32[3,16,32,128]{3,2,1,0:T(8,128)}, f32[3,64,1024]{2,1,0:T(8,128)}, f32[3,64,1024]{2,1,0:T(8,128)}, f32[3,64,1024]{2,1,0:T(8,128)}) custom-call(f32[3,8,32,128]{3,2,1,0:T(8,128)S(1)} %get-tuple-element.199.refs_0_, f32[3,8,32,128]{3,2,1,0:T(8,128)S(1)} %get-tuple-element.200.refs_1_, ...), custom_call_target="tpu_custom_call" | custom-call | tf_op jit(solution)/shard_map/buildings/pallas_call | solution.py:622
  (56 shorter events, 4.5 us)
Async XLA Ops:
  2.8 29.6 %collective-permute-start = (f32[52,32,128]{2,1,0:T(8,128)S(1)}, f32[52,32,128]{2,1,0:T(8,128)S(1)}, u32[]{:S(2)}, u32[]{:S(2)}) collective-permute-start(f32[52,32,128]{2,1,0:T(8,128)S(1)} %get-tuple-element.109), channel_id=1, source_target_pairs={{0,8},{8,16},{16,24},{24,32},{32,40},{40,48},{48,56},{56,64},{64,7... | collective-permute-start | bytes 2555912 | tf_op jit(solution)/shard_map/ppermute | solution.py:31
  5.3 27.0 %collective-permute-start.1 = (f32[52,32,128]{2,1,0:T(8,128)S(1)}, f32[52,32,128]{2,1,0:T(8,128)S(1)}, u32[]{:S(2)}, u32[]{:S(2)}) collective-permute-start(f32[52,32,128]{2,1,0:T(8,128)S(1)} %get-tuple-element.110), channel_id=1, source_target_pairs={{0,120},{8,0},{16,8},{24,16},{32,24},{40,32},{48,40},{56,48},{64,5... | collective-permute-start | bytes 2555912 | tf_op jit(solution)/shard_map/ppermute | solution.py:31
  9.9 22.4 %collective-permute-start.2 = (f32[144,8,128]{2,1,0:T(8,128)S(1)}, f32[144,8,128]{2,1,0:T(8,128)S(1)}, u32[]{:S(2)}, u32[]{:S(2)}) collective-permute-start(f32[144,8,128]{2,1,0:T(8,128)S(1)} %get-tuple-element.111), channel_id=1, source_target_pairs={{0,1},{1,2},{2,3},{3,4},{4,5},{5,6},{6,7},{7,0},{8,9},{9,10},{10,1... | collective-permute-start | bytes 1769480 | tf_op jit(solution)/shard_map/ppermute | solution.py:31
  12.0 20.3 %collective-permute-start.3 = (f32[144,8,128]{2,1,0:T(8,128)S(1)}, f32[144,8,128]{2,1,0:T(8,128)S(1)}, u32[]{:S(2)}, u32[]{:S(2)}) collective-permute-start(f32[144,8,128]{2,1,0:T(8,128)S(1)} %get-tuple-element.112), channel_id=1, source_target_pairs={{0,7},{1,0},{2,1},{3,2},{4,3},{5,4},{6,5},{7,6},{8,15},{9,8},{10,9... | collective-permute-start | bytes 1769480 | tf_op jit(solution)/shard_map/ppermute | solution.py:31
  33.3 9.5 %collective-permute-start.4 = (f32[2,52,8,128]{3,2,1,0:T(8,128)}, f32[2,52,8,128]{3,2,1,0:T(8,128)}, u32[]{:S(2)}, u32[]{:S(2)}) collective-permute-start(f32[2,52,8,128]{3,2,1,0:T(8,128)} %get-tuple-element.116), channel_id=1, source_target_pairs={{0,1},{1,2},{2,3},{3,4},{4,5},{5,6},{6,7},{7,0},{8,9},{9,10},{10,1... | collective-permute-start | bytes 1277960 | tf_op jit(solution)/shard_map/ppermute | solution.py:31
  34.9 7.9 %collective-permute-start.5 = (f32[2,52,8,128]{3,2,1,0:T(8,128)}, f32[2,52,8,128]{3,2,1,0:T(8,128)}, u32[]{:S(2)}, u32[]{:S(2)}) collective-permute-start(f32[2,52,8,128]{3,2,1,0:T(8,128)} %get-tuple-element.117), channel_id=1, source_target_pairs={{0,7},{1,0},{2,1},{3,2},{4,3},{5,4},{6,5},{7,6},{8,15},{9,8},{10,9... | collective-permute-start | bytes 1277960 | tf_op jit(solution)/shard_map/ppermute | solution.py:31
  42.8 8.1 %copy-start = (f32[3,64,1024]{2,1,0:T(8,128)S(1)}, f32[3,64,1024]{2,1,0:T(8,128)}, u32[]{:S(2)}) copy-start(f32[3,64,1024]{2,1,0:T(8,128)} %d_in.1) | copy-start | bytes 2359300
  42.8 8.1 %copy-start.1 = (f32[3,64,1024]{2,1,0:T(8,128)S(1)}, f32[3,64,1024]{2,1,0:T(8,128)}, u32[]{:S(2)}) copy-start(f32[3,64,1024]{2,1,0:T(8,128)} %v_in.1) | copy-start | bytes 2359300
  42.8 8.1 %copy-start.2 = (f32[3,64,1024]{2,1,0:T(8,128)S(1)}, f32[3,64,1024]{2,1,0:T(8,128)}, u32[]{:S(2)}) copy-start(f32[3,64,1024]{2,1,0:T(8,128)} %hf.1) | copy-start | bytes 2359300
  42.8 8.1 %copy-start.3 = (s32[3,64,1024]{2,1,0:T(8,128)S(1)}, s32[3,64,1024]{2,1,0:T(8,128)}, u32[]{:S(2)}) copy-start(s32[3,64,1024]{2,1,0:T(8,128)} %br.1) | copy-start | bytes 2359300
  42.9 8.1 %copy-start.4 = (f32[64,1024]{1,0:T(8,128)S(1)}, f32[64,1024]{1,0:T(8,128)}, u32[]{:S(2)}) copy-start(f32[64,1024]{1,0:T(8,128)} %st.1) | copy-start | bytes 786436
  42.9 8.1 %copy-start.5 = (f32[64,1024]{1,0:T(8,128)S(1)}, f32[64,1024]{1,0:T(8,128)}, u32[]{:S(2)}) copy-start(f32[64,1024]{1,0:T(8,128)} %ms.1) | copy-start | bytes 786436
  42.9 8.1 %copy-start.6 = (f32[64,1024]{1,0:T(8,128)S(1)}, f32[64,1024]{1,0:T(8,128)}, u32[]{:S(2)}) copy-start(f32[64,1024]{1,0:T(8,128)} %yd.1) | copy-start | bytes 786436
  42.9 8.1 %copy-start.7 = (s32[1024]{0:T(1024)S(1)}, s32[1024]{0:T(1024)}, u32[]{:S(2)}) copy-start(s32[1024]{0:T(1024)} %param.27) | copy-start | bytes 12292
  45.6 12.6 %collective-permute-start.6 = (f32[24,32,128]{2,1,0:T(8,128)S(1)}, f32[24,32,128]{2,1,0:T(8,128)S(1)}, u32[]{:S(2)}, u32[]{:S(2)}) collective-permute-start(f32[24,32,128]{2,1,0:T(8,128)S(1)} %bitcast.16), channel_id=1, source_target_pairs={{0,8},{8,16},{16,24},{24,32},{32,40},{40,48},{48,56},{56,64},{64,7... | collective-permute-start | bytes 1179656 | tf_op jit(solution)/shard_map/ppermute | solution.py:31
  46.4 11.8 %collective-permute-start.7 = (f32[24,32,128]{2,1,0:T(8,128)S(1)}, f32[24,32,128]{2,1,0:T(8,128)S(1)}, u32[]{:S(2)}, u32[]{:S(2)}) collective-permute-start(f32[24,32,128]{2,1,0:T(8,128)S(1)} %bitcast.15), channel_id=1, source_target_pairs={{0,120},{8,0},{16,8},{24,16},{32,24},{40,32},{48,40},{56,48},{64,5... | collective-permute-start | bytes 1179656 | tf_op jit(solution)/shard_map/ppermute | solution.py:31
  53.7 8.3 %collective-permute-start.10 = (f32[3,16,8,128]{3,2,1,0:T(8,128)S(1)}, f32[3,16,8,128]{3,2,1,0:T(8,128)S(1)}, u32[]{:S(2)}, u32[]{:S(2)}) collective-permute-start(f32[3,16,8,128]{3,2,1,0:T(8,128)S(1)} %get-tuple-element.150), channel_id=1, source_target_pairs={{0,1},{1,2},{2,3},{3,4},{4,5},{5,6},{6,7},{7,0},{8,9},{9,10},{10,1... | collective-permute-start | bytes 589832 | tf_op jit(solution)/shard_map/ppermute | solution.py:31
  55.7 6.3 %collective-permute-start.11 = (f32[3,16,8,128]{3,2,1,0:T(8,128)S(1)}, f32[3,16,8,128]{3,2,1,0:T(8,128)S(1)}, u32[]{:S(2)}, u32[]{:S(2)}) collective-permute-start(f32[3,16,8,128]{3,2,1,0:T(8,128)S(1)} %get-tuple-element.151), channel_id=1, source_target_pairs={{0,7},{1,0},{2,1},{3,2},{4,3},{5,4},{6,5},{7,6},{8,15},{9,8},{10,9... | collective-permute-start | bytes 589832 | tf_op jit(solution)/shard_map/ppermute | solution.py:31
  58.2 9.8 %collective-permute-start.8 = (f32[2,24,8,128]{3,2,1,0:T(8,128)S(1)}, f32[2,24,8,128]{3,2,1,0:T(8,128)S(1)}, u32[]{:S(2)}, u32[]{:S(2)}) collective-permute-start(f32[2,24,8,128]{3,2,1,0:T(8,128)S(1)} %get-tuple-element.144), channel_id=1, source_target_pairs={{0,1},{1,2},{2,3},{3,4},{4,5},{5,6},{6,7},{7,0},{8,9},{9,10},{10,1... | collective-permute-start | bytes 589832 | tf_op jit(solution)/shard_map/ppermute | solution.py:31
  62.0 6.0 %collective-permute-start.9 = (f32[2,24,8,128]{3,2,1,0:T(8,128)S(1)}, f32[2,24,8,128]{3,2,1,0:T(8,128)S(1)}, u32[]{:S(2)}, u32[]{:S(2)}) collective-permute-start(f32[2,24,8,128]{3,2,1,0:T(8,128)S(1)} %get-tuple-element.145), channel_id=1, source_target_pairs={{0,7},{1,0},{2,1},{3,2},{4,3},{5,4},{6,5},{7,6},{8,15},{9,8},{10,9... | collective-permute-start | bytes 589832 | tf_op jit(solution)/shard_map/ppermute | solution.py:31
  69.9 12.8 %collective-permute-start.12 = (f32[24,32,128]{2,1,0:T(8,128)S(1)}, f32[24,32,128]{2,1,0:T(8,128)S(1)}, u32[]{:S(2)}, u32[]{:S(2)}) collective-permute-start(f32[24,32,128]{2,1,0:T(8,128)S(1)} %bitcast.18), channel_id=1, source_target_pairs={{0,8},{8,16},{16,24},{24,32},{32,40},{40,48},{48,56},{56,64},{64,7... | collective-permute-start | bytes 1179656 | tf_op jit(solution)/shard_map/ppermute | solution.py:31
  70.0 12.7 %collective-permute-start.13 = (f32[24,32,128]{2,1,0:T(8,128)S(1)}, f32[24,32,128]{2,1,0:T(8,128)S(1)}, u32[]{:S(2)}, u32[]{:S(2)}) collective-permute-start(f32[24,32,128]{2,1,0:T(8,128)S(1)} %bitcast.17), channel_id=1, source_target_pairs={{0,120},{8,0},{16,8},{24,16},{32,24},{40,32},{48,40},{56,48},{64,5... | collective-permute-start | bytes 1179656 | tf_op jit(solution)/shard_map/ppermute | solution.py:31
  75.1 10.8 %collective-permute-start.16 = (f32[3,16,8,128]{3,2,1,0:T(8,128)S(1)}, f32[3,16,8,128]{3,2,1,0:T(8,128)S(1)}, u32[]{:S(2)}, u32[]{:S(2)}) collective-permute-start(f32[3,16,8,128]{3,2,1,0:T(8,128)S(1)} %get-tuple-element.165), channel_id=1, source_target_pairs={{0,1},{1,2},{2,3},{3,4},{4,5},{5,6},{6,7},{7,0},{8,9},{9,10},{10,1... | collective-permute-start | bytes 589832 | tf_op jit(solution)/shard_map/ppermute | solution.py:31
  77.1 8.8 %collective-permute-start.17 = (f32[3,16,8,128]{3,2,1,0:T(8,128)S(1)}, f32[3,16,8,128]{3,2,1,0:T(8,128)S(1)}, u32[]{:S(2)}, u32[]{:S(2)}) collective-permute-start(f32[3,16,8,128]{3,2,1,0:T(8,128)S(1)} %get-tuple-element.166), channel_id=1, source_target_pairs={{0,7},{1,0},{2,1},{3,2},{4,3},{5,4},{6,5},{7,6},{8,15},{9,8},{10,9... | collective-permute-start | bytes 589832 | tf_op jit(solution)/shard_map/ppermute | solution.py:31
  82.7 9.1 %collective-permute-start.14 = (f32[2,24,8,128]{3,2,1,0:T(8,128)S(1)}, f32[2,24,8,128]{3,2,1,0:T(8,128)S(1)}, u32[]{:S(2)}, u32[]{:S(2)}) collective-permute-start(f32[2,24,8,128]{3,2,1,0:T(8,128)S(1)} %get-tuple-element.162), channel_id=1, source_target_pairs={{0,1},{1,2},{2,3},{3,4},{4,5},{5,6},{6,7},{7,0},{8,9},{9,10},{10,1... | collective-permute-start | bytes 589832 | tf_op jit(solution)/shard_map/ppermute | solution.py:31
  85.8 6.0 %collective-permute-start.15 = (f32[2,24,8,128]{3,2,1,0:T(8,128)S(1)}, f32[2,24,8,128]{3,2,1,0:T(8,128)S(1)}, u32[]{:S(2)}, u32[]{:S(2)}) collective-permute-start(f32[2,24,8,128]{3,2,1,0:T(8,128)S(1)} %get-tuple-element.163), channel_id=1, source_target_pairs={{0,7},{1,0},{2,1},{3,2},{4,3},{5,4},{6,5},{7,6},{8,15},{9,8},{10,9... | collective-permute-start | bytes 589832 | tf_op jit(solution)/shard_map/ppermute | solution.py:31
  93.8 11.9 %collective-permute-start.18 = (f32[24,32,128]{2,1,0:T(8,128)S(1)}, f32[24,32,128]{2,1,0:T(8,128)S(1)}, u32[]{:S(2)}, u32[]{:S(2)}) collective-permute-start(f32[24,32,128]{2,1,0:T(8,128)S(1)} %bitcast.20), channel_id=1, source_target_pairs={{0,8},{8,16},{16,24},{24,32},{32,40},{40,48},{48,56},{56,64},{64,7... | collective-permute-start | bytes 1179656 | tf_op jit(solution)/shard_map/ppermute | solution.py:31
  93.8 11.9 %collective-permute-start.19 = (f32[24,32,128]{2,1,0:T(8,128)S(1)}, f32[24,32,128]{2,1,0:T(8,128)S(1)}, u32[]{:S(2)}, u32[]{:S(2)}) collective-permute-start(f32[24,32,128]{2,1,0:T(8,128)S(1)} %bitcast.19), channel_id=1, source_target_pairs={{0,120},{8,0},{16,8},{24,16},{32,24},{40,32},{48,40},{56,48},{64,5... | collective-permute-start | bytes 1179656 | tf_op jit(solution)/shard_map/ppermute | solution.py:31
  99.0 10.8 %collective-permute-start.22 = (f32[3,16,8,128]{3,2,1,0:T(8,128)S(1)}, f32[3,16,8,128]{3,2,1,0:T(8,128)S(1)}, u32[]{:S(2)}, u32[]{:S(2)}) collective-permute-start(f32[3,16,8,128]{3,2,1,0:T(8,128)S(1)} %get-tuple-element.189), channel_id=1, source_target_pairs={{0,1},{1,2},{2,3},{3,4},{4,5},{5,6},{6,7},{7,0},{8,9},{9,10},{10,1... | collective-permute-start | bytes 589832 | tf_op jit(solution)/shard_map/ppermute | solution.py:31
  101.0 8.8 %collective-permute-start.23 = (f32[3,16,8,128]{3,2,1,0:T(8,128)S(1)}, f32[3,16,8,128]{3,2,1,0:T(8,128)S(1)}, u32[]{:S(2)}, u32[]{:S(2)}) collective-permute-start(f32[3,16,8,128]{3,2,1,0:T(8,128)S(1)} %get-tuple-element.190), channel_id=1, source_target_pairs={{0,7},{1,0},{2,1},{3,2},{4,3},{5,4},{6,5},{7,6},{8,15},{9,8},{10,9... | collective-permute-start | bytes 589832 | tf_op jit(solution)/shard_map/ppermute | solution.py:31
  105.7 10.1 %collective-permute-start.20 = (f32[2,24,8,128]{3,2,1,0:T(8,128)S(1)}, f32[2,24,8,128]{3,2,1,0:T(8,128)S(1)}, u32[]{:S(2)}, u32[]{:S(2)}) collective-permute-start(f32[2,24,8,128]{3,2,1,0:T(8,128)S(1)} %get-tuple-element.186), channel_id=1, source_target_pairs={{0,1},{1,2},{2,3},{3,4},{4,5},{5,6},{6,7},{7,0},{8,9},{9,10},{10,1... | collective-permute-start | bytes 589832 | tf_op jit(solution)/shard_map/ppermute | solution.py:31
  109.8 6.0 %collective-permute-start.21 = (f32[2,24,8,128]{3,2,1,0:T(8,128)S(1)}, f32[2,24,8,128]{3,2,1,0:T(8,128)S(1)}, u32[]{:S(2)}, u32[]{:S(2)}) collective-permute-start(f32[2,24,8,128]{3,2,1,0:T(8,128)S(1)} %get-tuple-element.187), channel_id=1, source_target_pairs={{0,7},{1,0},{2,1},{3,2},{4,3},{5,4},{6,5},{7,6},{8,15},{9,8},{10,9... | collective-permute-start | bytes 589832 | tf_op jit(solution)/shard_map/ppermute | solution.py:31

commit v6 on v5

--- a/solution.py
+++ b/solution.py
@@ -314,7 +314,14 @@
     patch_two_steps(prev, lam, mu, q, ue, s, s2, hs, u1, top, bot, hist, right, left, mz)
 
 
-def request_kernel(tile, cell, req, key, kmod, a_ref, bhi, blo):
+def request_kernel(tiles, cells, req, key, kmod, a_ref, bhi, blo, near, sem):
+    copies = [pltpu.make_async_copy(src, near.at[n], sem.at[n]) for n, src in enumerate((tiles, cells))]
+    for cp in copies:
+        cp.start()
+    for cp in copies:
+        cp.wait()
+    tile = near[0].astype(F32)
+    cell = near[1].astype(F32)
     ones = jnp.ones((128, 128), F32)
     sub = lax.broadcasted_iota(jnp.int32, (128, 128), 0)
     lan = lax.broadcasted_iota(jnp.int32, (128, 128), 1)
@@ -517,12 +524,13 @@
     req, key, kmod = pl.pallas_call(
         request_kernel,
         out_shape=[sds(128, 4, 128), sds(8, 128), sds(8, 128)],
-        in_specs=[VM] * 2,
+        in_specs=[HB] * 2,
         out_specs=[VM] * 3,
-        scratch_shapes=[pltpu.VMEM((512, 1024), BF16)] + [pltpu.VMEM((128, 1024), BF16)] * 2,
+        scratch_shapes=[pltpu.VMEM((512, 1024), BF16)] + [pltpu.VMEM((128, 1024), BF16)] * 2
+        + [pltpu.VMEM((2, 8, 128), jnp.int32), pltpu.SemaphoreType.DMA((2,))],
         compiler_params=CP,
         name="requests",
-    )(tile.reshape(8, 128).astype(F32), cell.reshape(8, 128).astype(F32))
+    )(*[pltpu.with_memory_space_constraint(x.reshape(8, 128), pltpu.HBM) for x in (tile, cell)])
     incoming = lax.all_to_all(req, ("gx", "gy"), 0, 0, tiled=True)
     north, south, west, east, incoming = lax.optimization_barrier((north, south, west, east, incoming))
 

time: 146 us -> 146 us (level)
  transfers between devices with their start and end apart: 24 -> 24, of which waited for: 3 -> 3; matrix products, arithmetic and copies ran while one was open for 1% -> 0% of each run, Pallas kernels for 21% -> 22%
where the time goes in v6:
time: 146 us
  Pallas kernels  50.7 us (35%)
  starting transfers between devices  44.2 us (30%)
  blocking collectives  38.4 us (26%)
  waiting for transfers between devices  10.9 us (7%)
    ppermute x24, starting transfers between devices, ring(): return lax.ppermute(x, axis, [(i, (i + step) % n) for i in range(n)])  44.2 us
    all_to_all x1, blocking collectives, local(): returned = lax.all_to_all(answers, ('gx', 'gy'), 0, 0, tiled=True)  19.9 us
    all_to_all x1, blocking collectives, local(): incoming = lax.all_to_all(req, ('gx', 'gy'), 0, 0, tiled=True)  18.5 us
    pallas_call x3, Pallas kernels, local(): pl.pallas_call(round_kernel, out_shape=work, in_specs=[SM] + [VM] * 10, o...  18 us
    ppermute x24, waiting for transfers between devices, ring(): return lax.ppermute(x, axis, [(i, (i + step) % n) for i in range(n)])  10.9 us
    pallas_call x1, Pallas kernels, local(): pl.pallas_call(first_round_kernel, out_shape=work + mats, in_specs=[SM] +...  7.79 us
    pallas_call x3, Pallas kernels, local(): pl.pallas_call(patch_kernel, out_shape=work + [side, side], in_specs=[SM]...  6.33 us
    pallas_call x1, Pallas kernels, local(): pl.pallas_call(building_kernel, out_shape=[sds(3, 16, 32, 128)] * 2 + [sd...  6.12 us
  transfers between devices with their start and end apart: 24, of which 3 were waited for; matrix products, arithmetic and copies ran while one was open for 0% of the time, Pallas kernels for 22%

profile of v6, /device:TPU:1, one launch (start us, length us, event | category | flops | bytes accessed | tf_op | source)
XLA Modules:
  0.0 145.5 jit_solution(11516581213290479235)
XLA Ops:
  0.6 2.1 %pack_first.1 = (f32[52,32,128]{2,1,0:T(8,128)S(1)}, f32[52,32,128]{2,1,0:T(8,128)S(1)}, f32[144,8,128]{2,1,0:T(8,128)S(1)}, f32[144,8,128]{2,1,0:T(8,128)S(1)}) custom-call(f32[3,16,32,128]{3,2,1,0:T(8,128)} %u.3, f32[3,16,32,128]{3,2,1,0:T(8,128)} %p.3, f32[16,32,128]{2,1,0:T(8,128)} %la.3, f32[16,32,128]{2,1,0:T(8,128)} %mu.3, f32[16,32,128]{2,1,0:T(8,128)} %de.3), custom_call_target="tpu_custom_call" | custom-call | tf_op jit(solution)/shard_map/pack_first/pallas_call | solution.py:512
  2.8 2.5 %collective-permute-start = (f32[52,32,128]{2,1,0:T(8,128)S(1)}, f32[52,32,128]{2,1,0:T(8,128)S(1)}, u32[]{:S(2)}, u32[]{:S(2)}) collective-permute-start(f32[52,32,128]{2,1,0:T(8,128)S(1)} %get-tuple-element.109), channel_id=1, source_target_pairs={{0,8},{8,16},{16,24},{24,32},{32,40},{40,48},{48,56},{56,64},{64,7... | collective-permute-start | bytes 2555912 | tf_op jit(solution)/shard_map/ppermute | solution.py:31
  5.3 4.7 %collective-permute-start.1 = (f32[52,32,128]{2,1,0:T(8,128)S(1)}, f32[52,32,128]{2,1,0:T(8,128)S(1)}, u32[]{:S(2)}, u32[]{:S(2)}) collective-permute-start(f32[52,32,128]{2,1,0:T(8,128)S(1)} %get-tuple-element.110), channel_id=1, source_target_pairs={{0,120},{8,0},{16,8},{24,16},{32,24},{40,32},{48,40},{56,48},{64,5... | collective-permute-start | bytes 2555912 | tf_op jit(solution)/shard_map/ppermute | solution.py:31
  9.9 2.1 %collective-permute-start.2 = (f32[144,8,128]{2,1,0:T(8,128)S(1)}, f32[144,8,128]{2,1,0:T(8,128)S(1)}, u32[]{:S(2)}, u32[]{:S(2)}) collective-permute-start(f32[144,8,128]{2,1,0:T(8,128)S(1)} %get-tuple-element.111), channel_id=1, source_target_pairs={{0,1},{1,2},{2,3},{3,4},{4,5},{5,6},{6,7},{7,0},{8,9},{9,10},{10,1... | collective-permute-start | bytes 1769480 | tf_op jit(solution)/shard_map/ppermute | solution.py:31
  12.0 1.8 %requests.1 = (f32[128,4,128]{2,1,0:T(4,128)S(1)}, f32[8,128]{1,0:T(8,128)S(1)}, f32[8,128]{1,0:T(8,128)S(1)}) custom-call(s32[8,128]{1,0:T(8,128)} %bitcast.22, s32[8,128]{1,0:T(8,128)} %bitcast.23), custom_call_target="tpu_custom_call" | custom-call | tf_op jit(solution)/shard_map/requests/pallas_call | solution.py:524
  13.8 18.5 %all_to_all.10.inc = f32[128,4,128]{2,1,0:T(4,128)S(1)} all-to-all(f32[128,4,128]{2,1,0:T(4,128)S(1)} %get-tuple-element.113), channel_id=1, replica_groups=mesh['gx'=16,'gy'=8] {'gx','gy'}, dimensions={0} | all-to-all | bytes 524288 | tf_op jit(solution)/shard_map/all_to_all | solution.py:534
  32.3 1.0 pack_corner.4
  33.3 1.9 %collective-permute-start.4 = (f32[2,52,8,128]{3,2,1,0:T(8,128)}, f32[2,52,8,128]{3,2,1,0:T(8,128)}, u32[]{:S(2)}, u32[]{:S(2)}) collective-permute-start(f32[2,52,8,128]{3,2,1,0:T(8,128)} %get-tuple-element.116), channel_id=1, source_target_pairs={{0,1},{1,2},{2,3},{3,4},{4,5},{5,6},{6,7},{7,0},{8,9},{9,10},{10,1... | collective-permute-start | bytes 1277960 | tf_op jit(solution)/shard_map/ppermute | solution.py:31
  35.3 7.8 %wave_first.1 = (f32[3,32,56,128]{3,2,1,0:T(8,128)S(1)}, f32[6,28,56,128]{3,2,1,0:T(8,128)S(1)}, f32[6,20,56,128]{3,2,1,0:T(8,128)S(1)}, f32[16,48,128]{2,1,0:T(...) custom-call(f32[1,4]{1,0:T(1,128)S(1)} %add_convert_fusion.flags.ref, ...), custom_call_target="tpu_custom_call" | custom-call | tf_op jit(solution)/shard_map/wave_first/pallas_call | solution.py:550
  43.2 2.7 %patch_first.1 = (f32[3,32,56,128]{3,2,1,0:T(8,128)S(1)}, f32[6,28,56,128]{3,2,1,0:T(8,128)S(1)}, f32[6,20,56,128]{3,2,1,0:T(8,128)S(1)}, f32[16,48,128]{2,1,0:T...) custom-call(f32[1,4]{1,0:T(1,128)S(1)} %add_convert_fusion.flags.ref, ...), custom_call_target="tpu_custom_call", output_to_operand_aliasing={{0}: (3, {}), {1}: (4, {}), {2}: (5, {}), {3}: (6, {}), {4}... | custom-call | tf_op jit(solution)/shard_map/patch_first/pallas_call | solution.py:559
  46.4 4.5 %collective-permute-start.7 = (f32[24,32,128]{2,1,0:T(8,128)S(1)}, f32[24,32,128]{2,1,0:T(8,128)S(1)}, u32[]{:S(2)}, u32[]{:S(2)}) collective-permute-start(f32[24,32,128]{2,1,0:T(8,128)S(1)} %bitcast.14), channel_id=1, source_target_pairs={{0,120},{8,0},{16,8},{24,16},{32,24},{40,32},{48,40},{56,48},{64,5... | collective-permute-start | bytes 1179656 | tf_op jit(solution)/shard_map/ppermute | solution.py:31
  51.0 2.1 %building_start.1 = (f32[3,64,1024]{2,1,0:T(8,128)S(1)}, f32[3,64,1024]{2,1,0:T(8,128)S(1)}, f32[3,64,1024]{2,1,0:T(8,128)S(1)}, f32[64,1024]{1,0:T(8,128)S(1)},...) custom-call(f32[3,64,1024]{2,1,0:T(8,128)S(1)} %copy-done, f32[3,64,1024]{2,1,0:T(8,128)S(1)} %copy-done.1, ...), custom_call_target="tpu_custom_call" | custom-call | tf_op jit(solution)/shard_map/building_start/pallas_call | solution.py:488
  53.7 2.2 %collective-permute-start.10 = (f32[3,16,8,128]{3,2,1,0:T(8,128)S(1)}, f32[3,16,8,128]{3,2,1,0:T(8,128)S(1)}, u32[]{:S(2)}, u32[]{:S(2)}) collective-permute-start(f32[3,16,8,128]{3,2,1,0:T(8,128)S(1)} %get-tuple-element.150), channel_id=1, source_target_pairs={{0,1},{1,2},{2,3},{3,4},{4,5},{5,6},{6,7},{7,0},{8,9},{9,10},{10,1... | collective-permute-start | bytes 589832 | tf_op jit(solution)/shard_map/ppermute | solution.py:31
  55.9 2.5 %collective-permute-done.6.north = f32[24,32,128]{2,1,0:T(8,128)S(1)} collective-permute-done((f32[24,32,128]{2,1,0:T(8,128)S(1)}, f32[24,32,128]{2,1,0:T(8,128)S(1)}, u32[]{:S(2)}, u32[]{:S(2)}) %collective-permute-start.6) | collective-permute-done | bytes 393248 | tf_op jit(solution)/shard_map/ppermute | solution.py:31
  58.4 3.6 %collective-permute-start.8 = (f32[2,24,8,128]{3,2,1,0:T(8,128)S(1)}, f32[2,24,8,128]{3,2,1,0:T(8,128)S(1)}, u32[]{:S(2)}, u32[]{:S(2)}) collective-permute-start(f32[2,24,8,128]{3,2,1,0:T(8,128)S(1)} %get-tuple-element.144), channel_id=1, source_target_pairs={{0,1},{1,2},{2,3},{3,4},{4,5},{5,6},{6,7},{7,0},{8,9},{9,10},{10,1... | collective-permute-start | bytes 589832 | tf_op jit(solution)/shard_map/ppermute | solution.py:31
  62.1 6.0 %wave_round.3 = (f32[3,32,56,128]{3,2,1,0:T(8,128)S(1)}, f32[6,28,56,128]{3,2,1,0:T(8,128)S(1)}, f32[6,20,56,128]{3,2,1,0:T(8,128)S(1)}, f32[16,48,128]{2,1,0:T(...) custom-call(f32[1,4]{1,0:T(1,128)S(1)} %add_convert_fusion.flags.ref, ...), custom_call_target="tpu_custom_call" | custom-call | tf_op jit(solution)/shard_map/wave_round/pallas_call | solution.py:599
  68.1 1.9 %patch_round.3 = (f32[3,32,56,128]{3,2,1,0:T(8,128)S(1)}, f32[6,28,56,128]{3,2,1,0:T(8,128)S(1)}, f32[6,20,56,128]{3,2,1,0:T(8,128)S(1)}, f32[16,48,128]{2,1,0:T...) custom-call(f32[1,4]{1,0:T(1,128)S(1)} %add_convert_fusion.flags.ref, ...), custom_call_target="tpu_custom_call", output_to_operand_aliasing={{0}: (7, {}), {1}: (8, {}), {2}: (9, {}), {3}: (10, {}), {4... | custom-call | tf_op jit(solution)/shard_map/patch_round/pallas_call | solution.py:608
  70.1 5.0 %collective-permute-start.13 = (f32[24,32,128]{2,1,0:T(8,128)S(1)}, f32[24,32,128]{2,1,0:T(8,128)S(1)}, u32[]{:S(2)}, u32[]{:S(2)}) collective-permute-start(f32[24,32,128]{2,1,0:T(8,128)S(1)} %bitcast.16), channel_id=1, source_target_pairs={{0,120},{8,0},{16,8},{24,16},{32,24},{40,32},{48,40},{56,48},{64,5... | collective-permute-start | bytes 1179656 | tf_op jit(solution)/shard_map/ppermute | solution.py:31
  75.1 2.1 %collective-permute-start.16 = (f32[3,16,8,128]{3,2,1,0:T(8,128)S(1)}, f32[3,16,8,128]{3,2,1,0:T(8,128)S(1)}, u32[]{:S(2)}, u32[]{:S(2)}) collective-permute-start(f32[3,16,8,128]{3,2,1,0:T(8,128)S(1)} %get-tuple-element.165), channel_id=1, source_target_pairs={{0,1},{1,2},{2,3},{3,4},{4,5},{5,6},{6,7},{7,0},{8,9},{9,10},{10,1... | collective-permute-start | bytes 589832 | tf_op jit(solution)/shard_map/ppermute | solution.py:31
  77.1 5.4 %collective-permute-done.12.north = f32[24,32,128]{2,1,0:T(8,128)S(1)} collective-permute-done((f32[24,32,128]{2,1,0:T(8,128)S(1)}, f32[24,32,128]{2,1,0:T(8,128)S(1)}, u32[]{:S(2)}, u32[]{:S(2)}) %collective-permute-start.12) | collective-permute-done | bytes 393248 | tf_op jit(solution)/shard_map/ppermute | solution.py:31
  82.6 3.2 %collective-permute-start.14 = (f32[2,24,8,128]{3,2,1,0:T(8,128)S(1)}, f32[2,24,8,128]{3,2,1,0:T(8,128)S(1)}, u32[]{:S(2)}, u32[]{:S(2)}) collective-permute-start(f32[2,24,8,128]{3,2,1,0:T(8,128)S(1)} %get-tuple-element.162), channel_id=1, source_target_pairs={{0,1},{1,2},{2,3},{3,4},{4,5},{5,6},{6,7},{7,0},{8,9},{9,10},{10,1... | collective-permute-start | bytes 589832 | tf_op jit(solution)/shard_map/ppermute | solution.py:31
  85.8 6.0 %wave_round.4 = (f32[3,32,56,128]{3,2,1,0:T(8,128)S(1)}, f32[6,28,56,128]{3,2,1,0:T(8,128)S(1)}, f32[6,20,56,128]{3,2,1,0:T(8,128)S(1)}, f32[16,48,128]{2,1,0:T(...) custom-call(f32[1,4]{1,0:T(1,128)S(1)} %add_convert_fusion.flags.ref, ...), custom_call_target="tpu_custom_call" | custom-call | tf_op jit(solution)/shard_map/wave_round/pallas_call | solution.py:599
  91.8 1.9 %patch_round.4 = (f32[3,32,56,128]{3,2,1,0:T(8,128)S(1)}, f32[6,28,56,128]{3,2,1,0:T(8,128)S(1)}, f32[6,20,56,128]{3,2,1,0:T(8,128)S(1)}, f32[16,48,128]{2,1,0:T...) custom-call(f32[1,4]{1,0:T(1,128)S(1)} %add_convert_fusion.flags.ref, ...), custom_call_target="tpu_custom_call", output_to_operand_aliasing={{0}: (7, {}), {1}: (8, {}), {2}: (9, {}), {3}: (10, {}), {4... | custom-call | tf_op jit(solution)/shard_map/patch_round/pallas_call | solution.py:608
  93.8 5.1 %collective-permute-start.19 = (f32[24,32,128]{2,1,0:T(8,128)S(1)}, f32[24,32,128]{2,1,0:T(8,128)S(1)}, u32[]{:S(2)}, u32[]{:S(2)}) collective-permute-start(f32[24,32,128]{2,1,0:T(8,128)S(1)} %bitcast.18), channel_id=1, source_target_pairs={{0,120},{8,0},{16,8},{24,16},{32,24},{40,32},{48,40},{56,48},{64,5... | collective-permute-start | bytes 1179656 | tf_op jit(solution)/shard_map/ppermute | solution.py:31
  98.9 2.0 %collective-permute-start.22 = (f32[3,16,8,128]{3,2,1,0:T(8,128)S(1)}, f32[3,16,8,128]{3,2,1,0:T(8,128)S(1)}, u32[]{:S(2)}, u32[]{:S(2)}) collective-permute-start(f32[3,16,8,128]{3,2,1,0:T(8,128)S(1)} %get-tuple-element.189), channel_id=1, source_target_pairs={{0,1},{1,2},{2,3},{3,4},{4,5},{5,6},{6,7},{7,0},{8,9},{9,10},{10,1... | collective-permute-start | bytes 589832 | tf_op jit(solution)/shard_map/ppermute | solution.py:31
  101.5 1.2 early_answers.1
  102.7 2.9 %collective-permute-done.18.north = f32[24,32,128]{2,1,0:T(8,128)S(1)} collective-permute-done((f32[24,32,128]{2,1,0:T(8,128)S(1)}, f32[24,32,128]{2,1,0:T(8,128)S(1)}, u32[]{:S(2)}, u32[]{:S(2)}) %collective-permute-start.18) | collective-permute-done | bytes 393248 | tf_op jit(solution)/shard_map/ppermute | solution.py:31
  105.6 4.2 %collective-permute-start.20 = (f32[2,24,8,128]{3,2,1,0:T(8,128)S(1)}, f32[2,24,8,128]{3,2,1,0:T(8,128)S(1)}, u32[]{:S(2)}, u32[]{:S(2)}) collective-permute-start(f32[2,24,8,128]{3,2,1,0:T(8,128)S(1)} %get-tuple-element.186), channel_id=1, source_target_pairs={{0,1},{1,2},{2,3},{3,4},{4,5},{5,6},{6,7},{7,0},{8,9},{9,10},{10,1... | collective-permute-start | bytes 589832 | tf_op jit(solution)/shard_map/ppermute | solution.py:31
  109.9 6.0 %wave_round.5 = (f32[3,32,56,128]{3,2,1,0:T(8,128)S(1)}, f32[6,28,56,128]{3,2,1,0:T(8,128)S(1)}, f32[6,20,56,128]{3,2,1,0:T(8,128)S(1)}, f32[16,48,128]{2,1,0:T(...) custom-call(f32[1,4]{1,0:T(1,128)S(1)} %add_convert_fusion.flags.ref, ...), custom_call_target="tpu_custom_call" | custom-call | tf_op jit(solution)/shard_map/wave_round/pallas_call | solution.py:599
  115.9 2.6 %patch_round.5 = (f32[3,32,56,128]{3,2,1,0:T(8,128)S(1)}, f32[6,28,56,128]{3,2,1,0:T(8,128)S(1)}, f32[6,20,56,128]{3,2,1,0:T(8,128)S(1)}, f32[16,48,128]{2,1,0:T...) custom-call(f32[1,4]{1,0:T(1,128)S(1)} %add_convert_fusion.flags.ref, ...), custom_call_target="tpu_custom_call", output_to_operand_aliasing={{0}: (7, {}), {1}: (8, {}), {2}: (9, {}), {3}: (10, {}), {4... | custom-call | tf_op jit(solution)/shard_map/patch_round/pallas_call | solution.py:608
  119.3 19.9 %all_to_all.11.refs_3_ = f32[128,4,128]{2,1,0:T(4,128)S(1)} all-to-all(f32[128,4,128]{2,1,0:T(4,128)S(1)} %answers.1), channel_id=1, replica_groups=mesh['gx'=16,'gy'=8] {'gx','gy'}, dimensions={0} | all-to-all | bytes 524288 | tf_op jit(solution)/shard_map/all_to_all | solution.py:629
  139.2 6.1 %buildings.1 = (f32[3,16,32,128]{3,2,1,0:T(8,128)}, f32[3,16,32,128]{3,2,1,0:T(8,128)}, f32[3,64,1024]{2,1,0:T(8,128)}, f32[3,64,1024]{2,1,0:T(8,128)}, f32[3,64,1024]{2,1,0:T(8,128)}) custom-call(f32[3,8,32,128]{3,2,1,0:T(8,128)S(1)} %get-tuple-element.199.refs_0_, f32[3,8,32,128]{3,2,1,0:T(8,128)S(1)} %get-tuple-element.200.refs_1_, ...), custom_call_target="tpu_custom_call" | custom-call | tf_op jit(solution)/shard_map/buildings/pallas_call | solution.py:630
  (54 shorter events, 2.9 us)
Async XLA Ops:
  2.8 29.6 %collective-permute-start = (f32[52,32,128]{2,1,0:T(8,128)S(1)}, f32[52,32,128]{2,1,0:T(8,128)S(1)}, u32[]{:S(2)}, u32[]{:S(2)}) collective-permute-start(f32[52,32,128]{2,1,0:T(8,128)S(1)} %get-tuple-element.109), channel_id=1, source_target_pairs={{0,8},{8,16},{16,24},{24,32},{32,40},{40,48},{48,56},{56,64},{64,7... | collective-permute-start | bytes 2555912 | tf_op jit(solution)/shard_map/ppermute | solution.py:31
  5.3 27.0 %collective-permute-start.1 = (f32[52,32,128]{2,1,0:T(8,128)S(1)}, f32[52,32,128]{2,1,0:T(8,128)S(1)}, u32[]{:S(2)}, u32[]{:S(2)}) collective-permute-start(f32[52,32,128]{2,1,0:T(8,128)S(1)} %get-tuple-element.110), channel_id=1, source_target_pairs={{0,120},{8,0},{16,8},{24,16},{32,24},{40,32},{48,40},{56,48},{64,5... | collective-permute-start | bytes 2555912 | tf_op jit(solution)/shard_map/ppermute | solution.py:31
  9.9 22.4 %collective-permute-start.2 = (f32[144,8,128]{2,1,0:T(8,128)S(1)}, f32[144,8,128]{2,1,0:T(8,128)S(1)}, u32[]{:S(2)}, u32[]{:S(2)}) collective-permute-start(f32[144,8,128]{2,1,0:T(8,128)S(1)} %get-tuple-element.111), channel_id=1, source_target_pairs={{0,1},{1,2},{2,3},{3,4},{4,5},{5,6},{6,7},{7,0},{8,9},{9,10},{10,1... | collective-permute-start | bytes 1769480 | tf_op jit(solution)/shard_map/ppermute | solution.py:31
  12.0 20.3 %collective-permute-start.3 = (f32[144,8,128]{2,1,0:T(8,128)S(1)}, f32[144,8,128]{2,1,0:T(8,128)S(1)}, u32[]{:S(2)}, u32[]{:S(2)}) collective-permute-start(f32[144,8,128]{2,1,0:T(8,128)S(1)} %get-tuple-element.112), channel_id=1, source_target_pairs={{0,7},{1,0},{2,1},{3,2},{4,3},{5,4},{6,5},{7,6},{8,15},{9,8},{10,9... | collective-permute-start | bytes 1769480 | tf_op jit(solution)/shard_map/ppermute | solution.py:31
  33.3 9.7 %collective-permute-start.4 = (f32[2,52,8,128]{3,2,1,0:T(8,128)}, f32[2,52,8,128]{3,2,1,0:T(8,128)}, u32[]{:S(2)}, u32[]{:S(2)}) collective-permute-start(f32[2,52,8,128]{3,2,1,0:T(8,128)} %get-tuple-element.116), channel_id=1, source_target_pairs={{0,1},{1,2},{2,3},{3,4},{4,5},{5,6},{6,7},{7,0},{8,9},{9,10},{10,1... | collective-permute-start | bytes 1277960 | tf_op jit(solution)/shard_map/ppermute | solution.py:31
  35.2 7.9 %collective-permute-start.5 = (f32[2,52,8,128]{3,2,1,0:T(8,128)}, f32[2,52,8,128]{3,2,1,0:T(8,128)}, u32[]{:S(2)}, u32[]{:S(2)}) collective-permute-start(f32[2,52,8,128]{3,2,1,0:T(8,128)} %get-tuple-element.117), channel_id=1, source_target_pairs={{0,7},{1,0},{2,1},{3,2},{4,3},{5,4},{6,5},{7,6},{8,15},{9,8},{10,9... | collective-permute-start | bytes 1277960 | tf_op jit(solution)/shard_map/ppermute | solution.py:31
  43.1 7.8 %copy-start = (f32[3,64,1024]{2,1,0:T(8,128)S(1)}, f32[3,64,1024]{2,1,0:T(8,128)}, u32[]{:S(2)}) copy-start(f32[3,64,1024]{2,1,0:T(8,128)} %d_in.1) | copy-start | bytes 2359300
  43.1 7.8 %copy-start.1 = (f32[3,64,1024]{2,1,0:T(8,128)S(1)}, f32[3,64,1024]{2,1,0:T(8,128)}, u32[]{:S(2)}) copy-start(f32[3,64,1024]{2,1,0:T(8,128)} %v_in.1) | copy-start | bytes 2359300
  43.1 7.8 %copy-start.2 = (f32[3,64,1024]{2,1,0:T(8,128)S(1)}, f32[3,64,1024]{2,1,0:T(8,128)}, u32[]{:S(2)}) copy-start(f32[3,64,1024]{2,1,0:T(8,128)} %hf.1) | copy-start | bytes 2359300
  43.1 7.8 %copy-start.3 = (s32[3,64,1024]{2,1,0:T(8,128)S(1)}, s32[3,64,1024]{2,1,0:T(8,128)}, u32[]{:S(2)}) copy-start(s32[3,64,1024]{2,1,0:T(8,128)} %br.1) | copy-start | bytes 2359300
  43.1 7.8 %copy-start.4 = (f32[64,1024]{1,0:T(8,128)S(1)}, f32[64,1024]{1,0:T(8,128)}, u32[]{:S(2)}) copy-start(f32[64,1024]{1,0:T(8,128)} %st.1) | copy-start | bytes 786436
  43.1 7.8 %copy-start.5 = (f32[64,1024]{1,0:T(8,128)S(1)}, f32[64,1024]{1,0:T(8,128)}, u32[]{:S(2)}) copy-start(f32[64,1024]{1,0:T(8,128)} %ms.1) | copy-start | bytes 786436
  43.1 7.8 %copy-start.6 = (f32[64,1024]{1,0:T(8,128)S(1)}, f32[64,1024]{1,0:T(8,128)}, u32[]{:S(2)}) copy-start(f32[64,1024]{1,0:T(8,128)} %yd.1) | copy-start | bytes 786436
  43.2 7.8 %copy-start.7 = (s32[1024]{0:T(1024)S(1)}, s32[1024]{0:T(1024)}, u32[]{:S(2)}) copy-start(s32[1024]{0:T(1024)} %param.27) | copy-start | bytes 12292
  45.9 12.5 %collective-permute-start.6 = (f32[24,32,128]{2,1,0:T(8,128)S(1)}, f32[24,32,128]{2,1,0:T(8,128)S(1)}, u32[]{:S(2)}, u32[]{:S(2)}) collective-permute-start(f32[24,32,128]{2,1,0:T(8,128)S(1)} %bitcast.15), channel_id=1, source_target_pairs={{0,8},{8,16},{16,24},{24,32},{32,40},{40,48},{48,56},{56,64},{64,7... | collective-permute-start | bytes 1179656 | tf_op jit(solution)/shard_map/ppermute | solution.py:31
  46.4 12.0 %collective-permute-start.7 = (f32[24,32,128]{2,1,0:T(8,128)S(1)}, f32[24,32,128]{2,1,0:T(8,128)S(1)}, u32[]{:S(2)}, u32[]{:S(2)}) collective-permute-start(f32[24,32,128]{2,1,0:T(8,128)S(1)} %bitcast.14), channel_id=1, source_target_pairs={{0,120},{8,0},{16,8},{24,16},{32,24},{40,32},{48,40},{56,48},{64,5... | collective-permute-start | bytes 1179656 | tf_op jit(solution)/shard_map/ppermute | solution.py:31
  53.7 8.4 %collective-permute-start.10 = (f32[3,16,8,128]{3,2,1,0:T(8,128)S(1)}, f32[3,16,8,128]{3,2,1,0:T(8,128)S(1)}, u32[]{:S(2)}, u32[]{:S(2)}) collective-permute-start(f32[3,16,8,128]{3,2,1,0:T(8,128)S(1)} %get-tuple-element.150), channel_id=1, source_target_pairs={{0,1},{1,2},{2,3},{3,4},{4,5},{5,6},{6,7},{7,0},{8,9},{9,10},{10,1... | collective-permute-start | bytes 589832 | tf_op jit(solution)/shard_map/ppermute | solution.py:31
  55.9 6.2 %collective-permute-start.11 = (f32[3,16,8,128]{3,2,1,0:T(8,128)S(1)}, f32[3,16,8,128]{3,2,1,0:T(8,128)S(1)}, u32[]{:S(2)}, u32[]{:S(2)}) collective-permute-start(f32[3,16,8,128]{3,2,1,0:T(8,128)S(1)} %get-tuple-element.151), channel_id=1, source_target_pairs={{0,7},{1,0},{2,1},{3,2},{4,3},{5,4},{6,5},{7,6},{8,15},{9,8},{10,9... | collective-permute-start | bytes 589832 | tf_op jit(solution)/shard_map/ppermute | solution.py:31
  58.4 9.6 %collective-permute-start.8 = (f32[2,24,8,128]{3,2,1,0:T(8,128)S(1)}, f32[2,24,8,128]{3,2,1,0:T(8,128)S(1)}, u32[]{:S(2)}, u32[]{:S(2)}) collective-permute-start(f32[2,24,8,128]{3,2,1,0:T(8,128)S(1)} %get-tuple-element.144), channel_id=1, source_target_pairs={{0,1},{1,2},{2,3},{3,4},{4,5},{5,6},{6,7},{7,0},{8,9},{9,10},{10,1... | collective-permute-start | bytes 589832 | tf_op jit(solution)/shard_map/ppermute | solution.py:31
  62.1 6.0 %collective-permute-start.9 = (f32[2,24,8,128]{3,2,1,0:T(8,128)S(1)}, f32[2,24,8,128]{3,2,1,0:T(8,128)S(1)}, u32[]{:S(2)}, u32[]{:S(2)}) collective-permute-start(f32[2,24,8,128]{3,2,1,0:T(8,128)S(1)} %get-tuple-element.145), channel_id=1, source_target_pairs={{0,7},{1,0},{2,1},{3,2},{4,3},{5,4},{6,5},{7,6},{8,15},{9,8},{10,9... | collective-permute-start | bytes 589832 | tf_op jit(solution)/shard_map/ppermute | solution.py:31
  70.0 12.6 %collective-permute-start.12 = (f32[24,32,128]{2,1,0:T(8,128)S(1)}, f32[24,32,128]{2,1,0:T(8,128)S(1)}, u32[]{:S(2)}, u32[]{:S(2)}) collective-permute-start(f32[24,32,128]{2,1,0:T(8,128)S(1)} %bitcast.17), channel_id=1, source_target_pairs={{0,8},{8,16},{16,24},{24,32},{32,40},{40,48},{48,56},{56,64},{64,7... | collective-permute-start | bytes 1179656 | tf_op jit(solution)/shard_map/ppermute | solution.py:31
  70.1 12.5 %collective-permute-start.13 = (f32[24,32,128]{2,1,0:T(8,128)S(1)}, f32[24,32,128]{2,1,0:T(8,128)S(1)}, u32[]{:S(2)}, u32[]{:S(2)}) collective-permute-start(f32[24,32,128]{2,1,0:T(8,128)S(1)} %bitcast.16), channel_id=1, source_target_pairs={{0,120},{8,0},{16,8},{24,16},{32,24},{40,32},{48,40},{56,48},{64,5... | collective-permute-start | bytes 1179656 | tf_op jit(solution)/shard_map/ppermute | solution.py:31
  75.1 10.7 %collective-permute-start.16 = (f32[3,16,8,128]{3,2,1,0:T(8,128)S(1)}, f32[3,16,8,128]{3,2,1,0:T(8,128)S(1)}, u32[]{:S(2)}, u32[]{:S(2)}) collective-permute-start(f32[3,16,8,128]{3,2,1,0:T(8,128)S(1)} %get-tuple-element.165), channel_id=1, source_target_pairs={{0,1},{1,2},{2,3},{3,4},{4,5},{5,6},{6,7},{7,0},{8,9},{9,10},{10,1... | collective-permute-start | bytes 589832 | tf_op jit(solution)/shard_map/ppermute | solution.py:31
  77.1 8.7 %collective-permute-start.17 = (f32[3,16,8,128]{3,2,1,0:T(8,128)S(1)}, f32[3,16,8,128]{3,2,1,0:T(8,128)S(1)}, u32[]{:S(2)}, u32[]{:S(2)}) collective-permute-start(f32[3,16,8,128]{3,2,1,0:T(8,128)S(1)} %get-tuple-element.166), channel_id=1, source_target_pairs={{0,7},{1,0},{2,1},{3,2},{4,3},{5,4},{6,5},{7,6},{8,15},{9,8},{10,9... | collective-permute-start | bytes 589832 | tf_op jit(solution)/shard_map/ppermute | solution.py:31
  82.6 9.2 %collective-permute-start.14 = (f32[2,24,8,128]{3,2,1,0:T(8,128)S(1)}, f32[2,24,8,128]{3,2,1,0:T(8,128)S(1)}, u32[]{:S(2)}, u32[]{:S(2)}) collective-permute-start(f32[2,24,8,128]{3,2,1,0:T(8,128)S(1)} %get-tuple-element.162), channel_id=1, source_target_pairs={{0,1},{1,2},{2,3},{3,4},{4,5},{5,6},{6,7},{7,0},{8,9},{9,10},{10,1... | collective-permute-start | bytes 589832 | tf_op jit(solution)/shard_map/ppermute | solution.py:31
  85.8 6.0 %collective-permute-start.15 = (f32[2,24,8,128]{3,2,1,0:T(8,128)S(1)}, f32[2,24,8,128]{3,2,1,0:T(8,128)S(1)}, u32[]{:S(2)}, u32[]{:S(2)}) collective-permute-start(f32[2,24,8,128]{3,2,1,0:T(8,128)S(1)} %get-tuple-element.163), channel_id=1, source_target_pairs={{0,7},{1,0},{2,1},{3,2},{4,3},{5,4},{6,5},{7,6},{8,15},{9,8},{10,9... | collective-permute-start | bytes 589832 | tf_op jit(solution)/shard_map/ppermute | solution.py:31
  93.7 11.9 %collective-permute-start.18 = (f32[24,32,128]{2,1,0:T(8,128)S(1)}, f32[24,32,128]{2,1,0:T(8,128)S(1)}, u32[]{:S(2)}, u32[]{:S(2)}) collective-permute-start(f32[24,32,128]{2,1,0:T(8,128)S(1)} %bitcast.19), channel_id=1, source_target_pairs={{0,8},{8,16},{16,24},{24,32},{32,40},{40,48},{48,56},{56,64},{64,7... | collective-permute-start | bytes 1179656 | tf_op jit(solution)/shard_map/ppermute | solution.py:31
  93.8 11.8 %collective-permute-start.19 = (f32[24,32,128]{2,1,0:T(8,128)S(1)}, f32[24,32,128]{2,1,0:T(8,128)S(1)}, u32[]{:S(2)}, u32[]{:S(2)}) collective-permute-start(f32[24,32,128]{2,1,0:T(8,128)S(1)} %bitcast.18), channel_id=1, source_target_pairs={{0,120},{8,0},{16,8},{24,16},{32,24},{40,32},{48,40},{56,48},{64,5... | collective-permute-start | bytes 1179656 | tf_op jit(solution)/shard_map/ppermute | solution.py:31
  98.9 10.9 %collective-permute-start.22 = (f32[3,16,8,128]{3,2,1,0:T(8,128)S(1)}, f32[3,16,8,128]{3,2,1,0:T(8,128)S(1)}, u32[]{:S(2)}, u32[]{:S(2)}) collective-permute-start(f32[3,16,8,128]{3,2,1,0:T(8,128)S(1)} %get-tuple-element.189), channel_id=1, source_target_pairs={{0,1},{1,2},{2,3},{3,4},{4,5},{5,6},{6,7},{7,0},{8,9},{9,10},{10,1... | collective-permute-start | bytes 589832 | tf_op jit(solution)/shard_map/ppermute | solution.py:31
  100.9 8.9 %collective-permute-start.23 = (f32[3,16,8,128]{3,2,1,0:T(8,128)S(1)}, f32[3,16,8,128]{3,2,1,0:T(8,128)S(1)}, u32[]{:S(2)}, u32[]{:S(2)}) collective-permute-start(f32[3,16,8,128]{3,2,1,0:T(8,128)S(1)} %get-tuple-element.190), channel_id=1, source_target_pairs={{0,7},{1,0},{2,1},{3,2},{4,3},{5,4},{6,5},{7,6},{8,15},{9,8},{10,9... | collective-permute-start | bytes 589832 | tf_op jit(solution)/shard_map/ppermute | solution.py:31
  105.6 10.2 %collective-permute-start.20 = (f32[2,24,8,128]{3,2,1,0:T(8,128)S(1)}, f32[2,24,8,128]{3,2,1,0:T(8,128)S(1)}, u32[]{:S(2)}, u32[]{:S(2)}) collective-permute-start(f32[2,24,8,128]{3,2,1,0:T(8,128)S(1)} %get-tuple-element.186), channel_id=1, source_target_pairs={{0,1},{1,2},{2,3},{3,4},{4,5},{5,6},{6,7},{7,0},{8,9},{9,10},{10,1... | collective-permute-start | bytes 589832 | tf_op jit(solution)/shard_map/ppermute | solution.py:31
  109.8 6.0 %collective-permute-start.21 = (f32[2,24,8,128]{3,2,1,0:T(8,128)S(1)}, f32[2,24,8,128]{3,2,1,0:T(8,128)S(1)}, u32[]{:S(2)}, u32[]{:S(2)}) collective-permute-start(f32[2,24,8,128]{3,2,1,0:T(8,128)S(1)} %get-tuple-element.187), channel_id=1, source_target_pairs={{0,7},{1,0},{2,1},{3,2},{4,3},{5,4},{6,5},{7,6},{8,15},{9,8},{10,9... | collective-permute-start | bytes 589832 | tf_op jit(solution)/shard_map/ppermute | solution.py:31
